TPU v7x, 32 devices: a whole 2x2x4 slice. The times are simulated.
32 devices in a mesh: grp: 2 (over x), seq: 16 (over z, y, core).
Axes of the slice: x: 2, y: 2, z: 4, core: 2. Of those that a mesh axis runs over, the one named last changes fastest.
Arguments:
- query_stream: bfloat16 [4096, 2048], P(('grp', 'seq')), parts along dimension 0, may hold values from -6 to 6
- key_stream: bfloat16 [4096, 2048], P(('grp', 'seq')), parts along dimension 0, may hold values from -6 to 6
- value_stream: bfloat16 [4096, 2048], P(('grp', 'seq')), parts along dimension 0, may hold values from -6 to 6
- cotangent: bfloat16 [4096, 2048], P(('grp', 'seq')), parts along dimension 0, may hold values from -6 to 6
- decay_rate: float32 [128, 16], replicated, may hold values from 0 to 1, as said below
- residue: float32 [128, 16], replicated, may hold values from -4 to 4
Outputs:
- mixer_out: bfloat16 [4096, 2048], P(('grp', 'seq')), parts along dimension 0
- query_grad: bfloat16 [4096, 2048], P(('grp', 'seq')), parts along dimension 0
- key_grad: bfloat16 [4096, 2048], P(('grp', 'seq')), parts along dimension 0
- value_grad: bfloat16 [4096, 2048], P(('grp', 'seq')), parts along dimension 0
- filter_grad: float32 [256, 16], P('grp'), parts along dimension 0
There are 2 independent parts, one for each index of `grp`. A program takes and returns all parts, laid end to end along the dimension named above; an argument that names none is the same for every part. Nothing has to cross between parts.
Inputs may be any that keep to these rules, and one draw needn't show every extreme that they name: `decay_rate`: positive decay rates.
All inputs are finite; a program needn't handle non-finite values.
Results may differ from a plain program's by a relative error of at most 0.0023.
Values sent between devices are 32-bit elements; how exact they have to be, the bound alone decides.
No kernel may reach another device: no remote copies, remote signals or barrier semaphores. Data moves between devices by JAX's collectives and lax.ppermute only.
A program may use at most 192 MiB of HBM per device.

v0:
```python
import math

import jax
import jax.numpy as jnp
from jax import lax
from jax.sharding import PartitionSpec as P

PRECISE = lax.Precision.HIGHEST


def prefix(shard, axis, combine, identity, reverse):
    count, position = (lax.axis_size(axis), lax.axis_index(axis))
    everything = jax.tree.map(lambda part: lax.all_gather(part, axis), shard)
    start = jax.tree.map(
        lambda part, zero: jnp.broadcast_to(jnp.asarray(zero, part.dtype), part.shape),
        shard,
        identity,
    )

    def hop(k, before):
        at = count - 1 - k if reverse else k
        reached = at > position if reverse else at < position
        new = combine(before, jax.tree.map(lambda part: part[at], everything))
        return jax.tree.map(lambda a, b: jnp.where(reached, a, b), new, before)

    return lax.fori_loop(0, count, hop, start)


def lag_sums(correlation):
    groups_here, length, width_here = correlation.shape
    flipped = correlation[:, :, ::-1]
    padded = jnp.concatenate([flipped, jnp.zeros_like(flipped)], axis=2)
    flattened = padded.reshape(groups_here, 2 * length * length)[:, : length * (2 * length - 1)]
    skewed = flattened.reshape(groups_here, length, 2 * length - 1)
    return jnp.sum(skewed[:, :, length - 1 :], axis=1)


def forward_combine(earlier, later):
    return (earlier[0] * later[1] + later[0], earlier[1] * later[1])


def backward_combine(earlier, later):
    return (later[0] + later[1] * earlier[0], earlier[1] * later[1])


def per_device(query_stream, key_stream, value_stream, cotangent, decay_rate, residue):
    length, width = query_stream.shape
    groups, modes = decay_rate.shape
    per_group = width // groups
    devices = lax.axis_size("seq")
    total = length * devices
    positions = jnp.arange(length, dtype=jnp.float32)
    weights = residue * jnp.sqrt(2.0 * decay_rate / modes)
    decay_grid = decay_rate[:, :, None]
    start_table = jnp.exp(-decay_grid * positions)
    lag_filter = jnp.einsum("gn,gnl->gl", weights, start_table, precision=PRECISE)
    rate_wide = jnp.repeat(decay_rate.T, per_group, axis=1)
    query_full = query_stream.astype(jnp.float32)
    key_full = key_stream.astype(jnp.float32)
    value_full = value_stream.astype(jnp.float32)
    cotangent_full = cotangent.astype(jnp.float32)
    gated = key_full * value_full
    upstream = cotangent_full * query_full
    gated_lanes = gated.reshape(length, groups, per_group).transpose(1, 2, 0)
    upstream_lanes = upstream.reshape(length, groups, per_group).transpose(1, 2, 0)
    end_powers = jnp.exp(-decay_grid * (length - 1.0 - positions))
    block_power = jnp.exp(-rate_wide * length)
    end_state = jnp.einsum("gnt,gkt->ngk", end_powers, gated_lanes, precision=PRECISE).reshape(
        modes, width
    )
    start_state = jnp.einsum(
        "gnt,gkt->ngk", start_table, upstream_lanes, precision=PRECISE
    ).reshape(modes, width)
    identity = (jnp.zeros_like(end_state), jnp.ones_like(block_power))
    incoming, power_seen = prefix((end_state, block_power), "seq", forward_combine, identity, False)
    outgoing, power_after = prefix(
        (start_state, block_power), "seq", backward_combine, identity, True
    )
    lag_index = (
        jnp.arange(length, dtype=jnp.int32)[:, None] - jnp.arange(length, dtype=jnp.int32)[None, :]
    )
    causal = (lag_index >= 0)[None]
    clipped = jnp.maximum(lag_index, 0)
    block_groups = math.gcd(groups, 32)
    local_parts = []
    local_grads = []
    lag_parts = []
    for block_index in range(groups // block_groups):
        group_slice = slice(block_index * block_groups, (block_index + 1) * block_groups)
        toeplitz = jnp.where(causal, lag_filter[group_slice][:, clipped], 0.0)
        gated_block = gated_lanes[group_slice]
        upstream_block = upstream_lanes[group_slice]
        local_parts.append(jnp.einsum("gts,gks->gkt", toeplitz, gated_block, precision=PRECISE))
        local_grads.append(jnp.einsum("gts,gkt->gks", toeplitz, upstream_block, precision=PRECISE))
        correlation = jnp.einsum("gkt,gks->gts", upstream_block, gated_block, precision=PRECISE)
        lag_parts.append(lag_sums(correlation))
    forward_coef = weights[:, :, None] * jnp.exp(-decay_grid * (positions + 1.0))
    backward_coef = weights[:, :, None] * jnp.exp(-decay_grid * (length - positions))
    incoming_groups = incoming.reshape(modes, groups, per_group)
    outgoing_groups = outgoing.reshape(modes, groups, per_group)
    carried = jnp.einsum("gnt,ngk->gkt", forward_coef, incoming_groups, precision=PRECISE)
    returned = jnp.einsum("gnt,ngk->gkt", backward_coef, outgoing_groups, precision=PRECISE)
    mixed_sum = (
        (jnp.concatenate(local_parts, axis=0) + carried).transpose(2, 0, 1).reshape(length, width)
    )
    gated_grad = (
        (jnp.concatenate(local_grads, axis=0) + returned).transpose(2, 0, 1).reshape(length, width)
    )
    mixer_out = (query_full * mixed_sum).astype(jnp.bfloat16)
    query_grad = (cotangent_full * mixed_sum).astype(jnp.bfloat16)
    key_grad = (gated_grad * value_full).astype(jnp.bfloat16)
    value_grad = (gated_grad * key_full).astype(jnp.bfloat16)
    lag_total = jnp.concatenate(lag_parts, axis=0)
    local_residue = jnp.einsum("gl,gnl->gn", lag_total, start_table, precision=PRECISE)
    step_decay = jnp.exp(-decay_rate).T[:, :, None]
    crossing = jnp.sum(
        incoming_groups * step_decay * start_state.reshape(modes, groups, per_group), axis=2
    )
    local_residue = local_residue + crossing.T
    residue_total = lax.psum(local_residue, "seq")
    filter_grad = residue_total * jnp.sqrt(2.0 * decay_rate / modes) / math.sqrt(total)
    return (mixer_out, query_grad, key_grad, value_grad, filter_grad)


def solution(mesh):
    return jax.shard_map(
        per_device,
        mesh=mesh,
        in_specs=(
            P(("grp", "seq"), None),
            P(("grp", "seq"), None),
            P(("grp", "seq"), None),
            P(("grp", "seq"), None),
            P(),
            P(),
        ),
        out_specs=(
            P(("grp", "seq"), None),
            P(("grp", "seq"), None),
            P(("grp", "seq"), None),
            P(("grp", "seq"), None),
            P("grp", None),
        ),
        check_vma=False,
    )
```

profile of v0, /device:TPU:0, one launch (start us, length us, event | category | flops | bytes accessed | tf_op | source)
XLA Modules:
  0.0 536.8 jit_solution(13908101762132657484)
XLA Ops:
  14.6 54.5 %gather_fusion.3 = f32[16384,32]{1,0:T(8,128)} fusion(f32[32,128]{0,1:T(8,128)S(1)} %copy.93, s32[16384]{0:T(1024)S(1)} %bitcast_clamp_fusion), kind=kCustom, calls=%fused_computation.3 | custom fusion | bytes 4259840 | tf_op jit(solution)/shard_map/gather | solution.py:90
  69.1 6.5 %copy.70 = f32[128,128,32]{1,0,2:T(8,128)} copy(f32[128,128,32]{2,1,0:T(8,128)} %bitcast.119) | data formatting | bytes 4194304 | tf_op jit(solution)/shard_map/gather | solution.py:90
  75.7 54.5 %gather_fusion.2 = f32[16384,32]{1,0:T(8,128)} fusion(f32[32,128]{0,1:T(8,128)S(1)} %copy.92, s32[16384]{0:T(1024)S(1)} %bitcast_clamp_fusion), kind=kCustom, calls=%fused_computation.2 | custom fusion | bytes 4259840 | tf_op jit(solution)/shard_map/gather | solution.py:90
  130.2 6.5 %copy.69 = f32[128,128,32]{1,0,2:T(8,128)} copy(f32[128,128,32]{2,1,0:T(8,128)} %bitcast.120) | data formatting | bytes 4194304 | tf_op jit(solution)/shard_map/gather | solution.py:90
  136.8 54.5 %gather_fusion.1 = f32[16384,32]{1,0:T(8,128)} fusion(f32[32,128]{0,1:T(8,128)S(1)} %copy.91, s32[16384]{0:T(1024)S(1)} %bitcast_clamp_fusion), kind=kCustom, calls=%fused_computation.1 | custom fusion | bytes 4259840 | tf_op jit(solution)/shard_map/gather | solution.py:90
  191.3 6.5 %copy.68 = f32[128,128,32]{1,0,2:T(8,128)} copy(f32[128,128,32]{2,1,0:T(8,128)} %bitcast.121) | data formatting | bytes 4194304 | tf_op jit(solution)/shard_map/gather | solution.py:90
  197.9 54.5 %gather_fusion = f32[16384,32]{1,0:T(8,128)} fusion(f32[32,128]{0,1:T(8,128)S(1)} %copy.90, s32[16384]{0:T(1024)S(1)} %bitcast_clamp_fusion), kind=kCustom, calls=%fused_computation | custom fusion | bytes 4259840 | tf_op jit(solution)/shard_map/gather | solution.py:90
  252.4 6.5 %copy.67 = f32[128,128,32]{1,0,2:T(8,128)} copy(f32[128,128,32]{2,1,0:T(8,128)} %bitcast.118) | data formatting | bytes 4194304 | tf_op jit(solution)/shard_map/gather | solution.py:90
  259.0 3.6 fusion.3
  270.2 17.5 %while.31 = (s32[]{:T(128)}, f32[16,2048]{1,0:T(8,128)S(1)}, s32[]{:T(128)}, f32[16,16,2048]{2,1,0:T(8,128)}, f32[16,16,2048]{2,1,0:T(8,128)}, /*index=5*/s32[]{:T(128)}, s32[]{:T(128)}, s32[]{:T(128)}, s32[]{:T(128)}) while((s32[]{:T(128)}, f32[16,2048]{1,0:T(8,128)S(1)}, s32[]{:T(128)}, f32[16,16,2048]{2,1,0:T(8,128)}, ...), condition=%wide.region_3.4_spmd.clone, body=%wide.region_2.3_spmd.clone.sunk | while | flops 131080 | bytes 524459 | solution.py:26
  288.1 3.9 convolution_add_fusion
  297.8 4.8 fusion.69
  302.5 4.8 fusion.71
  310.2 14.9 %rev.15 = f32[32,128,128]{2,1,0:T(8,128)S(1)} reverse(f32[32,128,128]{2,1,0:T(8,128)} %fusion.69), dimensions={2} | reverse | bytes 4194304 | tf_op jit(solution)/shard_map/rev | solution.py:31
  330.3 9.6 %reshape.134 = f32[32,128,255]{2,1,0:T(8,128)} reshape(f32[32,32640]{1,0:T(8,128)} %slice.102) | data formatting | bytes 8355840 | tf_op jit(solution)/shard_map/reshape | solution.py:34
  339.9 14.9 %rev.14 = f32[32,128,128]{2,1,0:T(8,128)S(1)} reverse(f32[32,128,128]{2,1,0:T(8,128)} %fusion.71), dimensions={2} | reverse | bytes 4194304 | tf_op jit(solution)/shard_map/rev | solution.py:31
  360.1 9.5 %reshape.132 = f32[32,128,255]{2,1,0:T(8,128)} reshape(f32[32,32640]{1,0:T(8,128)} %slice.99) | data formatting | bytes 8355840 | tf_op jit(solution)/shard_map/reshape | solution.py:34
  369.6 5.8 %fusion.73 = f32[32,128,128]{2,1,0:T(8,128)} fusion(f32[128,16,128]{2,1,0:T(8,128)S(1)} %bitcast.140, f32[128,16,128]{2,1,0:T(8,128)} %bitcast.127), kind=kOutput, calls=%fused_computation.95 | convolution fusion | flops 100663296 | bytes 3407872 | tf_op jit(solution)/shard_map/gkt,gks->gts/dot_general | solution.py:95
  375.3 15.4 %rev.13 = f32[32,128,128]{2,1,0:T(8,128)S(1)} reverse(f32[32,128,128]{2,1,0:T(8,128)} %fusion.73), dimensions={2} | reverse | bytes 4194304 | tf_op jit(solution)/shard_map/rev | solution.py:31
  395.9 9.5 %reshape.130 = f32[32,128,255]{2,1,0:T(8,128)} reshape(f32[32,32640]{1,0:T(8,128)} %slice.96) | data formatting | bytes 8355840 | tf_op jit(solution)/shard_map/reshape | solution.py:34
  405.4 5.7 %fusion.75 = f32[32,128,128]{2,1,0:T(8,128)} fusion(f32[128,16,128]{2,1,0:T(8,128)S(1)} %bitcast.141, f32[128,16,128]{2,1,0:T(8,128)} %bitcast.128), kind=kOutput, calls=%fused_computation.97 | convolution fusion | flops 100663296 | bytes 3407872 | tf_op jit(solution)/shard_map/gkt,gks->gts/dot_general | solution.py:95
  411.1 14.9 %rev.12 = f32[32,128,128]{2,1,0:T(8,128)S(1)} reverse(f32[32,128,128]{2,1,0:T(8,128)} %fusion.75), dimensions={2} | reverse | bytes 4194304 | tf_op jit(solution)/shard_map/rev | solution.py:31
  431.2 9.5 %reshape.128 = f32[32,128,255]{2,1,0:T(8,128)} reshape(f32[32,32640]{1,0:T(8,128)} %slice.93) | data formatting | bytes 8355840 | tf_op jit(solution)/shard_map/reshape | solution.py:34
  440.8 4.8 slice_reduce_fusion
  445.5 3.4 slice_reduce_fusion.2
  450.9 5.8 %fusion.5 = f32[32,16,128]{2,1,0:T(8,128)} fusion(f32[128,16,128]{2,1,0:T(8,128)S(1)} %bitcast.129, f32[128,128,32]{1,0,2:T(8,128)} %copy.70, pred[128,128]{1,0:T(8,128)(4,1)S(1)} %subtract_compare_fusion), kind=kOutput, calls=%fused_computation.16 | convolution fusion | flops 101187584 | bytes 3424256 | tf_op jit(solution)/shard_map/gts,gks->gkt/dot_general | solution.py:93
  456.7 4.1 fusion.9
  460.8 4.0 fusion.13
  464.8 4.1 fusion.17
  468.9 17.5 %while.30 = (s32[]{:T(128)}, f32[16,2048]{1,0:T(8,128)S(1)}, s32[]{:T(128)}, f32[16,16,2048]{2,1,0:T(8,128)}, f32[16,16,2048]{2,1,0:T(8,128)}, /*index=5*/s32[]{:T(128)}, s32[]{:T(128)}) while((s32[]{:T(128)}, f32[16,2048]{1,0:T(8,128)S(1)}, s32[]{:T(128)}, f32[16,16,2048]{2,1,0:T(8,128)}, f32[16,16,2048]{2,1,0:T(8,128)}, ...), condition=%wide.region_1.2_spmd.clone, body=%wide.region_0.1_spmd.clone.sunk | while | flops 131076 | bytes 524397 | solution.py:26
  486.9 2.8 convolution_add_fusion.1
  494.0 35.4 %psum.7 = f32[128,16]{0,1:T(8,128)S(1)} all-reduce(f32[128,16]{0,1:T(8,128)S(1)} %bitcast_add_fusion.1), channel_id=1, replica_groups=mesh['grp'=2,'seq'=16] {'seq'}, use_global_device_ids=true, to_apply=%region_9.10 | all-reduce | flops 2048 | bytes 16384 | tf_op jit(solution)/shard_map/psum | solution.py:120
  (137 shorter events, 86.5 us)
Async XLA Ops:
  7.2 2.6 copy-start.13
  7.2 2.6 copy-start.14
  7.2 263.1 %all-gather.4.cloned.1.call-start = ((), (), s32[]{:S(2)}) async-start(), calls=%async_computation | async-start | bytes 2228224 | tf_op jit(solution)/shard_map/all_gather | solution.py:13
  9.7 260.6 %all-gather.8.cloned.1.call-start = ((), (), s32[]{:S(2)}) async-start(), calls=%async_computation.2 | async-start | bytes 2228224 | tf_op jit(solution)/shard_map/all_gather | solution.py:13
  10.2 257.5 %copy-start.3 = (f32[128,2048]{0,1:T(8,128)}, f32[128,2048]{0,1:T(8,128)S(1)}, u32[]{:S(2)}) copy-start(f32[128,2048]{0,1:T(8,128)S(1)} %copy.76) | copy-start | bytes 3145732
  13.2 455.8 %all-gather.6.cloned.1.call-start = ((), (), s32[]{:S(2)}) async-start(), calls=%async_computation.1 | async-start | bytes 2228224 | tf_op jit(solution)/shard_map/all_gather | solution.py:13
  259.0 3.6 copy-start.7
  262.6 2.6 copy-start.9
  265.1 2.6 copy-start.11
  288.1 5.4 %copy-start.15 = (bf16[128,2048]{1,0:T(8,128)(2,1)S(1)}, bf16[128,2048]{1,0:T(8,128)(2,1)}, u32[]{:S(2)}) copy-start(bf16[128,2048]{1,0:T(8,128)(2,1)} %param.11) | copy-start | bytes 1572868
  296.1 1.7 copy-start.4
  297.8 9.6 %copy-start.1 = (f32[128,2048]{0,1:T(8,128)}, f32[128,2048]{0,1:T(8,128)S(1)}, u32[]{:S(2)}) copy-start(f32[128,2048]{0,1:T(8,128)S(1)} %copy.65) | copy-start | bytes 3145732
  360.1 9.5 %copy-start.5 = (f32[128,2048]{0,1:T(8,128)S(1)}, f32[128,2048]{0,1:T(8,128)}, u32[]{:S(2)}) copy-start(f32[128,2048]{0,1:T(8,128)} %copy-done.3) | copy-start | bytes 3145732
  395.9 9.5 %copy-start.6 = (f32[128,2048]{0,1:T(8,128)S(1)}, f32[128,2048]{0,1:T(8,128)}, u32[]{:S(2)}) copy-start(f32[128,2048]{0,1:T(8,128)} %copy-done.3) | copy-start | bytes 3145732
  440.8 4.8 copy-start
  445.5 5.3 copy-start.2
  450.9 5.8 %copy-start.8 = (f32[128,128,32]{1,0,2:T(8,128)S(1)}, f32[128,128,32]{1,0,2:T(8,128)}, u32[]{:S(2)}) copy-start(f32[128,128,32]{1,0,2:T(8,128)} %copy.69) | copy-start | bytes 6291460
  456.7 4.1 copy-start.10
  460.8 4.1 copy-start.12
  468.9 17.9 %copy-start.17 = (f32[32,16,128]{2,1,0:T(8,128)S(1)}, f32[32,16,128]{2,1,0:T(8,128)}, u32[]{:S(2)}) copy-start(f32[32,16,128]{2,1,0:T(8,128)} %fusion.5) | copy-start | bytes 786436
  468.9 17.9 %copy-start.18 = (f32[32,16,128]{2,1,0:T(8,128)S(1)}, f32[32,16,128]{2,1,0:T(8,128)}, u32[]{:S(2)}) copy-start(f32[32,16,128]{2,1,0:T(8,128)} %fusion.9) | copy-start | bytes 786436
  468.9 18.0 %copy-start.19 = (f32[32,16,128]{2,1,0:T(8,128)S(1)}, f32[32,16,128]{2,1,0:T(8,128)}, u32[]{:S(2)}) copy-start(f32[32,16,128]{2,1,0:T(8,128)} %fusion.13) | copy-start | bytes 786436
  468.9 18.0 %copy-start.20 = (f32[32,16,128]{2,1,0:T(8,128)S(1)}, f32[32,16,128]{2,1,0:T(8,128)}, u32[]{:S(2)}) copy-start(f32[32,16,128]{2,1,0:T(8,128)} %fusion.17) | copy-start | bytes 786436
  491.2 38.3 %copy-start.16 = (f32[128,16]{0,1:T(8,128)S(1)}, f32[128,16]{0,1:T(8,128)}, u32[]{:S(2)}) copy-start(f32[128,16]{0,1:T(8,128)} %param.14) | copy-start | bytes 24580
Sparse Core Ops, SparseCore 0:
  10.2 44.0 all-gather.3
  57.1 40.1 all-gather.7
  310.3 44.0 all-gather.5
where the time goes:
time: 544 us; the launch traced here: 537 us
  local copies, waits for them, and re-layouts  373 us (69%)
  matrix products  62.4 us (11%)
  other arithmetic  50.1 us (9%)
  blocking collectives  35.4 us (7%)
  between operations  14.4 us (3%)
    gather x8, local copies, waits for them, and re-layouts, per_device(): toeplitz = jnp.where(causal, lag_filter[group_slice][:, clipped], 0.0)  244 us
    rev x4, local copies, waits for them, and re-layouts, lag_sums(): flipped = correlation[:, :, ::-1]  60.2 us
    reshape x4, local copies, waits for them, and re-layouts, lag_sums(): skewed = flattened.reshape(groups_here, length, 2 * length - 1)  38.2 us
    psum x1, blocking collectives, per_device(): residue_total = lax.psum(local_residue, 'seq')  35.4 us
    select_n x32, other arithmetic, hop(): return jax.tree.map(lambda a, b: jnp.where(reached, a, b), new, before)  34.3 us
    dot_general x4, matrix products, per_device(): jnp.einsum('gkt,gks->gts', upstream_block, gated_block, precision=PRECISE)  21 us
    dot_general x4, matrix products, per_device(): jnp.einsum('gts,gks->gkt', toeplitz, gated_block, precision=PRECISE)  18 us
    dot_general x4, matrix products, per_device(): jnp.einsum('gts,gkt->gks', toeplitz, upstream_block, precision=PRECISE)  11.2 us
  transfers between devices with their start and end apart: 3, of which 0 were waited for; matrix products, arithmetic and copies ran while one was open for 78% of the time, Pallas kernels for 0%

commit v1 on v0

v1 whole, which is shorter than its diff:
```python
import functools
import math

import jax
import jax.numpy as jnp
from jax import lax
from jax.experimental import pallas as pl
from jax.experimental.pallas import tpu as pltpu
from jax.sharding import PartitionSpec as P

PER = 16
MODES = 16
LANES = 128
PACK = LANES // PER
F32 = jnp.float32
BF16 = jnp.bfloat16


def lane_iota(shape):
    return lax.broadcasted_iota(jnp.int32, shape, 1)


def row_iota(shape):
    return lax.broadcasted_iota(jnp.int32, shape, 0)


def split(value):
    high = value.astype(BF16)
    return high, (value - high.astype(F32)).astype(BF16)


def dot3(left, right):
    left_high, left_low = split(left)
    right_high, right_low = split(right)
    return jnp.dot(
        jnp.concatenate([left_high, left_high, left_low], axis=1),
        jnp.concatenate([right_high, right_low, right_high], axis=0),
        preferred_element_type=F32,
    )


def own_group(stack):
    group = lane_iota((MODES, LANES)) // PER
    total = jnp.zeros((MODES, LANES), F32)
    for g in range(PACK):
        total = total + jnp.where(group == g, stack[g * MODES : (g + 1) * MODES], 0.0)
    return total


def columns(transposed, block):
    return jnp.concatenate(
        [
            jnp.broadcast_to(transposed[:MODES, g : g + 1], (MODES, LANES))
            for g in range(block * PACK, (block + 1) * PACK)
        ],
        axis=0,
    )


def group_rows(product):
    width = product.shape[1]
    count = width // LANES
    tall = jnp.concatenate([product[:, i * LANES : (i + 1) * LANES] for i in range(count)], axis=0)
    high, low = split(tall)
    same = (lane_iota((LANES, LANES)) // PER == row_iota((LANES, LANES)) // PER).astype(F32)
    sums = jnp.dot(
        jnp.concatenate([high, low], axis=1),
        jnp.concatenate([same, same], axis=0).astype(BF16),
        preferred_element_type=F32,
    )
    pick = lane_iota((MODES, LANES)) % PER == row_iota((MODES, LANES))
    rows = [
        jnp.sum(jnp.where(pick, sums[i * MODES : (i + 1) * MODES], 0.0), axis=0, keepdims=True)
        for i in range(count)
    ]
    return jnp.concatenate(rows, axis=1)


def position():
    return lax.axis_index("seq")


def bit_of(index, mask):
    return (index & mask) != 0


def params(limit=48):
    return pltpu.CompilerParams(vmem_limit_bytes=limit << 20)


def states_kernel(k_ref, v_ref, q_ref, c_ref, decay_ref, send_ref, keep_ref, rate_ref, pad_ref):
    step = pl.program_id(0)
    length, width = k_ref.shape
    groups = decay_ref.shape[0]
    pad_ref[:groups, :MODES] = decay_ref[...]
    transposed = pad_ref[...].T
    time = lane_iota((LANES, length)).astype(F32)
    ends = []
    starts = []
    rates = []
    for block in range(width // LANES):
        lanes = slice(block * LANES, (block + 1) * LANES)
        rate = columns(transposed, block)
        gated = k_ref[:, lanes].astype(F32) * v_ref[:, lanes].astype(F32)
        upstream = q_ref[:, lanes].astype(F32) * c_ref[:, lanes].astype(F32)
        ends.append(own_group(dot3(jnp.exp(-rate * (length - 1.0 - time)), gated)))
        starts.append(own_group(dot3(jnp.exp(-rate * time), upstream)))
        rates.append(own_group(rate))
    rate_ref[...] = jnp.concatenate(rates, axis=1)
    both = jnp.concatenate(
        [jnp.concatenate(ends, axis=1), jnp.concatenate(starts, axis=1)], axis=0
    )
    steps = pl.num_programs(0)
    mine = (step >= steps // 2) == bit_of(position(), 1)
    place = pl.ds(pl.multiple_of((step % (steps // 2)) * width, width), width)

    @pl.when(mine)
    def _():
        keep_ref[:, place] = both

    @pl.when(jnp.logical_not(mine))
    def _():
        send_ref[:, place] = both


def states(k, v, q, c, decay):
    length, total = k.shape
    groups = decay.shape[0]
    steps = 4
    width = total // steps
    stream = pl.BlockSpec((length, width), lambda i: (0, i))
    whole = pl.BlockSpec((2 * MODES, total // 2), lambda i: (0, 0))
    return pl.pallas_call(
        states_kernel,
        grid=(steps,),
        in_specs=[stream] * 4 + [pl.BlockSpec((groups // steps, MODES), lambda i: (i, 0))],
        out_specs=[whole, whole, pl.BlockSpec((MODES, width), lambda i: (0, i))],
        out_shape=[
            jax.ShapeDtypeStruct((2 * MODES, total // 2), F32),
            jax.ShapeDtypeStruct((2 * MODES, total // 2), F32),
            jax.ShapeDtypeStruct((MODES, total), F32),
        ],
        scratch_shapes=[pltpu.VMEM((LANES, LANES), F32)],
        compiler_params=params(),
        name="states",
    )(k, v, q, c, decay)


def tables_kernel(length, decay_ref, residue_ref, weight_ref, fh_ref, fl_ref, bh_ref, bl_ref, pad_ref):
    groups = decay_ref.shape[0]
    width = weight_ref.shape[1]
    pad_ref[:groups, :MODES] = decay_ref[...]
    rates = pad_ref[...].T
    pad_ref[:groups, :MODES] = residue_ref[...] * jnp.sqrt(2.0 * decay_ref[...] / MODES)
    weights = pad_ref[...].T
    time = lane_iota((LANES, length)).astype(F32)
    for block in range(width // LANES):
        lanes = slice(block * LANES, (block + 1) * LANES)
        rate = columns(rates, block)
        weight = columns(weights, block)
        weight_ref[:, lanes] = own_group(weight)
        high, low = split((weight * jnp.exp(-rate * (time + 1.0))).T)
        fh_ref[:, lanes] = high
        fl_ref[:, lanes] = low
        high, low = split((weight * jnp.exp(-rate * (length - time))).T)
        bh_ref[:, lanes] = high
        bl_ref[:, lanes] = low


def tables(decay, residue, length):
    groups = decay.shape[0]
    total = groups * PER
    steps = 4
    small = pl.BlockSpec((groups // steps, MODES), lambda i: (i, 0))
    tall = pl.BlockSpec((length, total // steps), lambda i: (0, i))
    return pl.pallas_call(
        functools.partial(tables_kernel, length),
        grid=(steps,),
        in_specs=[small, small],
        out_specs=[pl.BlockSpec((MODES, total // steps), lambda i: (0, i))] + [tall] * 4,
        out_shape=[jax.ShapeDtypeStruct((MODES, total), F32)]
        + [jax.ShapeDtypeStruct((length, total), BF16)] * 4,
        scratch_shapes=[pltpu.VMEM((LANES, LANES), F32)],
        compiler_params=params(),
        name="tables",
    )(decay, residue)


def lag_kernel(k_ref, v_ref, q_ref, c_ref, rate_ref, out_ref, gated_ref, upstream_ref):
    step = pl.program_id(0)
    length, width = k_ref.shape
    gated_ref[...] = k_ref[...].astype(F32) * v_ref[...].astype(F32)
    upstream_ref[...] = q_ref[...].astype(F32) * c_ref[...].astype(F32)
    decay = jnp.exp(-rate_ref[...])

    def eight(i, carry):
        state, total = carry
        base = pl.multiple_of(i * 8, 8)
        x_rows = gated_ref[pl.ds(base, 8), :]
        u_rows = upstream_ref[pl.ds(base, 8), :]
        for j in range(8):
            state = state * decay + jnp.broadcast_to(x_rows[j : j + 1], (MODES, width))
            total = total + state * jnp.broadcast_to(u_rows[j : j + 1], (MODES, width))
        return state, total

    zero = jnp.zeros((MODES, width), F32)
    _, total = lax.fori_loop(0, length // 8, eight, (zero, zero))
    out_ref[pl.ds(step, 1), :] = group_rows(total)


def lag_part(k, v, q, c, rate):
    length, total = k.shape
    steps = 4
    width = total // steps
    stream = pl.BlockSpec((length, width), lambda i: (0, i))
    return pl.pallas_call(
        lag_kernel,
        grid=(steps,),
        in_specs=[stream] * 4 + [pl.BlockSpec((MODES, width), lambda i: (0, i))],
        out_specs=pl.BlockSpec((8, width), lambda i: (0, 0)),
        out_shape=jax.ShapeDtypeStruct((8, width), F32),
        scratch_shapes=[pltpu.VMEM((length, width), F32)] * 2,
        compiler_params=params(),
        name="lag_part",
    )(k, v, q, c, rate)


def fold(first, second, shift, row):
    low = (row & shift) == 0
    kept = jnp.where(low, first, second)
    moved = jnp.where(low, second, first)
    return kept + pltpu.roll(moved, shift, 0)


def scan_kernel(reverse, a_ref, b_ref, rate_ref, weight_ref, out_ref, in_ref):
    length, width = a_ref.shape
    in_ref[...] = a_ref[...].astype(F32) * b_ref[...].astype(F32)
    decay = jnp.exp(-rate_ref[...])
    weight = weight_ref[...]
    row = row_iota((8, width))

    def eight(i, state):
        at = length // 8 - 1 - i if reverse else i
        base = pl.multiple_of(at * 8, 8)
        rows = in_ref[pl.ds(base, 8), :]
        parts = [None] * 8
        for j in reversed(range(8)) if reverse else range(8):
            state = state * decay + jnp.broadcast_to(rows[j : j + 1], (MODES, width))
            product = state * weight
            parts[j] = product[:8] + product[8:]
        four = [fold(parts[2 * j], parts[2 * j + 1], 1, row) for j in range(4)]
        two = [fold(four[2 * j], four[2 * j + 1], 2, row) for j in range(2)]
        out_ref[pl.ds(base, 8), :] = fold(two[0], two[1], 4, row)
        return state

    lax.fori_loop(0, length // 8, eight, jnp.zeros((MODES, width), F32))


def scan_part(a, b, rate, weight, reverse):
    length, total = a.shape
    steps = 4
    width = total // steps
    stream = pl.BlockSpec((length, width), lambda i: (0, i))
    wide = pl.BlockSpec((MODES, width), lambda i: (0, i))
    return pl.pallas_call(
        functools.partial(scan_kernel, reverse),
        grid=(steps,),
        in_specs=[stream, stream, wide, wide],
        out_specs=stream,
        out_shape=jax.ShapeDtypeStruct((length, total), F32),
        scratch_shapes=[pltpu.VMEM((length, width), F32)],
        compiler_params=params(),
        name="scan_back" if reverse else "scan_fore",
    )(a, b, rate, weight)


def join(own, other, late, power, step_decay):
    own_end, own_start = own[:MODES], own[MODES : 2 * MODES]
    other_end, other_start = other[:MODES], other[MODES : 2 * MODES]
    early_end = jnp.where(late, other_end, own_end)
    late_end = jnp.where(late, own_end, other_end)
    early_start = jnp.where(late, other_start, own_start)
    late_start = jnp.where(late, own_start, other_start)
    end = late_end + power * early_end
    start = early_start + power * late_start
    return end, start, early_end * late_start * step_decay


def pass_down(first, second, before, after, power):
    early = (before, second + power * after)
    late = (first + power * before, after)
    return early, late


def quarter_of(index, half):
    both = (index & 1) * 2 + ((index >> 1) & 1)
    return pl.ds(pl.multiple_of(both * half, half), half)


def core_kernel(length, own_ref, other_ref, rate_ref, send_ref, keep_ref, lag_ref):
    index = position()
    half = own_ref.shape[1]
    quarter = half // 2
    place = pl.ds(pl.multiple_of((index & 1) * half, half), half)
    rate = rate_ref[:, place]
    end, start, cross = join(
        own_ref[...],
        other_ref[...],
        bit_of(index, 1),
        jnp.exp(-rate * length),
        jnp.exp(-rate),
    )
    both = jnp.concatenate([end, start], axis=0)
    second = bit_of(index, 2)
    keep_ref[...] = jnp.where(second, both[:, quarter:], both[:, :quarter])
    send_ref[...] = jnp.where(second, both[:, :quarter], both[:, quarter:])
    rows = group_rows(cross)
    lag_ref[0:1, :] = rows[:, :quarter]
    lag_ref[1:2, :] = rows[:, quarter:]


def core_join(length, own, other, rate):
    half = own.shape[1]
    return pl.pallas_call(
        functools.partial(core_kernel, length),
        out_shape=[
            jax.ShapeDtypeStruct((2 * MODES, half // 2), F32),
            jax.ShapeDtypeStruct((2 * MODES, half // 2), F32),
            jax.ShapeDtypeStruct((8, half // 2), F32),
        ],
        compiler_params=params(),
        name="core_join",
    )(own, other, rate)


def plane_kernel(length, own_ref, other_ref, lag_ref, core_lag_ref, rate_ref, out_ref):
    index = position()
    rate = rate_ref[:, quarter_of(index, own_ref.shape[1])]
    end, start, cross = join(
        own_ref[...],
        other_ref[...],
        bit_of(index, 2),
        jnp.exp(-rate * (2 * length)),
        jnp.exp(-rate),
    )
    out_ref[:MODES] = end
    out_ref[MODES : 2 * MODES] = start
    base = 2 * MODES
    out_ref[base : base + 4] = lag_ref[0:4]
    out_ref[base + 4 : base + 6] = core_lag_ref[0:2]
    out_ref[base + 6 : base + 7] = group_rows(cross)
    out_ref[base + 7 : base + 8] = jnp.zeros_like(out_ref[base + 7 : base + 8])


def plane_join(length, own, other, lag, core_lag, rate):
    return pl.pallas_call(
        functools.partial(plane_kernel, length),
        out_shape=jax.ShapeDtypeStruct((2 * MODES + 8, own.shape[1]), F32),
        compiler_params=params(),
        name="plane_join",
    )(own, other, lag, core_lag, rate)


def add_row(rows, extra):
    return rows + jnp.where(row_iota(rows.shape) == 6, extra, 0.0)


def line_kernel(length, mask, final, own_ref, other_ref, rate_ref, out_ref):
    index = position()
    rate = rate_ref[:, quarter_of(index, own_ref.shape[1])]
    end, start, cross = join(
        own_ref[...],
        other_ref[...],
        bit_of(index, mask),
        jnp.exp(-rate * (mask * length)),
        jnp.exp(-rate),
    )
    rows = add_row(own_ref[2 * MODES :] + other_ref[2 * MODES :], group_rows(cross))
    if final:
        out_ref[:MODES] = jnp.where(bit_of(index, 2 * mask), start, end)
        out_ref[MODES:] = rows
    else:
        out_ref[:MODES] = end
        out_ref[MODES : 2 * MODES] = start
        out_ref[2 * MODES :] = rows


def line_join(length, mask, final, own, other, rate):
    count = MODES + 8 if final else 2 * MODES + 8
    return pl.pallas_call(
        functools.partial(line_kernel, length, mask, final),
        out_shape=jax.ShapeDtypeStruct((count, own.shape[1]), F32),
        compiler_params=params(),
        name="line_join",
    )(own, other, rate)


def turn_kernel(length, masks, own_ref, other_ref, *refs):
    levels = refs[: len(masks) - 1]
    chip_ref, chip_other_ref, rate_ref, keep_ref, send_ref = refs[len(masks) - 1 :]
    index = position()
    rate = rate_ref[:, quarter_of(index, own_ref.shape[1])]
    own, other = own_ref[:MODES], other_ref[:MODES]
    late = bit_of(index, masks[-1])
    cross = own * other * jnp.exp(-rate)
    rows = add_row(own_ref[MODES:] + other_ref[MODES:], group_rows(cross))
    before = jnp.where(late, other, 0.0)
    after = jnp.where(late, 0.0, other)
    for mask, level in reversed(list(zip(masks[:-1], levels))):
        late = bit_of(index, mask)
        power = jnp.exp(-rate * (mask * length))
        before, after = (
            jnp.where(late, level[:MODES] + power * before, before),
            jnp.where(late, after, level[MODES : 2 * MODES] + power * after),
        )
    late = bit_of(index, 2)
    power = jnp.exp(-rate * (2 * length))
    early_end = jnp.where(late, chip_other_ref[:MODES], chip_ref[:MODES])
    late_start = jnp.where(late, chip_ref[MODES:], chip_other_ref[MODES:])
    early, later = pass_down(early_end, late_start, before, after, power)
    keep_ref[:MODES] = jnp.where(late, later[0], early[0])
    keep_ref[MODES : 2 * MODES] = jnp.where(late, later[1], early[1])
    keep_ref[2 * MODES :] = rows
    send_ref[:MODES] = jnp.where(late, early[0], later[0])
    send_ref[MODES : 2 * MODES] = jnp.where(late, early[1], later[1])
    send_ref[2 * MODES :] = rows


def turn(length, masks, own, other, levels, chip, chip_other, rate):
    shape = jax.ShapeDtypeStruct((2 * MODES + 8, own.shape[1]), F32)
    return pl.pallas_call(
        functools.partial(turn_kernel, length, masks),
        out_shape=[shape, shape],
        compiler_params=params(),
        name="turn",
    )(own, other, *levels, chip, chip_other, rate)


def chip_kernel(length, own_ref, other_ref, core_ref, core_other_ref, rate_ref, keep_ref, send_ref):
    index = position()
    quarter = own_ref.shape[1]
    half = 2 * quarter
    rate = rate_ref[:, pl.ds(pl.multiple_of((index & 1) * half, half), half)]
    power = jnp.exp(-rate * length)
    second = bit_of(index, 2)
    own, other = own_ref[...], other_ref[...]
    left = jnp.where(second, other, own)
    right = jnp.where(second, own, other)
    around = jnp.concatenate([left[: 2 * MODES], right[: 2 * MODES]], axis=1)
    before, after = around[:MODES], around[MODES:]
    late = bit_of(index, 1)
    early_end = jnp.where(late, core_other_ref[:MODES], core_ref[:MODES])
    late_start = jnp.where(late, core_ref[MODES:], core_other_ref[MODES:])
    early, later = pass_down(early_end, late_start, before, after, power)
    base = 2 * MODES
    rows = own[base:] + other[base:]
    cross = jnp.concatenate(
        [rows[4:5] + left[base + 6 : base + 7], rows[5:6] + right[base + 6 : base + 7]], axis=1
    )
    sums = jnp.concatenate(
        [
            jnp.concatenate([rows[0:1], rows[1:2]], axis=1),
            jnp.concatenate([rows[2:3], rows[3:4]], axis=1),
            cross,
            jnp.zeros((5, half), F32),
        ],
        axis=0,
    )
    keep_ref[:MODES] = jnp.where(late, later[0], early[0])
    keep_ref[MODES:base] = jnp.where(late, later[1], early[1])
    keep_ref[base:] = sums
    send_ref[:MODES] = jnp.where(late, early[0], later[0])
    send_ref[MODES:base] = jnp.where(late, early[1], later[1])
    send_ref[base:] = sums


def chip_split(length, own, other, core, core_other, rate):
    shape = jax.ShapeDtypeStruct((2 * MODES + 8, 2 * own.shape[1]), F32)
    return pl.pallas_call(
        functools.partial(chip_kernel, length),
        out_shape=[shape, shape],
        compiler_params=params(),
        name="chip_split",
    )(own, other, core, core_other, rate)


def spread(state):
    same = lane_iota((LANES, LANES)) // PER == row_iota((LANES, LANES)) // MODES
    return jnp.where(same, jnp.concatenate([state] * PACK, axis=0), 0.0)


def carried(high_ref, low_ref, lanes, state):
    high, low = split(spread(state))
    table = high_ref[:, lanes]
    return jnp.dot(
        jnp.concatenate([table, table, low_ref[:, lanes]], axis=1),
        jnp.concatenate([high, low, high], axis=0),
        preferred_element_type=F32,
    )


def outputs_kernel(
    scale,
    own_ref,
    other_ref,
    decay_ref,
    q_ref,
    k_ref,
    v_ref,
    c_ref,
    fore_ref,
    back_ref,
    fh_ref,
    fl_ref,
    bh_ref,
    bl_ref,
    out_ref,
    query_ref,
    key_ref,
    value_ref,
    grad_ref,
):
    step = pl.program_id(0)
    steps = pl.num_programs(0)
    index = position()
    width = q_ref.shape[1]
    late = bit_of(index, 1)
    mine = (step >= steps // 2) == late
    place = pl.ds(pl.multiple_of((step % (steps // 2)) * width, width), width)
    around = jnp.where(mine, own_ref[: 2 * MODES, place], other_ref[: 2 * MODES, place])
    for block in range(width // LANES):
        lanes = slice(block * LANES, (block + 1) * LANES)
        mixed = fore_ref[:, lanes] + carried(fh_ref, fl_ref, lanes, around[:MODES, lanes])
        out_ref[:, lanes] = (q_ref[:, lanes].astype(F32) * mixed).astype(BF16)
        query_ref[:, lanes] = (c_ref[:, lanes].astype(F32) * mixed).astype(BF16)
        grad = back_ref[:, lanes] + carried(bh_ref, bl_ref, lanes, around[MODES:, lanes])
        key_ref[:, lanes] = (grad * v_ref[:, lanes].astype(F32)).astype(BF16)
        value_ref[:, lanes] = (grad * k_ref[:, lanes].astype(F32)).astype(BF16)

    @pl.when(step == 0)
    def _():
        base = 2 * MODES
        half = own_ref.shape[1]
        own, other = own_ref[base:], other_ref[base:]
        lags = own[0:2] + other[0:2]
        first = jnp.where(late, other[2:3], own[2:3])
        second = jnp.where(late, own[2:3], other[2:3])
        rows = [lags[0:1] + first, lags[1:2] + second]
        blocks = half // LANES
        for i in range(2 * blocks):
            row = rows[i // blocks][:, (i % blocks) * LANES : (i % blocks + 1) * LANES]
            spun = jnp.broadcast_to(row, (PACK, LANES))
            for bit in (1, 2, 4):
                turned = pltpu.roll(spun, LANES - bit * MODES, 1)
                spun = jnp.where((row_iota(spun.shape) & bit) != 0, turned, spun)
            groups = slice(i * PACK, (i + 1) * PACK)
            rate = decay_ref[groups, :]
            grad_ref[groups, :] = spun[:, :MODES] * jnp.sqrt(2.0 * rate / MODES) * scale


def outputs(scale, own, other, decay, q, k, v, c, fore, back, table):
    length, total = q.shape
    steps = 4
    width = total // steps
    stream = pl.BlockSpec((length, width), lambda i: (0, i))
    whole = pl.BlockSpec(own.shape, lambda i: (0, 0))
    small = pl.BlockSpec(decay.shape, lambda i: (0, 0))
    wide = jax.ShapeDtypeStruct((length, total), BF16)
    return pl.pallas_call(
        functools.partial(outputs_kernel, scale),
        grid=(steps,),
        in_specs=[whole, whole, small] + [stream] * 10,
        out_specs=[stream] * 4 + [small],
        out_shape=[wide] * 4 + [jax.ShapeDtypeStruct(decay.shape, F32)],
        compiler_params=params(),
        name="outputs",
    )(own, other, decay, q, k, v, c, fore, back, *table)


def per_device(query, key, value, cotangent, decay, residue):
    length = query.shape[0]
    count = lax.axis_size("seq")
    masks = [1 << i for i in range(2, count.bit_length() - 1)]

    def swap(array, mask):
        return lax.ppermute(array, "seq", [(i, i ^ mask) for i in range(count)])

    core_send, core, rate = states(key, value, query, cotangent, decay)
    core_other = swap(core_send, 1)
    weight, *table = tables(decay, residue, length)
    chip_send, chip, core_lag = core_join(length, core, core_other, rate)
    chip_other = swap(chip_send, 2)
    lag = lag_part(key, value, query, cotangent, rate)
    message = plane_join(length, chip, chip_other, lag, core_lag, rate)
    levels = []
    for mask in masks[:-1]:
        levels.append(swap(message, mask))
        message = line_join(length, mask, mask == masks[-2], message, levels[-1], rate)
    fore = scan_part(key, value, rate, weight, False)
    top = swap(message, masks[-1])
    keep, send = turn(length, masks, message, top, levels, chip, chip_other, rate)
    back = scan_part(query, cotangent, rate, weight, True)
    arrived = swap(send, 2)
    own, send = chip_split(length, keep, arrived, core, core_other, rate)
    other = swap(send, 1)
    scale = 1.0 / math.sqrt(length * count)
    return outputs(scale, own, other, decay, query, key, value, cotangent, fore, back, table)


def solution(mesh):
    rows = P(("grp", "seq"), None)
    return jax.shard_map(
        per_device,
        mesh=mesh,
        in_specs=(rows, rows, rows, rows, P(), P()),
        out_specs=(rows, rows, rows, rows, P("grp", None)),
        check_vma=False,
    )
```

time: 544 us -> 47 us (0.09); the launches traced: 537 us -> 46.6 us
  local copies, waits for them, and re-layouts: 373 us -> 5.75 us
  matrix products: 62.4 us -> 0 us
  other arithmetic: 50.1 us -> 0 us
  blocking collectives: 35.4 us -> 0 us
  Pallas kernels: 0 us -> 21.5 us
  between operations: 14.4 us -> 0.78 us
  waiting for transfers between devices: 0.07 us -> 9.98 us
  starting transfers between devices: 0.59 us -> 8.61 us
    gather x8 -> x0, local copies, waits for them, and re-layouts: 244 us -> none  [per_device(): toeplitz = jnp.where(causal, lag_filter[group_slice][:, clipped], 0.0)]
    dot_general x17 -> x0, matrix products: 62.4 us -> none  [the longest x4 21 us: per_device(): jnp.einsum('gkt,gks->gts', upstream_block, gated_block, precision=PRECISE)]
    rev x4 -> x0, local copies, waits for them, and re-layouts: 60.2 us -> none  [lag_sums(): flipped = correlation[:, :, ::-1]]
    reshape x7 -> x0, local copies, waits for them, and re-layouts: 41.6 us -> none  [the longest x4 38.2 us: lag_sums(): skewed = flattened.reshape(groups_here, length, 2 * length - 1)]
    psum x1 -> x0, blocking collectives: 35.4 us -> none  [per_device(): residue_total = lax.psum(local_residue, 'seq')]
    select_n x32 -> x0, other arithmetic: 34.3 us -> none  [hop(): return jax.tree.map(lambda a, b: jnp.where(reached, a, b), new, before)]
    pallas_call x0 -> x11, Pallas kernels: none -> 21.5 us  [the longest x2 7.82 us: scan_part(): pl.pallas_call(functools.partial(scan_kernel, reverse), grid=(steps,), in...]
    ppermute x0 -> x6, waiting for transfers between devices: none -> 9.98 us  [swap(): return lax.ppermute(array, 'seq', [(i, i ^ mask) for i in range(count)])]
  transfers between devices with their start and end apart: 3 -> 6, of which waited for: 0 -> 4; matrix products, arithmetic and copies ran while one was open for 78% -> 0% of each run, Pallas kernels for 0% -> 29%
where the time goes in v1:
time: 47 us; the launch traced here: 46.6 us
  Pallas kernels  21.5 us (46%)
  waiting for transfers between devices  9.98 us (21%)
  starting transfers between devices  8.61 us (18%)
  local copies, waits for them, and re-layouts  5.75 us (12%)
  between operations  0.78 us (2%)
    ppermute x6, waiting for transfers between devices, swap(): return lax.ppermute(array, 'seq', [(i, i ^ mask) for i in range(count)])  9.98 us
    ppermute x6, starting transfers between devices, swap(): return lax.ppermute(array, 'seq', [(i, i ^ mask) for i in range(count)])  8.61 us
    pallas_call x2, Pallas kernels, scan_part(): pl.pallas_call(functools.partial(scan_kernel, reverse), grid=(steps,), in...  7.82 us
    unnamed x22, local copies, waits for them, and re-layouts  5.08 us
    pallas_call x1, Pallas kernels, outputs(): pl.pallas_call(functools.partial(outputs_kernel, scale), grid=(steps,), i...  4.66 us
    pallas_call x1, Pallas kernels, lag_part(): pl.pallas_call(lag_kernel, grid=(steps,), in_specs=[stream] * 4 + [pl.Blo...  3.52 us
    pallas_call x1, Pallas kernels, states(): pl.pallas_call(states_kernel, grid=(steps,), in_specs=[stream] * 4 + [pl....  2.42 us
    pallas_call x1, Pallas kernels, tables(): pl.pallas_call(functools.partial(tables_kernel, length), grid=(steps,), i...  2.27 us
  transfers between devices with their start and end apart: 6, of which 4 were waited for; matrix products, arithmetic and copies ran while one was open for 0% of the time, Pallas kernels for 29%

profile of v1, /device:TPU:0, one launch (start us, length us, event | category | flops | bytes accessed | tf_op | source)
XLA Modules:
  0.0 46.6 jit_solution(8950691205492830227)
XLA Ops:
  0.6 0.8 %copy.11.decay_ref = f32[128,16]{1,0:T(8,128)S(1)} copy(f32[128,16]{0,1:T(8,128)} %param.10) | data formatting | bytes 16384 | tf_op args[4]
  1.4 1.0 %copy-done = bf16[128,2048]{1,0:T(8,128)(2,1)S(1)} copy-done((bf16[128,2048]{1,0:T(8,128)(2,1)S(1)}, bf16[128,2048]{1,0:T(8,128)(2,1)}, u32[]{:S(2)}) %copy-start) | copy-done | bytes 524312
  2.5 1.0 %copy-done.2 = bf16[128,2048]{1,0:T(8,128)(2,1)S(1)} copy-done((bf16[128,2048]{1,0:T(8,128)(2,1)S(1)}, bf16[128,2048]{1,0:T(8,128)(2,1)}, u32[]{:S(2)}) %copy-start.2) | copy-done | bytes 524312
  3.5 1.0 %copy-done.4 = bf16[128,2048]{1,0:T(8,128)(2,1)S(1)} copy-done((bf16[128,2048]{1,0:T(8,128)(2,1)S(1)}, bf16[128,2048]{1,0:T(8,128)(2,1)}, u32[]{:S(2)}) %copy-start.4) | copy-done | bytes 524312
  4.6 1.0 %copy-done.6 = bf16[128,2048]{1,0:T(8,128)(2,1)S(1)} copy-done((bf16[128,2048]{1,0:T(8,128)(2,1)S(1)}, bf16[128,2048]{1,0:T(8,128)(2,1)}, u32[]{:S(2)}) %copy-start.6) | copy-done | bytes 524312
  5.6 2.4 %states.1 = (f32[32,1024]{1,0:T(8,128)S(1)}, f32[32,1024]{1,0:T(8,128)S(1)}, f32[16,2048]{1,0:T(8,128)S(1)}) custom-call(bf16[128,2048]{1,0:T(8,128)(2,1)S(1)} %copy-done, bf16[128,2048]{1,0:T(8,128)(2,1)S(1)} %copy-done.2, bf16[128,2048]{1,0:T(8,128)(2,1)S(1)} %copy-done.4, bf16[128,2048]{1,0:T(8,128)(2,1)S(1)} %copy-done.6, f32[128,16]{1,0:T(8,128)S(1)} %copy.11.decay_ref), custom_call_target="tpu_custom_call" | custom-call | tf_op jit(solution)/shard_map/states/pallas_call | solution.py:133
  8.0 0.5 %collective-permute-start = (f32[32,1024]{1,0:T(8,128)S(1)}, f32[32,1024]{1,0:T(8,128)S(1)}, u32[]{:S(2)}, u32[]{:S(2)}) collective-permute-start(f32[32,1024]{1,0:T(8,128)S(1)} %get-tuple-element.21), channel_id=1, source_target_pairs={{0,1},{1,0},{2,3},{3,2},{4,5},{5,4},{6,7},{7,6},{8,9},{9,8},{10,11... | collective-permute-start | bytes 393224 | tf_op jit(solution)/shard_map/ppermute | solution.py:586
  8.6 1.0 %collective-permute-done.other_ref.core_other_ref = f32[32,1024]{1,0:T(8,128)S(1)} collective-permute-done((f32[32,1024]{1,0:T(8,128)S(1)}, f32[32,1024]{1,0:T(8,128)S(1)}, u32[]{:S(2)}, u32[]{:S(2)}) %collective-permute-start) | collective-permute-done | bytes 131104 | tf_op jit(solution)/shard_map/ppermute | solution.py:586
  9.5 0.2 core_join.1
  9.7 2.9 %collective-permute-start.1 = (f32[32,512]{1,0:T(8,128)S(1)}, f32[32,512]{1,0:T(8,128)S(1)}, u32[]{:S(2)}, u32[]{:S(2)}) collective-permute-start(f32[32,512]{1,0:T(8,128)S(1)} %get-tuple-element.24), channel_id=1, source_target_pairs={{0,2},{1,3},{2,0},{3,1},{4,6},{5,7},{6,4},{7,5},{8,10},{9,11},{10,... | collective-permute-start | bytes 196616 | tf_op jit(solution)/shard_map/ppermute | solution.py:586
  12.7 3.5 %lag_part.1.lag_ref = f32[8,512]{1,0:T(8,128)S(1)} custom-call(bf16[128,2048]{1,0:T(8,128)(2,1)S(1)} %copy-done.1, bf16[128,2048]{1,0:T(8,128)(2,1)S(1)} %copy-done.3, bf16[128,2048]{1,0:T(8,128)(2,1)S(1)} %copy-done.4, bf16[128,2048]{1,0:T(8,128)(2,1)S(1)} %copy-done.6, f32[16,2048]{1,0:T(8,128)S(1)} %get-tuple-element.22.rate_ref.refs_3_), custom_call_target="tpu_custom_call" | custom-call | tf_op jit(solution)/shard_map/lag_part/pallas_call | solution.py:216
  16.2 0.0 collective-permute-done.1.other_ref.refs_2_
  16.2 0.2 plane_join.1.own_ref
  16.4 1.6 %collective-permute-start.2 = (f32[40,512]{1,0:T(8,128)S(1)}, f32[40,512]{1,0:T(8,128)S(1)}, u32[]{:S(2)}, u32[]{:S(2)}) collective-permute-start(f32[40,512]{1,0:T(8,128)S(1)} %plane_join.1.own_ref), channel_id=1, source_target_pairs={{0,4},{1,5},{2,6},{3,7},{4,0},{5,1},{6,2},{7,3},{8,12},{9,13},{10,... | collective-permute-start | bytes 245768 | tf_op jit(solution)/shard_map/ppermute | solution.py:586
  18.0 2.9 %collective-permute-done.2.other_ref.refs_0_ = f32[40,512]{1,0:T(8,128)S(1)} collective-permute-done((f32[40,512]{1,0:T(8,128)S(1)}, f32[40,512]{1,0:T(8,128)S(1)}, u32[]{:S(2)}, u32[]{:S(2)}) %collective-permute-start.2) | collective-permute-done | bytes 81952 | tf_op jit(solution)/shard_map/ppermute | solution.py:586
  20.9 0.2 line_join.1.own_ref
  21.1 0.0 copy-start.5
  21.1 0.0 copy-start.7
  21.1 2.7 %collective-permute-start.3 = (f32[24,512]{1,0:T(8,128)S(1)}, f32[24,512]{1,0:T(8,128)S(1)}, u32[]{:S(2)}, u32[]{:S(2)}) collective-permute-start(f32[24,512]{1,0:T(8,128)S(1)} %line_join.1.own_ref), channel_id=1, source_target_pairs={{0,8},{1,9},{2,10},{3,11},{4,12},{5,13},{6,14},{7,15},{8,0},{9,1},... | collective-permute-start | bytes 147464 | tf_op jit(solution)/shard_map/ppermute | solution.py:586
  23.7 2.4 %collective-permute-done.3.other_ref = f32[24,512]{1,0:T(8,128)S(1)} collective-permute-done((f32[24,512]{1,0:T(8,128)S(1)}, f32[24,512]{1,0:T(8,128)S(1)}, u32[]{:S(2)}, u32[]{:S(2)}) %collective-permute-start.3) | collective-permute-done | bytes 49184 | tf_op jit(solution)/shard_map/ppermute | solution.py:586
  26.1 0.2 turn.1
  26.3 0.8 %collective-permute-start.4 = (f32[40,512]{1,0:T(8,128)S(1)}, f32[40,512]{1,0:T(8,128)S(1)}, u32[]{:S(2)}, u32[]{:S(2)}) collective-permute-start(f32[40,512]{1,0:T(8,128)S(1)} %get-tuple-element.27), channel_id=1, source_target_pairs={{0,2},{1,3},{2,0},{3,1},{4,6},{5,7},{6,4},{7,5},{8,10},{9,11},{10,... | collective-permute-start | bytes 245768 | tf_op jit(solution)/shard_map/ppermute | solution.py:586
  27.1 3.7 %collective-permute-done.4.other_ref = f32[40,512]{1,0:T(8,128)S(1)} collective-permute-done((f32[40,512]{1,0:T(8,128)S(1)}, f32[40,512]{1,0:T(8,128)S(1)}, u32[]{:S(2)}, u32[]{:S(2)}) %collective-permute-start.4) | collective-permute-done | bytes 81952 | tf_op jit(solution)/shard_map/ppermute | solution.py:586
  30.8 0.1 chip_split.1
  30.9 0.1 collective-permute-start.5
  31.0 0.1 copy.13.residue_ref
  31.1 2.3 %tables.1 = (f32[16,2048]{1,0:T(8,128)S(1)}, bf16[128,2048]{1,0:T(8,128)(2,1)S(1)}, bf16[128,2048]{1,0:T(8,128)(2,1)S(1)}, bf16[128,2048]{1,0:T(8,128)(2,1)S(1)}, bf16[128,2048]{1,0:T(8,128)(2,1)S(1)}) custom-call(f32[128,16]{1,0:T(8,128)S(1)} %copy.11.decay_ref, f32[128,16]{1,0:T(8,128)S(1)} %copy.13.residue_ref), custom_call_target="tpu_custom_call" | custom-call | tf_op jit(solution)/shard_map/tables/pallas_call | solution.py:176
  33.4 3.9 %scan_back.1.back_ref = f32[128,2048]{1,0:T(8,128)S(1)} custom-call(bf16[128,2048]{1,0:T(8,128)(2,1)S(1)} %copy-done.5, bf16[128,2048]{1,0:T(8,128)(2,1)S(1)} %copy-done.7, f32[16,2048]{1,0:T(8,128)S(1)} %get-tuple-element.22.rate_ref.refs_3_, f32[16,2048]{1,0:T(8,128)S(1)} %get-tuple-element.30.weight_ref), custom_call_target="tpu_custom_call" | custom-call | tf_op jit(solution)/shard_map/scan_back/pallas_call | solution.py:265
  37.3 3.9 %scan_fore.1.fore_ref = f32[128,2048]{1,0:T(8,128)S(1)} custom-call(bf16[128,2048]{1,0:T(8,128)(2,1)S(1)} %copy-done.1, bf16[128,2048]{1,0:T(8,128)(2,1)S(1)} %copy-done.3, f32[16,2048]{1,0:T(8,128)S(1)} %get-tuple-element.22.rate_ref.refs_3_, f32[16,2048]{1,0:T(8,128)S(1)} %get-tuple-element.30.weight_ref), custom_call_target="tpu_custom_call" | custom-call | tf_op jit(solution)/shard_map/scan_fore/pallas_call | solution.py:265
  41.2 0.0 collective-permute-done.5.other_ref
  41.2 4.7 %outputs.1 = (bf16[128,2048]{1,0:T(8,128)(2,1)}, bf16[128,2048]{1,0:T(8,128)(2,1)}, bf16[128,2048]{1,0:T(8,128)(2,1)}, bf16[128,2048]{1,0:T(8,128)(2,1)}, f32[128,16]{1,0:T(8,128)S(1)}) custom-call(f32[40,1024]{1,0:T(8,128)S(1)} %get-tuple-element.28.own_ref, f32[40,1024]{1,0:T(8,128)S(1)} %collective-permute-done.5.other_ref, ...), custom_call_target="tpu_custom_call" | custom-call | tf_op jit(solution)/shard_map/outputs/pallas_call | solution.py:569
  45.9 0.7 %copy.15 = f32[128,16]{0,1:T(8,128)} copy(f32[128,16]{1,0:T(8,128)S(1)} %get-tuple-element.39) | data formatting | bytes 16384 | tf_op jit(solution)/shard_map/outputs/pallas_call | solution.py:569
  (14 shorter events, 0.0 us)
Async XLA Ops:
  1.4 1.0 %copy-start = (bf16[128,2048]{1,0:T(8,128)(2,1)S(1)}, bf16[128,2048]{1,0:T(8,128)(2,1)}, u32[]{:S(2)}) copy-start(bf16[128,2048]{1,0:T(8,128)(2,1)} %k_ref.5) | copy-start | bytes 1572868
  2.5 1.0 %copy-start.2 = (bf16[128,2048]{1,0:T(8,128)(2,1)S(1)}, bf16[128,2048]{1,0:T(8,128)(2,1)}, u32[]{:S(2)}) copy-start(bf16[128,2048]{1,0:T(8,128)(2,1)} %v_ref.5) | copy-start | bytes 1572868
  3.5 1.0 %copy-start.4 = (bf16[128,2048]{1,0:T(8,128)(2,1)S(1)}, bf16[128,2048]{1,0:T(8,128)(2,1)}, u32[]{:S(2)}) copy-start(bf16[128,2048]{1,0:T(8,128)(2,1)} %q_ref.5) | copy-start | bytes 1572868
  4.6 1.0 %copy-start.6 = (bf16[128,2048]{1,0:T(8,128)(2,1)S(1)}, bf16[128,2048]{1,0:T(8,128)(2,1)}, u32[]{:S(2)}) copy-start(bf16[128,2048]{1,0:T(8,128)(2,1)} %c_ref.5) | copy-start | bytes 1572868
  5.6 7.1 %copy-start.1 = (bf16[128,2048]{1,0:T(8,128)(2,1)S(1)}, bf16[128,2048]{1,0:T(8,128)(2,1)}, u32[]{:S(2)}) copy-start(bf16[128,2048]{1,0:T(8,128)(2,1)} %k_ref.5) | copy-start | bytes 1572868
  5.6 7.1 %copy-start.3 = (bf16[128,2048]{1,0:T(8,128)(2,1)S(1)}, bf16[128,2048]{1,0:T(8,128)(2,1)}, u32[]{:S(2)}) copy-start(bf16[128,2048]{1,0:T(8,128)(2,1)} %v_ref.5) | copy-start | bytes 1572868
  8.0 1.5 %collective-permute-start = (f32[32,1024]{1,0:T(8,128)S(1)}, f32[32,1024]{1,0:T(8,128)S(1)}, u32[]{:S(2)}, u32[]{:S(2)}) collective-permute-start(f32[32,1024]{1,0:T(8,128)S(1)} %get-tuple-element.21), channel_id=1, source_target_pairs={{0,1},{1,0},{2,3},{3,2},{4,5},{5,4},{6,7},{7,6},{8,9},{9,8},{10,11... | collective-permute-start | bytes 393224 | tf_op jit(solution)/shard_map/ppermute | solution.py:586
  9.7 6.5 %collective-permute-start.1 = (f32[32,512]{1,0:T(8,128)S(1)}, f32[32,512]{1,0:T(8,128)S(1)}, u32[]{:S(2)}, u32[]{:S(2)}) collective-permute-start(f32[32,512]{1,0:T(8,128)S(1)} %get-tuple-element.24), channel_id=1, source_target_pairs={{0,2},{1,3},{2,0},{3,1},{4,6},{5,7},{6,4},{7,5},{8,10},{9,11},{10,... | collective-permute-start | bytes 196616 | tf_op jit(solution)/shard_map/ppermute | solution.py:586
  16.4 4.5 %collective-permute-start.2 = (f32[40,512]{1,0:T(8,128)S(1)}, f32[40,512]{1,0:T(8,128)S(1)}, u32[]{:S(2)}, u32[]{:S(2)}) collective-permute-start(f32[40,512]{1,0:T(8,128)S(1)} %plane_join.1.own_ref), channel_id=1, source_target_pairs={{0,4},{1,5},{2,6},{3,7},{4,0},{5,1},{6,2},{7,3},{8,12},{9,13},{10,... | collective-permute-start | bytes 245768 | tf_op jit(solution)/shard_map/ppermute | solution.py:586
  20.9 10.1 %copy-start.9 = (f32[128,16]{0,1:T(8,128)S(1)}, f32[128,16]{0,1:T(8,128)}, u32[]{:S(2)}) copy-start(f32[128,16]{0,1:T(8,128)} %param.11) | copy-start | bytes 24580
  21.1 12.3 %copy-start.5 = (bf16[128,2048]{1,0:T(8,128)(2,1)S(1)}, bf16[128,2048]{1,0:T(8,128)(2,1)}, u32[]{:S(2)}) copy-start(bf16[128,2048]{1,0:T(8,128)(2,1)} %q_ref.5) | copy-start | bytes 1572868
  21.1 12.3 %copy-start.7 = (bf16[128,2048]{1,0:T(8,128)(2,1)S(1)}, bf16[128,2048]{1,0:T(8,128)(2,1)}, u32[]{:S(2)}) copy-start(bf16[128,2048]{1,0:T(8,128)(2,1)} %c_ref.5) | copy-start | bytes 1572868
  21.1 5.1 %collective-permute-start.3 = (f32[24,512]{1,0:T(8,128)S(1)}, f32[24,512]{1,0:T(8,128)S(1)}, u32[]{:S(2)}, u32[]{:S(2)}) collective-permute-start(f32[24,512]{1,0:T(8,128)S(1)} %line_join.1.own_ref), channel_id=1, source_target_pairs={{0,8},{1,9},{2,10},{3,11},{4,12},{5,13},{6,14},{7,15},{8,0},{9,1},... | collective-permute-start | bytes 147464 | tf_op jit(solution)/shard_map/ppermute | solution.py:586
  26.3 4.5 %collective-permute-start.4 = (f32[40,512]{1,0:T(8,128)S(1)}, f32[40,512]{1,0:T(8,128)S(1)}, u32[]{:S(2)}, u32[]{:S(2)}) collective-permute-start(f32[40,512]{1,0:T(8,128)S(1)} %get-tuple-element.27), channel_id=1, source_target_pairs={{0,2},{1,3},{2,0},{3,1},{4,6},{5,7},{6,4},{7,5},{8,10},{9,11},{10,... | collective-permute-start | bytes 245768 | tf_op jit(solution)/shard_map/ppermute | solution.py:586
  30.9 10.3 %collective-permute-start.5 = (f32[40,1024]{1,0:T(8,128)S(1)}, f32[40,1024]{1,0:T(8,128)S(1)}, u32[]{:S(2)}, u32[]{:S(2)}) collective-permute-start(f32[40,1024]{1,0:T(8,128)S(1)} %get-tuple-element.29), channel_id=1, source_target_pairs={{0,1},{1,0},{2,3},{3,2},{4,5},{5,4},{6,7},{7,6},{8,9},{9,8},{10,11... | collective-permute-start | bytes 491528 | tf_op jit(solution)/shard_map/ppermute | solution.py:586
  37.3 3.9 %copy-start.8 = (f32[128,2048]{1,0:T(8,128)}, f32[128,2048]{1,0:T(8,128)S(1)}, u32[]{:S(2)}) copy-start(f32[128,2048]{1,0:T(8,128)S(1)} %scan_back.1.back_ref) | copy-start | bytes 3145732

commit v2 on v0

v2 whole, which is shorter than its diff:
```python
import functools
import math

import jax
import jax.numpy as jnp
from jax import lax
from jax.experimental import pallas as pl
from jax.experimental.pallas import tpu as pltpu
from jax.sharding import PartitionSpec as P

PER = 16
MODES = 16
LANES = 128
PACK = LANES // PER
F32 = jnp.float32
BF16 = jnp.bfloat16


def lane_iota(shape):
    return lax.broadcasted_iota(jnp.int32, shape, 1)


def row_iota(shape):
    return lax.broadcasted_iota(jnp.int32, shape, 0)


def split(value):
    high = value.astype(BF16)
    return high, (value - high.astype(F32)).astype(BF16)


def lanes_of(block):
    return slice(block * LANES, (block + 1) * LANES)


def rows_of(block):
    return slice(block * MODES, (block + 1) * MODES)


def dot3(left, right):
    left_high, left_low = split(left)
    right_high, right_low = split(right)
    return jnp.dot(
        jnp.concatenate([left_high, left_high, left_low], axis=1),
        jnp.concatenate([right_high, right_low, right_high], axis=0),
        preferred_element_type=F32,
    )


def own_group(stack):
    group = lane_iota((MODES, LANES)) // PER
    total = stack[rows_of(0)]
    for g in range(1, PACK):
        total = jnp.where(group == g, stack[rows_of(g)], total)
    return total


def columns(by_filter, first):
    return jnp.concatenate(
        [
            jnp.broadcast_to(by_filter[:, g : g + 1], (MODES, LANES))
            for g in range(first, first + PACK)
        ],
        axis=0,
    )


def filter_sums(stack, first):
    high, low = split(stack)
    spot = lane_iota((LANES, LANES)) % PACK == row_iota((LANES, LANES)) // PER
    spot = spot.astype(F32).astype(BF16)
    sums = jnp.dot(
        jnp.concatenate([high, low], axis=1),
        jnp.concatenate([spot, spot], axis=0),
        preferred_element_type=F32,
    )
    block = lane_iota((MODES, LANES)) // PACK - first
    total = jnp.zeros((MODES, LANES), F32)
    for i in range(stack.shape[0] // MODES):
        total = total + jnp.where(block == i, sums[rows_of(i)], 0.0)
    return total


def bit_of(index, mask):
    return (index & mask) != 0


def call(kernel, name, outs, *operands, scratch=(), outs_in=None, ins_in=None):
    ins_in = ins_in or [pltpu.VMEM] * len(operands)
    outs_in = outs_in or [pltpu.VMEM] * len(outs)
    return pl.pallas_call(
        kernel,
        in_specs=[pl.BlockSpec(memory_space=space) for space in ins_in],
        out_specs=[pl.BlockSpec(memory_space=space) for space in outs_in],
        out_shape=[jax.ShapeDtypeStruct(shape, dtype) for shape, dtype in outs],
        scratch_shapes=list(scratch),
        compiler_params=pltpu.CompilerParams(vmem_limit_bytes=16 << 20),
        name=name,
    )(*operands)


CHUNKS = 4


def states_kernel(
    k_hbm,
    v_hbm,
    q_hbm,
    c_hbm,
    decay_hbm,
    send_ref,
    keep_ref,
    rate_ref,
    gated_ref,
    upstream_ref,
    k_ref,
    v_ref,
    q_ref,
    c_ref,
    decay_ref,
    sems,
    decay_sem,
):
    length, total = gated_ref.shape
    width = total // CHUNKS
    core = lax.axis_index("seq") & 1
    copies = [
        [
            pltpu.make_async_copy(
                source.at[:, pl.ds(i * width, width)],
                target.at[:, pl.ds(i * width, width)],
                sems.at[n, i],
            )
            for n, (source, target) in enumerate(
                [(k_hbm, k_ref), (v_hbm, v_ref), (q_hbm, q_ref), (c_hbm, c_ref)]
            )
        ]
        for i in range(CHUNKS)
    ]
    decay_copy = pltpu.make_async_copy(decay_hbm, decay_ref, decay_sem)
    decay_copy.start()
    for chunk in copies:
        for copy in chunk:
            copy.start()
    decay_copy.wait()
    time = lane_iota((LANES, length)).astype(F32)
    decay = decay_ref[...]
    blocks = width // LANES
    for i, chunk in enumerate(copies):
        rates = [columns(decay, (i * blocks + n) * PACK) for n in range(blocks)]
        for copy in chunk:
            copy.wait()
        ends = []
        starts = []
        for n in range(blocks):
            block = i * blocks + n
            lanes = lanes_of(block)
            gated = k_ref[:, lanes].astype(F32) * v_ref[:, lanes].astype(F32)
            upstream = q_ref[:, lanes].astype(F32) * c_ref[:, lanes].astype(F32)
            gated_ref[:, lanes] = gated
            upstream_ref[:, lanes] = upstream
            rate = rates[n]
            rate_ref[rows_of(block)] = own_group(rate)
            ends.append(own_group(dot3(jnp.exp(-rate * (length - 1.0 - time)), gated)))
            starts.append(own_group(dot3(jnp.exp(-rate * time), upstream)))
        half = i // (CHUNKS // 2)
        tall = blocks * MODES
        base = (i % (CHUNKS // 2)) * tall
        offset = total // 2 // LANES * MODES

        def store(ref, ends=ends, starts=starts, base=base, tall=tall, offset=offset):
            ref[base : base + tall] = jnp.concatenate(ends, axis=0)
            ref[offset + base : offset + base + tall] = jnp.concatenate(starts, axis=0)

        pl.when(core == half)(functools.partial(store, keep_ref))
        pl.when(core != half)(functools.partial(store, send_ref))


def states(k, v, q, c, decay):
    length, total = k.shape
    rows = total // LANES * MODES
    stream = ((length, total), k.dtype)
    wide = ((length, total), F32)
    stack = ((rows, LANES), F32)
    arrays = [pltpu.with_memory_space_constraint(x, pltpu.HBM) for x in (k, v, q, c, decay)]
    return call(
        states_kernel,
        "states",
        [stack, stack, stack, wide, wide] + [stream] * 4,
        *arrays,
        scratch=[
            pltpu.VMEM(decay.shape, F32),
            pltpu.SemaphoreType.DMA((4, CHUNKS)),
            pltpu.SemaphoreType.DMA,
        ],
        ins_in=[pltpu.HBM] * 5,
    )


def tables_kernel(decay_ref, residue_ref, rate_ref, weight_ref, fh_ref, fl_ref, bh_ref, bl_ref):
    length, total = fh_ref.shape
    weights = residue_ref[...] * jnp.sqrt(2.0 * decay_ref[...] / MODES)
    pick = lane_iota((MODES, LANES)) % MODES == row_iota((MODES, LANES))
    time = row_iota((MODES, LANES)).astype(F32)

    def across(stack):
        return jnp.sum(jnp.where(pick, stack, 0.0), axis=0, keepdims=True)

    for block in range(total // LANES):
        lanes = lanes_of(block)
        weight = own_group(columns(weights, block * PACK))
        weight_ref[rows_of(block)] = weight
        rate = jnp.broadcast_to(across(rate_ref[rows_of(block)]), (MODES, LANES))
        weight = jnp.broadcast_to(across(weight), (MODES, LANES))
        step = jnp.exp(-rate * MODES)
        fore = weight * jnp.exp(-rate * (time + 1.0))
        back = weight * jnp.exp(-rate * (MODES - time))
        for i in range(length // MODES):
            rows = rows_of(i)
            fh_ref[rows, lanes], fl_ref[rows, lanes] = split(fore)
            rows = rows_of(length // MODES - 1 - i)
            bh_ref[rows, lanes], bl_ref[rows, lanes] = split(back)
            fore = fore * step
            back = back * step


def tables(decay, residue, rate, length):
    total = rate.shape[0] // MODES * LANES
    return call(
        tables_kernel,
        "tables",
        [(rate.shape, F32)] + [((length, total), BF16)] * 4,
        decay,
        residue,
        rate,
    )


GROUP = 4


def lag_kernel(first, count, gated_ref, upstream_ref, rate_ref, out_ref):
    length = gated_ref.shape[0]
    out = jnp.zeros((MODES, LANES), F32)
    for start in range(first, first + count, GROUP):
        blocks = range(start, start + GROUP)
        decays = [jnp.exp(-rate_ref[rows_of(block)]) for block in blocks]

        def eight(i, carry, blocks=blocks, decays=decays):
            states, totals = list(carry[0]), list(carry[1])
            base = pl.multiple_of(i * 8, 8)
            xs = [gated_ref[pl.ds(base, 8), lanes_of(block)] for block in blocks]
            us = [upstream_ref[pl.ds(base, 8), lanes_of(block)] for block in blocks]
            for j in range(8):
                for n in range(GROUP):
                    x = jnp.broadcast_to(xs[n][j : j + 1], (MODES, LANES))
                    u = jnp.broadcast_to(us[n][j : j + 1], (MODES, LANES))
                    states[n] = states[n] * decays[n] + x
                    totals[n] = totals[n] + states[n] * u
            return tuple(states), tuple(totals)

        zeros = (jnp.zeros((MODES, LANES), F32),) * GROUP
        _, totals = lax.fori_loop(0, length // 8, eight, (zeros, zeros))
        out = out + filter_sums(jnp.concatenate(totals, axis=0), start)
    out_ref[...] = out


def lag_part(gated, upstream, rate, first, count):
    return call(
        functools.partial(lag_kernel, first, count),
        "lag_part",
        [((MODES, LANES), F32)],
        gated,
        upstream,
        rate,
    )[0]


def fold(first, second, shift, row):
    low = (row & shift) == 0
    kept = jnp.where(low, first, second)
    moved = jnp.where(low, second, first)
    return kept + pltpu.roll(moved, shift, 0)


def scan_kernel(reverse, first, count, in_ref, rate_ref, weight_ref, out_ref):
    length = in_ref.shape[0]
    row = row_iota((8, LANES))
    for start in range(first, first + count, GROUP):
        blocks = range(start, start + GROUP)
        decays = [jnp.exp(-rate_ref[rows_of(block)]) for block in blocks]
        weights = [weight_ref[rows_of(block)] for block in blocks]

        def eight(i, carry, blocks=blocks, decays=decays, weights=weights):
            states = list(carry)
            at = length // 8 - 1 - i if reverse else i
            base = pl.multiple_of(at * 8, 8)
            rows = [in_ref[pl.ds(base, 8), lanes_of(block)] for block in blocks]
            parts = [[None] * 8 for _ in blocks]
            for j in reversed(range(8)) if reverse else range(8):
                for n in range(GROUP):
                    x = jnp.broadcast_to(rows[n][j : j + 1], (MODES, LANES))
                    states[n] = states[n] * decays[n] + x
                    product = states[n] * weights[n]
                    parts[n][j] = product[:8] + product[8:]
            for n, block in enumerate(blocks):
                part = parts[n]
                four = [fold(part[2 * j], part[2 * j + 1], 1, row) for j in range(4)]
                two = [fold(four[2 * j], four[2 * j + 1], 2, row) for j in range(2)]
                place = lanes_of(block - first)
                out_ref[pl.ds(base, 8), place] = fold(two[0], two[1], 4, row)
            return tuple(states)

        zeros = (jnp.zeros((MODES, LANES), F32),) * GROUP
        lax.fori_loop(0, length // 8, eight, zeros)


def scan_part(values, rate, weight, reverse, first, count):
    return call(
        functools.partial(scan_kernel, reverse, first, count),
        "scan_back" if reverse else "scan_fore",
        [((values.shape[0], count * LANES), F32)],
        values,
        rate,
        weight,
    )[0]


def join(own, other, late, power, step_decay):
    half = power.shape[0]
    own_end, own_start = own[:half], own[half : 2 * half]
    other_end, other_start = other[:half], other[half : 2 * half]
    early_end = jnp.where(late, other_end, own_end)
    late_end = jnp.where(late, own_end, other_end)
    early_start = jnp.where(late, other_start, own_start)
    late_start = jnp.where(late, own_start, other_start)
    end = late_end + power * early_end
    start = early_start + power * late_start
    return end, start, early_end * late_start * step_decay


def pass_down(first, second, before, after, power):
    early = (before, second + power * after)
    late = (first + power * before, after)
    return early, late


def quarter_start(index, rows):
    return pl.multiple_of(((index & 1) * 2 + ((index >> 1) & 1)) * rows, rows)


def core_kernel(length, own_ref, other_ref, rate_ref, send_ref, keep_ref, sums_ref):
    index = lax.axis_index("seq")
    half = own_ref.shape[0] // 2
    quarter = half // 2
    at = pl.multiple_of((index & 1) * half, half)
    rate = rate_ref[pl.ds(at, half)]
    end, start, cross = join(
        own_ref[...],
        other_ref[...],
        bit_of(index, 1),
        jnp.exp(-rate * length),
        jnp.exp(-rate),
    )
    second = bit_of(index, 2)
    keep_ref[:quarter] = jnp.where(second, end[quarter:], end[:quarter])
    keep_ref[quarter:] = jnp.where(second, start[quarter:], start[:quarter])
    send_ref[:quarter] = jnp.where(second, end[:quarter], end[quarter:])
    send_ref[quarter:] = jnp.where(second, start[:quarter], start[quarter:])
    sums_ref[...] = filter_sums(cross, at // MODES)


def core_join(length, own, other, rate):
    half = ((own.shape[0] // 2, LANES), F32)
    return call(
        functools.partial(core_kernel, length),
        "core_join",
        [half, half, ((MODES, LANES), F32)],
        own,
        other,
        rate,
    )


def plane_kernel(length, own_ref, other_ref, *refs):
    *sums_refs, rate_ref, out_ref = refs
    index = lax.axis_index("seq")
    quarter = own_ref.shape[0] // 2
    at = quarter_start(index, quarter)
    rate = rate_ref[pl.ds(at, quarter)]
    end, start, cross = join(
        own_ref[...],
        other_ref[...],
        bit_of(index, 2),
        jnp.exp(-rate * (2 * length)),
        jnp.exp(-rate),
    )
    out_ref[:quarter] = end
    out_ref[quarter : 2 * quarter] = start
    sums = filter_sums(cross, at // MODES)
    for ref in sums_refs:
        sums = sums + ref[...]
    out_ref[2 * quarter :] = sums


def plane_join(length, own, other, sums, rate):
    return call(
        functools.partial(plane_kernel, length),
        "plane_join",
        [((own.shape[0] + MODES, LANES), F32)],
        own,
        other,
        *sums,
        rate,
    )[0]


def line_kernel(length, mask, final, own_ref, other_ref, rate_ref, out_ref):
    index = lax.axis_index("seq")
    quarter = (own_ref.shape[0] - MODES) // 2
    at = quarter_start(index, quarter)
    rate = rate_ref[pl.ds(at, quarter)]
    end, start, cross = join(
        own_ref[...],
        other_ref[...],
        bit_of(index, mask),
        jnp.exp(-rate * (mask * length)),
        jnp.exp(-rate),
    )
    sums = own_ref[2 * quarter :] + other_ref[2 * quarter :] + filter_sums(cross, at // MODES)
    if final:
        out_ref[:quarter] = jnp.where(bit_of(index, 2 * mask), start, end)
        out_ref[quarter:] = sums
    else:
        out_ref[:quarter] = end
        out_ref[quarter : 2 * quarter] = start
        out_ref[2 * quarter :] = sums


def line_join(length, mask, final, own, other, rate):
    quarter = (own.shape[0] - MODES) // 2
    count = (quarter if final else 2 * quarter) + MODES
    return call(
        functools.partial(line_kernel, length, mask, final),
        "line_join",
        [((count, LANES), F32)],
        own,
        other,
        rate,
    )[0]


def turn_kernel(length, masks, own_ref, other_ref, *refs):
    levels = refs[: len(masks) - 1]
    chip_ref, chip_other_ref, rate_ref, keep_ref, send_ref = refs[len(masks) - 1 :]
    index = lax.axis_index("seq")
    quarter = own_ref.shape[0] - MODES
    at = quarter_start(index, quarter)
    rate = rate_ref[pl.ds(at, quarter)]
    own, other = own_ref[:quarter], other_ref[:quarter]
    late = bit_of(index, masks[-1])
    cross = own * other * jnp.exp(-rate)
    sums = own_ref[quarter:] + other_ref[quarter:] + filter_sums(cross, at // MODES)
    before = jnp.where(late, other, 0.0)
    after = jnp.where(late, 0.0, other)
    for mask, level in reversed(list(zip(masks[:-1], levels))):
        late = bit_of(index, mask)
        power = jnp.exp(-rate * (mask * length))
        before, after = (
            jnp.where(late, level[:quarter] + power * before, before),
            jnp.where(late, after, level[quarter : 2 * quarter] + power * after),
        )
    late = bit_of(index, 2)
    power = jnp.exp(-rate * (2 * length))
    early_end = jnp.where(late, chip_other_ref[:quarter], chip_ref[:quarter])
    late_start = jnp.where(late, chip_ref[quarter:], chip_other_ref[quarter:])
    early, later = pass_down(early_end, late_start, before, after, power)
    keep_ref[:quarter] = jnp.where(late, later[0], early[0])
    keep_ref[quarter : 2 * quarter] = jnp.where(late, later[1], early[1])
    keep_ref[2 * quarter :] = sums
    send_ref[:quarter] = jnp.where(late, early[0], later[0])
    send_ref[quarter : 2 * quarter] = jnp.where(late, early[1], later[1])
    send_ref[2 * quarter :] = sums


def turn(length, masks, own, other, levels, chip, chip_other, rate):
    shape = ((chip.shape[0] + MODES, LANES), F32)
    return call(
        functools.partial(turn_kernel, length, masks),
        "turn",
        [shape, shape],
        own,
        other,
        *levels,
        chip,
        chip_other,
        rate,
    )


def chip_kernel(length, own_ref, other_ref, core_ref, core_other_ref, rate_ref, keep_ref, send_ref):
    index = lax.axis_index("seq")
    quarter = (own_ref.shape[0] - MODES) // 2
    half = 2 * quarter
    rate = rate_ref[pl.ds(pl.multiple_of((index & 1) * half, half), half)]
    power = jnp.exp(-rate * length)
    second = bit_of(index, 2)
    own, other = own_ref[:half], other_ref[:half]
    left = jnp.where(second, other, own)
    right = jnp.where(second, own, other)
    before = jnp.concatenate([left[:quarter], right[:quarter]], axis=0)
    after = jnp.concatenate([left[quarter:], right[quarter:]], axis=0)
    late = bit_of(index, 1)
    early_end = jnp.where(late, core_other_ref[:half], core_ref[:half])
    late_start = jnp.where(late, core_ref[half:], core_other_ref[half:])
    early, later = pass_down(early_end, late_start, before, after, power)
    sums = own_ref[half:] + other_ref[half:]
    keep_ref[:half] = jnp.where(late, later[0], early[0])
    keep_ref[half : 2 * half] = jnp.where(late, later[1], early[1])
    keep_ref[2 * half :] = sums
    send_ref[:half] = jnp.where(late, early[0], later[0])
    send_ref[half : 2 * half] = jnp.where(late, early[1], later[1])
    send_ref[2 * half :] = sums


def chip_split(length, own, other, core, core_other, rate):
    shape = ((core.shape[0] + MODES, LANES), F32)
    return call(
        functools.partial(chip_kernel, length),
        "chip_split",
        [shape, shape],
        own,
        other,
        core,
        core_other,
        rate,
    )


def spread(state):
    same = lane_iota((LANES, LANES)) // PER == row_iota((LANES, LANES)) // MODES
    return jnp.where(same, jnp.concatenate([state] * PACK, axis=0), 0.0)


def carried(high_ref, low_ref, lanes, state):
    high, low = split(spread(state))
    table = high_ref[:, lanes]
    return jnp.dot(
        jnp.concatenate([table, table, low_ref[:, lanes]], axis=1),
        jnp.concatenate([high, low, high], axis=0),
        preferred_element_type=F32,
    )


OUT_CHUNKS = 8


def outputs_kernel(scale, fores, backs, *refs):
    own_ref, other_ref, decay_ref, q_ref, k_ref, v_ref, c_ref = refs[:7]
    fore_refs = refs[7 : 7 + fores]
    back_refs = refs[7 + fores : 7 + fores + backs]
    fh_ref, fl_ref, bh_ref, bl_ref = refs[7 + fores + backs : 11 + fores + backs]
    out_hbm, query_hbm, key_hbm, value_hbm, grad_ref = refs[11 + fores + backs : 16 + fores + backs]
    out_ref, query_ref, key_ref, value_ref, sems = refs[16 + fores + backs :]
    core = lax.axis_index("seq") & 1
    length, total = q_ref.shape
    blocks = total // LANES
    half = (own_ref.shape[0] - MODES) // 2

    def local(pieces, block):
        each = pieces[0].shape[1] // LANES
        for piece in pieces:
            each = piece.shape[1] // LANES
            if block < each:
                return piece[:, lanes_of(block)]
            block -= each

    copies = []
    per_chunk = blocks // OUT_CHUNKS
    for chunk in range(OUT_CHUNKS):
        for block in range(chunk * per_chunk, (chunk + 1) * per_chunk):
            lanes = lanes_of(block)
            mine = core == block // (blocks // 2)
            at = (block % (blocks // 2)) * MODES
            ends = slice(at, at + MODES)
            starts = slice(half + at, half + at + MODES)
            before = jnp.where(mine, own_ref[ends], other_ref[ends])
            after = jnp.where(mine, own_ref[starts], other_ref[starts])
            mixed = local(fore_refs, block) + carried(fh_ref, fl_ref, lanes, before)
            out_ref[:, lanes] = (q_ref[:, lanes].astype(F32) * mixed).astype(BF16)
            query_ref[:, lanes] = (c_ref[:, lanes].astype(F32) * mixed).astype(BF16)
            grad = local(back_refs, block) + carried(bh_ref, bl_ref, lanes, after)
            key_ref[:, lanes] = (grad * v_ref[:, lanes].astype(F32)).astype(BF16)
            value_ref[:, lanes] = (grad * k_ref[:, lanes].astype(F32)).astype(BF16)
        place = pl.ds(chunk * per_chunk * LANES, per_chunk * LANES)
        for n, (source, target) in enumerate(
            [(out_ref, out_hbm), (query_ref, query_hbm), (key_ref, key_hbm), (value_ref, value_hbm)]
        ):
            copy = pltpu.make_async_copy(source.at[:, place], target.at[:, place], sems.at[n, chunk])
            copy.start()
            copies.append(copy)
    sums = own_ref[2 * half :] + other_ref[2 * half :]
    grad_ref[...] = sums * jnp.sqrt(2.0 * decay_ref[...] / MODES) * scale
    for copy in copies:
        copy.wait()


def outputs(scale, own, other, decay, q, k, v, c, fore, back, table):
    length, total = q.shape
    wide = ((length, total), BF16)
    return call(
        functools.partial(outputs_kernel, scale, len(fore), len(back)),
        "outputs",
        [wide] * 4 + [(decay.shape, F32)],
        own,
        other,
        decay,
        q,
        k,
        v,
        c,
        *fore,
        *back,
        *table,
        scratch=[pltpu.VMEM((length, total), BF16)] * 4 + [pltpu.SemaphoreType.DMA((4, OUT_CHUNKS))],
        outs_in=[pltpu.HBM] * 4 + [pltpu.VMEM],
    )


def tie(*values):
    return lax.optimization_barrier(values)


def per_device(query, key, value, cotangent, decay, residue):
    length, total = query.shape
    blocks = total // LANES
    count = lax.axis_size("seq")
    masks = [1 << i for i in range(2, count.bit_length() - 1)]
    decay, residue = decay.T, residue.T

    def swap(array, mask):
        return lax.ppermute(array, "seq", [(i, i ^ mask) for i in range(count)])

    core_send, core, rate, gated, upstream, k, v, q, c = states(key, value, query, cotangent, decay)
    core_other = swap(core_send, 1)
    quarter = blocks // 4
    lag_first = lag_part(gated, upstream, rate, 0, quarter)
    core_other, lag_first = tie(core_other, lag_first)
    chip_send, chip, core_sums = core_join(length, core, core_other, rate)
    chip_send, gated, upstream = tie(chip_send, gated, upstream)
    chip_other = swap(chip_send, 2)
    lag_rest = lag_part(gated, upstream, rate, quarter, blocks - quarter)
    message = plane_join(length, chip, chip_other, [core_sums, lag_first, lag_rest], rate)
    message, gated, upstream, rate = tie(message, gated, upstream, rate)
    levels = []
    fore = []
    back = []
    for mask in masks[:-1]:
        levels.append(swap(message, mask))
        if mask == masks[0]:
            weight, *table = tables(decay, residue, rate, length)
            fore.append(scan_part(gated, rate, weight, False, 0, blocks // 2))
            levels[-1], fore[-1] = tie(levels[-1], fore[-1])
        message = line_join(length, mask, mask == masks[-2], message, levels[-1], rate)
    message, gated, upstream, rate = tie(message, gated, upstream, rate)
    top = swap(message, masks[-1])
    fore.append(scan_part(gated, rate, weight, False, blocks // 2, blocks // 2))
    top, fore[-1] = tie(top, fore[-1])
    keep, send = turn(length, masks, message, top, levels, chip, chip_other, rate)
    send, upstream, rate = tie(send, upstream, rate)
    arrived = swap(send, 2)
    back.append(scan_part(upstream, rate, weight, True, 0, blocks // 2))
    arrived, back[-1] = tie(arrived, back[-1])
    own, send = chip_split(length, keep, arrived, core, core_other, rate)
    send, upstream, rate = tie(send, upstream, rate)
    other = swap(send, 1)
    back.append(scan_part(upstream, rate, weight, True, blocks // 2, blocks // 2))
    scale = 1.0 / math.sqrt(length * count)
    *wide, grad = outputs(scale, own, other, decay, q, k, v, c, fore, back, table)
    return (*wide, grad.T)


def solution(mesh):
    rows = P(("grp", "seq"), None)
    return jax.shard_map(
        per_device,
        mesh=mesh,
        in_specs=(rows, rows, rows, rows, P(), P()),
        out_specs=(rows, rows, rows, rows, P("grp", None)),
        check_vma=False,
    )
```

time: 544 us -> 31 us (0.06); the launches traced: 537 us -> 30.8 us
  local copies, waits for them, and re-layouts: 373 us -> 0.01 us
  matrix products: 62.4 us -> 0 us
  other arithmetic: 50.1 us -> 0 us
  blocking collectives: 35.4 us -> 0 us
  Pallas kernels: 0 us -> 18.3 us
  between operations: 14.4 us -> 0.72 us
  starting transfers between devices: 0.59 us -> 10.1 us
    gather x8 -> x0, local copies, waits for them, and re-layouts: 244 us -> none  [per_device(): toeplitz = jnp.where(causal, lag_filter[group_slice][:, clipped], 0.0)]
    dot_general x17 -> x0, matrix products: 62.4 us -> none  [the longest x4 21 us: per_device(): jnp.einsum('gkt,gks->gts', upstream_block, gated_block, precision=PRECISE)]
    rev x4 -> x0, local copies, waits for them, and re-layouts: 60.2 us -> none  [lag_sums(): flipped = correlation[:, :, ::-1]]
    reshape x7 -> x0, local copies, waits for them, and re-layouts: 41.6 us -> none  [the longest x4 38.2 us: lag_sums(): skewed = flattened.reshape(groups_here, length, 2 * length - 1)]
    psum x1 -> x0, blocking collectives: 35.4 us -> none  [per_device(): residue_total = lax.psum(local_residue, 'seq')]
    select_n x32 -> x0, other arithmetic: 34.3 us -> none  [hop(): return jax.tree.map(lambda a, b: jnp.where(reached, a, b), new, before)]
    pallas_call x0 -> x14, Pallas kernels: none -> 18.3 us  [call(): pl.pallas_call(kernel, in_specs=[pl.BlockSpec(memory_space=space) for spa...]
    unnamed x51 -> x4, local copies, waits for them, and re-layouts: 10.3 us -> 0.01 us
  transfers between devices with their start and end apart: 3 -> 6, of which waited for: 0 -> 4; matrix products, arithmetic and copies ran while one was open for 78% -> 0% of each run, Pallas kernels for 0% -> 35%
where the time goes in v2:
time: 31 us; the launch traced here: 30.8 us
  Pallas kernels  18.3 us (59%)
  starting transfers between devices  10.1 us (33%)
  waiting for transfers between devices  1.63 us (5%)
  between operations  0.72 us (2%)
    pallas_call x14, Pallas kernels, call(): pl.pallas_call(kernel, in_specs=[pl.BlockSpec(memory_space=space) for spa...  18.3 us
    ppermute x6, starting transfers between devices, swap(): return lax.ppermute(array, 'seq', [(i, i ^ mask) for i in range(count)])  10.1 us
    ppermute x6, waiting for transfers between devices, swap(): return lax.ppermute(array, 'seq', [(i, i ^ mask) for i in range(count)])  1.63 us
  transfers between devices with their start and end apart: 6, of which 4 were waited for; matrix products, arithmetic and copies ran while one was open for 0% of the time, Pallas kernels for 35%

profile of v2, /device:TPU:0, one launch (start us, length us, event | category | flops | bytes accessed | tf_op | source)
XLA Modules:
  0.0 30.8 jit_solution(12630197627225431523)
XLA Ops:
  0.6 3.9 %states.1 = (f32[256,128]{1,0:T(8,128)S(1)}, f32[256,128]{1,0:T(8,128)S(1)}, f32[256,128]{1,0:T(8,128)S(1)}, f32[128,2048]{1,0:T(8,128)S(1)}, f32[128,2048]{1,0:...) custom-call(bf16[128,2048]{1,0:T(8,128)(2,1)} %k_hbm.1, ...), custom_call_target="tpu_custom_call" | custom-call | tf_op jit(solution)/shard_map/states/pallas_call | solution.py:91
  4.5 0.5 %collective-permute-start = (f32[256,128]{1,0:T(8,128)S(1)}, f32[256,128]{1,0:T(8,128)S(1)}, u32[]{:S(2)}, u32[]{:S(2)}) collective-permute-start(f32[256,128]{1,0:T(8,128)S(1)} %get-tuple-element.57), channel_id=1, source_target_pairs={{0,1},{1,0},{2,3},{3,2},{4,5},{5,4},{6,7},{7,6},{8,9},{9,8},{10,11... | collective-permute-start | bytes 393224 | tf_op jit(solution)/shard_map/ppermute | solution.py:642
  5.1 0.8 %lag_part.2.refs_1_ = f32[16,128]{1,0:T(8,128)S(1)} custom-call(f32[128,2048]{1,0:T(8,128)S(1)} %get-tuple-element.76.gated_ref.in_ref, f32[128,2048]{1,0:T(8,128)S(1)} %get-tuple-element.96.upstream_ref.in_ref, f32[256,128]{1,0:T(8,128)S(1)} %get-tuple-element.97.rate_ref.refs_3_), custom_call_target="tpu_custom_call" | custom-call | tf_op jit(solution)/shard_map/lag_part/pallas_call | solution.py:91
  5.8 0.2 collective-permute-done.other_ref.core_other_ref
  6.0 0.2 core_join.1
  6.2 2.9 %collective-permute-start.1 = (f32[128,128]{1,0:T(8,128)S(1)}, f32[128,128]{1,0:T(8,128)S(1)}, u32[]{:S(2)}, u32[]{:S(2)}) collective-permute-start(f32[128,128]{1,0:T(8,128)S(1)} %get-tuple-element.64), channel_id=1, source_target_pairs={{0,2},{1,3},{2,0},{3,1},{4,6},{5,7},{6,4},{7,5},{8,10},{9,11},{10,... | collective-permute-start | bytes 196616 | tf_op jit(solution)/shard_map/ppermute | solution.py:642
  9.2 2.2 %lag_part.3.refs_2_ = f32[16,128]{1,0:T(8,128)S(1)} custom-call(f32[128,2048]{1,0:T(8,128)S(1)} %get-tuple-element.76.gated_ref.in_ref, f32[128,2048]{1,0:T(8,128)S(1)} %get-tuple-element.96.upstream_ref.in_ref, f32[256,128]{1,0:T(8,128)S(1)} %get-tuple-element.97.rate_ref.refs_3_), custom_call_target="tpu_custom_call" | custom-call | tf_op jit(solution)/shard_map/lag_part/pallas_call | solution.py:91
  11.4 0.2 collective-permute-done.1.other_ref.refs_2_
  11.6 0.0 copy-start
  11.6 0.0 copy-start.1
  11.6 0.2 plane_join.1.own_ref
  11.7 2.0 %collective-permute-start.2 = (f32[144,128]{1,0:T(8,128)S(1)}, f32[144,128]{1,0:T(8,128)S(1)}, u32[]{:S(2)}, u32[]{:S(2)}) collective-permute-start(f32[144,128]{1,0:T(8,128)S(1)} %plane_join.1.own_ref), channel_id=1, source_target_pairs={{0,4},{1,5},{2,6},{3,7},{4,0},{5,1},{6,2},{7,3},{8,12},{9,13},{10,... | collective-permute-start | bytes 221192 | tf_op jit(solution)/shard_map/ppermute | solution.py:642
  13.7 0.0 copy-done
  13.7 0.0 copy-done.1
  13.7 0.8 %tables.1 = (f32[256,128]{1,0:T(8,128)S(1)}, bf16[128,2048]{1,0:T(8,128)(2,1)S(1)}, bf16[128,2048]{1,0:T(8,128)(2,1)S(1)}, bf16[128,2048]{1,0:T(8,128)(2,1)S(1)}, bf16[128,2048]{1,0:T(8,128)(2,1)S(1)}) custom-call(f32[16,128]{1,0:T(8,128)S(1)} %bitcast.4, f32[16,128]{1,0:T(8,128)S(1)} %bitcast.6, f32[256,128]{1,0:T(8,128)S(1)} %get-tuple-element.97.rate_ref.refs_3_), custom_call_target="tpu_custom_call" | custom-call | tf_op jit(solution)/shard_map/tables/pallas_call | solution.py:91
  14.5 1.8 %scan_fore.2.refs_7_ = f32[128,1024]{1,0:T(8,128)S(1)} custom-call(f32[128,2048]{1,0:T(8,128)S(1)} %get-tuple-element.76.gated_ref.in_ref, f32[256,128]{1,0:T(8,128)S(1)} %get-tuple-element.97.rate_ref.refs_3_, f32[256,128]{1,0:T(8,128)S(1)} %get-tuple-element.72.weight_ref), custom_call_target="tpu_custom_call" | custom-call | tf_op jit(solution)/shard_map/scan_fore/pallas_call | solution.py:91
  16.3 0.0 collective-permute-done.2.other_ref.refs_0_
  16.3 0.2 line_join.1.own_ref
  16.5 2.8 %collective-permute-start.3 = (f32[80,128]{1,0:T(8,128)S(1)}, f32[80,128]{1,0:T(8,128)S(1)}, u32[]{:S(2)}, u32[]{:S(2)}) collective-permute-start(f32[80,128]{1,0:T(8,128)S(1)} %line_join.1.own_ref), channel_id=1, source_target_pairs={{0,8},{1,9},{2,10},{3,11},{4,12},{5,13},{6,14},{7,15},{8,0},{9,1},... | collective-permute-start | bytes 122888 | tf_op jit(solution)/shard_map/ppermute | solution.py:642
  19.3 1.8 %scan_fore.3.refs_8_ = f32[128,1024]{1,0:T(8,128)S(1)} custom-call(f32[128,2048]{1,0:T(8,128)S(1)} %get-tuple-element.76.gated_ref.in_ref, f32[256,128]{1,0:T(8,128)S(1)} %get-tuple-element.97.rate_ref.refs_3_, f32[256,128]{1,0:T(8,128)S(1)} %get-tuple-element.72.weight_ref), custom_call_target="tpu_custom_call" | custom-call | tf_op jit(solution)/shard_map/scan_fore/pallas_call | solution.py:91
  21.1 0.4 %collective-permute-done.3.other_ref = f32[80,128]{1,0:T(8,128)S(1)} collective-permute-done((f32[80,128]{1,0:T(8,128)S(1)}, f32[80,128]{1,0:T(8,128)S(1)}, u32[]{:S(2)}, u32[]{:S(2)}) %collective-permute-start.3) | collective-permute-done | bytes 40992 | tf_op jit(solution)/shard_map/ppermute | solution.py:642
  21.4 0.2 turn.1
  21.6 1.8 %collective-permute-start.4 = (f32[144,128]{1,0:T(8,128)S(1)}, f32[144,128]{1,0:T(8,128)S(1)}, u32[]{:S(2)}, u32[]{:S(2)}) collective-permute-start(f32[144,128]{1,0:T(8,128)S(1)} %get-tuple-element.82), channel_id=1, source_target_pairs={{0,2},{1,3},{2,0},{3,1},{4,6},{5,7},{6,4},{7,5},{8,10},{9,11},{10,... | collective-permute-start | bytes 221192 | tf_op jit(solution)/shard_map/ppermute | solution.py:642
  23.4 1.8 %scan_back.2.refs_9_ = f32[128,1024]{1,0:T(8,128)S(1)} custom-call(f32[128,2048]{1,0:T(8,128)S(1)} %get-tuple-element.96.upstream_ref.in_ref, f32[256,128]{1,0:T(8,128)S(1)} %get-tuple-element.97.rate_ref.refs_3_, f32[256,128]{1,0:T(8,128)S(1)} %get-tuple-element.72.weight_ref), custom_call_target="tpu_custom_call" | custom-call | tf_op jit(solution)/shard_map/scan_back/pallas_call | solution.py:91
  25.1 0.9 %collective-permute-done.4.other_ref = f32[144,128]{1,0:T(8,128)S(1)} collective-permute-done((f32[144,128]{1,0:T(8,128)S(1)}, f32[144,128]{1,0:T(8,128)S(1)}, u32[]{:S(2)}, u32[]{:S(2)}) %collective-permute-start.4) | collective-permute-done | bytes 73760 | tf_op jit(solution)/shard_map/ppermute | solution.py:642
  26.0 0.1 chip_split.1
  26.1 0.1 collective-permute-start.5
  26.1 1.8 %scan_back.3.refs_10_ = f32[128,1024]{1,0:T(8,128)S(1)} custom-call(f32[128,2048]{1,0:T(8,128)S(1)} %get-tuple-element.96.upstream_ref.in_ref, f32[256,128]{1,0:T(8,128)S(1)} %get-tuple-element.97.rate_ref.refs_3_, f32[256,128]{1,0:T(8,128)S(1)} %get-tuple-element.72.weight_ref), custom_call_target="tpu_custom_call" | custom-call | tf_op jit(solution)/shard_map/scan_back/pallas_call | solution.py:91
  27.9 0.0 collective-permute-done.5.refs_1_
  27.9 2.9 %outputs.1 = (bf16[128,2048]{1,0:T(8,128)(2,1)}, bf16[128,2048]{1,0:T(8,128)(2,1)}, bf16[128,2048]{1,0:T(8,128)(2,1)}, bf16[128,2048]{1,0:T(8,128)(2,1)}, f32[16,128]{1,0:T(8,128)}) custom-call(f32[272,128]{1,0:T(8,128)S(1)} %get-tuple-element.86.refs_0_, f32[272,128]{1,0:T(8,128)S(1)} %collective-permute-done.5.refs_1_, f32[16,128]{1,0:T(8,128)S(1)} %bitcast.5, ...), custom_call_target="tpu_custom_call" | custom-call | tf_op jit(solution)/shard_map/outputs/pallas_call | solution.py:91
Async XLA Ops:
  4.5 1.5 %collective-permute-start = (f32[256,128]{1,0:T(8,128)S(1)}, f32[256,128]{1,0:T(8,128)S(1)}, u32[]{:S(2)}, u32[]{:S(2)}) collective-permute-start(f32[256,128]{1,0:T(8,128)S(1)} %get-tuple-element.57), channel_id=1, source_target_pairs={{0,1},{1,0},{2,3},{3,2},{4,5},{5,4},{6,7},{7,6},{8,9},{9,8},{10,11... | collective-permute-start | bytes 393224 | tf_op jit(solution)/shard_map/ppermute | solution.py:642
  6.2 5.3 %collective-permute-start.1 = (f32[128,128]{1,0:T(8,128)S(1)}, f32[128,128]{1,0:T(8,128)S(1)}, u32[]{:S(2)}, u32[]{:S(2)}) collective-permute-start(f32[128,128]{1,0:T(8,128)S(1)} %get-tuple-element.64), channel_id=1, source_target_pairs={{0,2},{1,3},{2,0},{3,1},{4,6},{5,7},{6,4},{7,5},{8,10},{9,11},{10,... | collective-permute-start | bytes 196616 | tf_op jit(solution)/shard_map/ppermute | solution.py:642
  11.6 2.1 %copy-start = (f32[128,16]{0,1:T(8,128)S(1)}, f32[128,16]{0,1:T(8,128)}, u32[]{:S(2)}) copy-start(f32[128,16]{0,1:T(8,128)} %param.10) | copy-start | bytes 24580
  11.6 2.1 %copy-start.1 = (f32[128,16]{0,1:T(8,128)S(1)}, f32[128,16]{0,1:T(8,128)}, u32[]{:S(2)}) copy-start(f32[128,16]{0,1:T(8,128)} %param.11) | copy-start | bytes 24580
  11.7 4.6 %collective-permute-start.2 = (f32[144,128]{1,0:T(8,128)S(1)}, f32[144,128]{1,0:T(8,128)S(1)}, u32[]{:S(2)}, u32[]{:S(2)}) collective-permute-start(f32[144,128]{1,0:T(8,128)S(1)} %plane_join.1.own_ref), channel_id=1, source_target_pairs={{0,4},{1,5},{2,6},{3,7},{4,0},{5,1},{6,2},{7,3},{8,12},{9,13},{10,... | collective-permute-start | bytes 221192 | tf_op jit(solution)/shard_map/ppermute | solution.py:642
  16.5 5.0 %collective-permute-start.3 = (f32[80,128]{1,0:T(8,128)S(1)}, f32[80,128]{1,0:T(8,128)S(1)}, u32[]{:S(2)}, u32[]{:S(2)}) collective-permute-start(f32[80,128]{1,0:T(8,128)S(1)} %line_join.1.own_ref), channel_id=1, source_target_pairs={{0,8},{1,9},{2,10},{3,11},{4,12},{5,13},{6,14},{7,15},{8,0},{9,1},... | collective-permute-start | bytes 122888 | tf_op jit(solution)/shard_map/ppermute | solution.py:642
  21.6 4.4 %collective-permute-start.4 = (f32[144,128]{1,0:T(8,128)S(1)}, f32[144,128]{1,0:T(8,128)S(1)}, u32[]{:S(2)}, u32[]{:S(2)}) collective-permute-start(f32[144,128]{1,0:T(8,128)S(1)} %get-tuple-element.82), channel_id=1, source_target_pairs={{0,2},{1,3},{2,0},{3,1},{4,6},{5,7},{6,4},{7,5},{8,10},{9,11},{10,... | collective-permute-start | bytes 221192 | tf_op jit(solution)/shard_map/ppermute | solution.py:642
  26.1 1.9 %collective-permute-start.5 = (f32[272,128]{1,0:T(8,128)S(1)}, f32[272,128]{1,0:T(8,128)S(1)}, u32[]{:S(2)}, u32[]{:S(2)}) collective-permute-start(f32[272,128]{1,0:T(8,128)S(1)} %get-tuple-element.88), channel_id=1, source_target_pairs={{0,1},{1,0},{2,3},{3,2},{4,5},{5,4},{6,7},{7,6},{8,9},{9,8},{10,11... | collective-permute-start | bytes 417800 | tf_op jit(solution)/shard_map/ppermute | solution.py:642

commit v3 on v2

v3 whole, which is shorter than its diff:
```python
import functools
import math

import jax
import jax.numpy as jnp
from jax import lax
from jax.experimental import pallas as pl
from jax.experimental.pallas import tpu as pltpu
from jax.sharding import PartitionSpec as P

PER = 16
MODES = 16
LANES = 128
PACK = LANES // PER
F32 = jnp.float32
BF16 = jnp.bfloat16


def lane_iota(shape):
    return lax.broadcasted_iota(jnp.int32, shape, 1)


def row_iota(shape):
    return lax.broadcasted_iota(jnp.int32, shape, 0)


def split(value):
    high = value.astype(BF16)
    return high, (value - high.astype(F32)).astype(BF16)


def lanes_of(block):
    return slice(block * LANES, (block + 1) * LANES)


def rows_of(block):
    return slice(block * MODES, (block + 1) * MODES)


def dot3(left, right):
    left_high, left_low = split(left)
    right_high, right_low = split(right)
    return jnp.dot(
        jnp.concatenate([left_high, left_high, left_low], axis=1),
        jnp.concatenate([right_high, right_low, right_high], axis=0),
        preferred_element_type=F32,
    )


def own_group(stack):
    group = lane_iota((MODES, LANES)) // PER
    total = stack[rows_of(0)]
    for g in range(1, PACK):
        total = jnp.where(group == g, stack[rows_of(g)], total)
    return total


def columns(by_filter, first):
    return jnp.concatenate(
        [
            jnp.broadcast_to(by_filter[:, g : g + 1], (MODES, LANES))
            for g in range(first, first + PACK)
        ],
        axis=0,
    )


def filter_sums(stack, first):
    high, low = split(stack)
    spot = lane_iota((LANES, LANES)) % PACK == row_iota((LANES, LANES)) // PER
    spot = spot.astype(F32).astype(BF16)
    sums = jnp.dot(
        jnp.concatenate([high, low], axis=1),
        jnp.concatenate([spot, spot], axis=0),
        preferred_element_type=F32,
    )
    block = lane_iota((MODES, LANES)) // PACK - first
    total = jnp.zeros((MODES, LANES), F32)
    for i in range(stack.shape[0] // MODES):
        total = total + jnp.where(block == i, sums[rows_of(i)], 0.0)
    return total


def bit_of(index, mask):
    return (index & mask) != 0


def kept_half(index):
    for shift in (8, 4, 2, 1):
        index = index ^ (index >> shift)
    return index & 1


def call(kernel, name, outs, *operands, scratch=(), outs_in=None, ins_in=None):
    ins_in = ins_in or [pltpu.VMEM] * len(operands)
    outs_in = outs_in or [pltpu.VMEM] * len(outs)
    return pl.pallas_call(
        kernel,
        in_specs=[pl.BlockSpec(memory_space=space) for space in ins_in],
        out_specs=[pl.BlockSpec(memory_space=space) for space in outs_in],
        out_shape=[jax.ShapeDtypeStruct(shape, dtype) for shape, dtype in outs],
        scratch_shapes=list(scratch),
        compiler_params=pltpu.CompilerParams(vmem_limit_bytes=16 << 20),
        name=name,
    )(*operands)


def of_half(by_filter, half):
    return jnp.where(half == 0, by_filter, pltpu.roll(by_filter, LANES // 2, 1))


def half_states(decay, k_ref, v_ref, q_ref, c_ref, state_ref, rate_ref, gated_ref, upstream_ref):
    length, width = gated_ref.shape
    time = lane_iota((LANES, length)).astype(F32)
    blocks = width // LANES
    for block in range(blocks):
        lanes = lanes_of(block)
        gated = k_ref[:, lanes].astype(F32) * v_ref[:, lanes].astype(F32)
        upstream = q_ref[:, lanes].astype(F32) * c_ref[:, lanes].astype(F32)
        gated_ref[:, lanes] = gated
        upstream_ref[:, lanes] = upstream
        rate = columns(decay, block * PACK)
        rate_ref[rows_of(block)] = own_group(rate)
        end = own_group(dot3(jnp.exp(-rate * (length - 1.0 - time)), gated))
        start = own_group(dot3(jnp.exp(-rate * time), upstream))
        state_ref[rows_of(block)] = end
        state_ref[rows_of(blocks + block)] = start


def send_states_kernel(*refs):
    sources, decay_hbm = refs[:4], refs[4]
    state_ref, rate_ref, gated_ref, upstream_ref, decay_ref = refs[5:10]
    sent, kept = refs[10:14], refs[14:18]
    sems, decay_sem = refs[18:]
    half = kept_half(lax.axis_index("seq"))
    width = gated_ref.shape[1]
    decay_copy = pltpu.make_async_copy(decay_hbm, decay_ref, decay_sem)
    decay_copy.start()
    copies = []
    for role, targets in enumerate([sent, kept]):
        at = pl.multiple_of((half if role else 1 - half) * width, width)
        for n in range(4):
            copy = pltpu.make_async_copy(
                sources[n].at[:, pl.ds(at, width)], targets[n], sems.at[role, n]
            )
            copy.start()
            copies.append(copy)
    decay_copy.wait()
    decay = of_half(decay_ref[...], 1 - half)
    for copy in copies[:4]:
        copy.wait()
    half_states(decay, *sent, state_ref, rate_ref, gated_ref, upstream_ref)
    for copy in copies[4:]:
        copy.wait()


def keep_states_kernel(decay_ref, *refs):
    decay = of_half(decay_ref[...], kept_half(lax.axis_index("seq")))
    half_states(decay, *refs)


def state_shapes(length, width):
    blocks = width // LANES
    return [
        ((2 * blocks * MODES, LANES), F32),
        ((blocks * MODES, LANES), F32),
        ((length, width), F32),
        ((length, width), F32),
    ]


def send_states(k, v, q, c, decay):
    length, total = k.shape
    arrays = [pltpu.with_memory_space_constraint(x, pltpu.HBM) for x in (k, v, q, c, decay)]
    outs = call(
        send_states_kernel,
        "send_states",
        state_shapes(length, total // 2)
        + [(decay.shape, F32)]
        + [((length, total // 2), k.dtype)] * 8,
        *arrays,
        scratch=[pltpu.SemaphoreType.DMA((2, 4)), pltpu.SemaphoreType.DMA],
        ins_in=[pltpu.HBM] * 5,
    )
    return outs[:4], outs[4], outs[5:9], outs[9:]


def keep_states(decay, streams):
    return call(
        keep_states_kernel, "keep_states", state_shapes(*streams[0].shape), decay, *streams
    )


def tables_kernel(keep, decay_ref, residue_ref, rate_ref, *refs):
    weight_ref, fh_ref, fl_ref, bh_ref, bl_ref = refs
    length, width = fh_ref.shape
    half = kept_half(lax.axis_index("seq"))
    weights = residue_ref[...] * jnp.sqrt(2.0 * decay_ref[...] / MODES)
    weights = of_half(weights, half if keep else 1 - half)
    pick = lane_iota((MODES, LANES)) % MODES == row_iota((MODES, LANES))
    time = row_iota((MODES, LANES)).astype(F32)

    def across(stack):
        return jnp.sum(jnp.where(pick, stack, 0.0), axis=0, keepdims=True)

    for block in range(width // LANES):
        lanes = lanes_of(block)
        weight = own_group(columns(weights, block * PACK))
        weight_ref[rows_of(block)] = weight
        rate = jnp.broadcast_to(across(rate_ref[rows_of(block)]), (MODES, LANES))
        weight = jnp.broadcast_to(across(weight), (MODES, LANES))
        step = jnp.exp(-rate * MODES)
        fore = weight * jnp.exp(-rate * (time + 1.0))
        back = weight * jnp.exp(-rate * (MODES - time))
        for i in range(length // MODES):
            rows = rows_of(i)
            fh_ref[rows, lanes], fl_ref[rows, lanes] = split(fore)
            rows = rows_of(length // MODES - 1 - i)
            bh_ref[rows, lanes], bl_ref[rows, lanes] = split(back)
            fore = fore * step
            back = back * step


def tables(keep, decay, residue, rate, length):
    width = rate.shape[0] // MODES * LANES
    return call(
        functools.partial(tables_kernel, keep),
        "tables",
        [(rate.shape, F32)] + [((length, width), BF16)] * 4,
        decay,
        residue,
        rate,
    )


GROUP = 4


def lag_kernel(keep, first, count, gated_ref, upstream_ref, rate_ref, out_ref):
    length, width = gated_ref.shape
    half = kept_half(lax.axis_index("seq"))
    offset = (half if keep else 1 - half) * (width // LANES)
    out = jnp.zeros((MODES, LANES), F32)
    for start in range(first, first + count, GROUP):
        blocks = range(start, start + GROUP)
        decays = [jnp.exp(-rate_ref[rows_of(block)]) for block in blocks]

        def eight(i, carry, blocks=blocks, decays=decays):
            states, totals = list(carry[0]), list(carry[1])
            base = pl.multiple_of(i * 8, 8)
            xs = [gated_ref[pl.ds(base, 8), lanes_of(block)] for block in blocks]
            us = [upstream_ref[pl.ds(base, 8), lanes_of(block)] for block in blocks]
            for j in range(8):
                for n in range(GROUP):
                    x = jnp.broadcast_to(xs[n][j : j + 1], (MODES, LANES))
                    u = jnp.broadcast_to(us[n][j : j + 1], (MODES, LANES))
                    states[n] = states[n] * decays[n] + x
                    totals[n] = totals[n] + states[n] * u
            return tuple(states), tuple(totals)

        zeros = (jnp.zeros((MODES, LANES), F32),) * GROUP
        _, totals = lax.fori_loop(0, length // 8, eight, (zeros, zeros))
        out = out + filter_sums(jnp.concatenate(totals, axis=0), offset + start)
    out_ref[...] = out


def lag_part(keep, gated, upstream, rate, first, count):
    return call(
        functools.partial(lag_kernel, keep, first, count),
        "lag_part",
        [((MODES, LANES), F32)],
        gated,
        upstream,
        rate,
    )[0]


def fold(first, second, shift, row):
    low = (row & shift) == 0
    kept = jnp.where(low, first, second)
    moved = jnp.where(low, second, first)
    return kept + pltpu.roll(moved, shift, 0)


def scan_kernel(tasks, *refs):
    row = row_iota((8, LANES))
    for n, (reverse, start) in enumerate(tasks):
        in_ref, rate_ref, weight_ref = refs[3 * n : 3 * n + 3]
        out_ref = refs[3 * len(tasks) + n]
        length = in_ref.shape[0]
        blocks = range(start, start + GROUP)
        decays = [jnp.exp(-rate_ref[rows_of(block)]) for block in blocks]
        weights = [weight_ref[rows_of(block)] for block in blocks]

        def eight(
            i,
            carry,
            reverse=reverse,
            blocks=blocks,
            decays=decays,
            weights=weights,
            in_ref=in_ref,
            out_ref=out_ref,
        ):
            states = list(carry)
            at = length // 8 - 1 - i if reverse else i
            base = pl.multiple_of(at * 8, 8)
            rows = [in_ref[pl.ds(base, 8), lanes_of(block)] for block in blocks]
            parts = [[None] * 8 for _ in blocks]
            for j in reversed(range(8)) if reverse else range(8):
                for n in range(GROUP):
                    x = jnp.broadcast_to(rows[n][j : j + 1], (MODES, LANES))
                    states[n] = states[n] * decays[n] + x
                    product = states[n] * weights[n]
                    parts[n][j] = product[:8] + product[8:]
            for n, block in enumerate(blocks):
                part = parts[n]
                four = [fold(part[2 * j], part[2 * j + 1], 1, row) for j in range(4)]
                two = [fold(four[2 * j], four[2 * j + 1], 2, row) for j in range(2)]
                place = lanes_of(n)
                out_ref[pl.ds(base, 8), place] = fold(two[0], two[1], 4, row)
            return tuple(states)

        zeros = (jnp.zeros((MODES, LANES), F32),) * GROUP
        lax.fori_loop(0, length // 8, eight, zeros)


def scan_part(tasks):
    operands = [x for task in tasks for x in task[:3]]
    return call(
        functools.partial(scan_kernel, [task[3:] for task in tasks]),
        "scan",
        [((tasks[0][0].shape[0], GROUP * LANES), F32)] * len(tasks),
        *operands,
    )


def join(own, other, late, power, step_decay):
    half = power.shape[0]
    own_end, own_start = own[:half], own[half : 2 * half]
    other_end, other_start = other[:half], other[half : 2 * half]
    early_end = jnp.where(late, other_end, own_end)
    late_end = jnp.where(late, own_end, other_end)
    early_start = jnp.where(late, other_start, own_start)
    late_start = jnp.where(late, own_start, other_start)
    end = late_end + power * early_end
    start = early_start + power * late_start
    return end, start, early_end * late_start * step_decay


def pass_down(first, second, before, after, power):
    early = (before, second + power * after)
    late = (first + power * before, after)
    return early, late


def quarter_of(index, ref):
    rows = ref.shape[0] // 2
    return pl.ds(pl.multiple_of(((index >> 1) & 1) * rows, rows), rows)


def first_block(index, rows):
    return (kept_half(index) * 2 + ((index >> 1) & 1)) * (rows // MODES)


def core_kernel(length, own_ref, other_ref, rate_ref, send_ref, keep_ref, sums_ref):
    index = lax.axis_index("seq")
    half = own_ref.shape[0] // 2
    quarter = half // 2
    rate = rate_ref[...]
    end, start, cross = join(
        own_ref[...],
        other_ref[...],
        bit_of(index, 1),
        jnp.exp(-rate * length),
        jnp.exp(-rate),
    )
    second = bit_of(index, 2)
    keep_ref[:quarter] = jnp.where(second, end[quarter:], end[:quarter])
    keep_ref[quarter:] = jnp.where(second, start[quarter:], start[:quarter])
    send_ref[:quarter] = jnp.where(second, end[:quarter], end[quarter:])
    send_ref[quarter:] = jnp.where(second, start[:quarter], start[quarter:])
    sums_ref[...] = filter_sums(cross, kept_half(index) * (half // MODES))


def core_join(length, own, other, rate):
    half = ((own.shape[0] // 2, LANES), F32)
    return call(
        functools.partial(core_kernel, length),
        "core_join",
        [half, half, ((MODES, LANES), F32)],
        own,
        other,
        rate,
    )


def plane_kernel(length, own_ref, other_ref, *refs):
    *sums_refs, rate_ref, out_ref = refs
    index = lax.axis_index("seq")
    quarter = own_ref.shape[0] // 2
    rate = rate_ref[quarter_of(index, rate_ref)]
    end, start, cross = join(
        own_ref[...],
        other_ref[...],
        bit_of(index, 2),
        jnp.exp(-rate * (2 * length)),
        jnp.exp(-rate),
    )
    out_ref[:quarter] = end
    out_ref[quarter : 2 * quarter] = start
    sums = filter_sums(cross, first_block(index, quarter))
    for ref in sums_refs:
        sums = sums + ref[...]
    out_ref[2 * quarter :] = sums


def plane_join(length, own, other, sums, rate):
    return call(
        functools.partial(plane_kernel, length),
        "plane_join",
        [((own.shape[0] + MODES, LANES), F32)],
        own,
        other,
        *sums,
        rate,
    )[0]


def line_kernel(length, mask, final, own_ref, other_ref, rate_ref, out_ref):
    index = lax.axis_index("seq")
    quarter = (own_ref.shape[0] - MODES) // 2
    rate = rate_ref[quarter_of(index, rate_ref)]
    end, start, cross = join(
        own_ref[...],
        other_ref[...],
        bit_of(index, mask),
        jnp.exp(-rate * (mask * length)),
        jnp.exp(-rate),
    )
    sums = own_ref[2 * quarter :] + other_ref[2 * quarter :] + filter_sums(cross, first_block(index, quarter))
    if final:
        out_ref[:quarter] = jnp.where(bit_of(index, 2 * mask), start, end)
        out_ref[quarter:] = sums
    else:
        out_ref[:quarter] = end
        out_ref[quarter : 2 * quarter] = start
        out_ref[2 * quarter :] = sums


def line_join(length, mask, final, own, other, rate):
    quarter = (own.shape[0] - MODES) // 2
    count = (quarter if final else 2 * quarter) + MODES
    return call(
        functools.partial(line_kernel, length, mask, final),
        "line_join",
        [((count, LANES), F32)],
        own,
        other,
        rate,
    )[0]


def turn_kernel(length, masks, own_ref, other_ref, *refs):
    levels = refs[: len(masks) - 1]
    chip_ref, chip_other_ref, rate_ref, keep_ref, send_ref = refs[len(masks) - 1 :]
    index = lax.axis_index("seq")
    quarter = own_ref.shape[0] - MODES
    rate = rate_ref[quarter_of(index, rate_ref)]
    own, other = own_ref[:quarter], other_ref[:quarter]
    late = bit_of(index, masks[-1])
    cross = own * other * jnp.exp(-rate)
    sums = own_ref[quarter:] + other_ref[quarter:] + filter_sums(cross, first_block(index, quarter))
    before = jnp.where(late, other, 0.0)
    after = jnp.where(late, 0.0, other)
    for mask, level in reversed(list(zip(masks[:-1], levels))):
        late = bit_of(index, mask)
        power = jnp.exp(-rate * (mask * length))
        before, after = (
            jnp.where(late, level[:quarter] + power * before, before),
            jnp.where(late, after, level[quarter : 2 * quarter] + power * after),
        )
    late = bit_of(index, 2)
    power = jnp.exp(-rate * (2 * length))
    early_end = jnp.where(late, chip_other_ref[:quarter], chip_ref[:quarter])
    late_start = jnp.where(late, chip_ref[quarter:], chip_other_ref[quarter:])
    early, later = pass_down(early_end, late_start, before, after, power)
    keep_ref[:quarter] = jnp.where(late, later[0], early[0])
    keep_ref[quarter : 2 * quarter] = jnp.where(late, later[1], early[1])
    keep_ref[2 * quarter :] = sums
    send_ref[:quarter] = jnp.where(late, early[0], later[0])
    send_ref[quarter : 2 * quarter] = jnp.where(late, early[1], later[1])
    send_ref[2 * quarter :] = sums


def turn(length, masks, own, other, levels, chip, chip_other, rate):
    shape = ((chip.shape[0] + MODES, LANES), F32)
    return call(
        functools.partial(turn_kernel, length, masks),
        "turn",
        [shape, shape],
        own,
        other,
        *levels,
        chip,
        chip_other,
        rate,
    )


def chip_kernel(length, own_ref, other_ref, core_ref, core_other_ref, rate_ref, keep_ref, send_ref):
    index = lax.axis_index("seq")
    quarter = (own_ref.shape[0] - MODES) // 2
    half = 2 * quarter
    rate = rate_ref[...]
    power = jnp.exp(-rate * length)
    second = bit_of(index, 2)
    own, other = own_ref[:half], other_ref[:half]
    left = jnp.where(second, other, own)
    right = jnp.where(second, own, other)
    before = jnp.concatenate([left[:quarter], right[:quarter]], axis=0)
    after = jnp.concatenate([left[quarter:], right[quarter:]], axis=0)
    late = bit_of(index, 1)
    early_end = jnp.where(late, core_other_ref[:half], core_ref[:half])
    late_start = jnp.where(late, core_ref[half:], core_other_ref[half:])
    early, later = pass_down(early_end, late_start, before, after, power)
    sums = own_ref[half:] + other_ref[half:]
    keep_ref[:half] = jnp.where(late, later[0], early[0])
    keep_ref[half : 2 * half] = jnp.where(late, later[1], early[1])
    keep_ref[2 * half :] = sums
    send_ref[:half] = jnp.where(late, early[0], later[0])
    send_ref[half : 2 * half] = jnp.where(late, early[1], later[1])
    send_ref[2 * half :] = sums


def chip_split(length, own, other, core, core_other, rate):
    shape = ((core.shape[0] + MODES, LANES), F32)
    return call(
        functools.partial(chip_kernel, length),
        "chip_split",
        [shape, shape],
        own,
        other,
        core,
        core_other,
        rate,
    )


def spread(state):
    same = lane_iota((LANES, LANES)) // PER == row_iota((LANES, LANES)) // MODES
    return jnp.where(same, jnp.concatenate([state] * PACK, axis=0), jnp.zeros((), state.dtype))


def carried(high_ref, low_ref, lanes, state):
    high, low = split(state)
    high, low = spread(high), spread(low)
    table = high_ref[:, lanes]
    return jnp.dot(
        jnp.concatenate([table, table, low_ref[:, lanes]], axis=1),
        jnp.concatenate([high, low, high], axis=0),
        preferred_element_type=F32,
    )


CHUNKS = 2


def outputs_kernel(keep, scale, *refs):
    around_ref, sums_refs, decay_ref = refs[0], refs[0:2], refs[2]
    k_ref, v_ref, q_ref, c_ref = refs[3:7]
    fh_ref, fl_ref, bh_ref, bl_ref = refs[7:11]
    length, width = k_ref.shape
    blocks = width // LANES
    pieces = blocks // GROUP
    fore_refs, back_refs = refs[11 : 11 + pieces], refs[11 + pieces : 11 + 2 * pieces]
    rest = refs[11 + 2 * pieces :]
    if not keep:
        rest = rest[4:]
    targets = rest[:4]
    if not keep:
        grad_ref, rest = rest[4], rest[1:]
    scratch, sems = rest[4:8], rest[8]
    out_ref, query_ref, key_ref, value_ref = scratch
    half = kept_half(lax.axis_index("seq"))
    half = half if keep else 1 - half
    copies = []
    each = blocks // CHUNKS
    for chunk in range(CHUNKS):
        for block in range(chunk * each, (chunk + 1) * each):
            lanes = lanes_of(block)
            local = lanes_of(block % GROUP)
            before = around_ref[rows_of(block)]
            after = around_ref[rows_of(blocks + block)]
            mixed = fore_refs[block // GROUP][:, local] + carried(fh_ref, fl_ref, lanes, before)
            out_ref[:, lanes] = (q_ref[:, lanes].astype(F32) * mixed).astype(BF16)
            query_ref[:, lanes] = (c_ref[:, lanes].astype(F32) * mixed).astype(BF16)
            grad = back_refs[block // GROUP][:, local] + carried(bh_ref, bl_ref, lanes, after)
            key_ref[:, lanes] = (grad * v_ref[:, lanes].astype(F32)).astype(BF16)
            value_ref[:, lanes] = (grad * k_ref[:, lanes].astype(F32)).astype(BF16)
        size = each * LANES
        here = pl.ds(chunk * size, size)
        there = pl.ds(pl.multiple_of(half * width + chunk * size, size), size)
        for n in range(4):
            copy = pltpu.make_async_copy(
                scratch[n].at[:, here], targets[n].at[:, there], sems.at[n, chunk]
            )
            copy.start()
            copies.append(copy)
    if not keep:
        base = 2 * blocks * MODES
        sums = sums_refs[0][base:] + sums_refs[1][base:]
        grad_ref[...] = sums * jnp.sqrt(2.0 * decay_ref[...] / MODES) * scale
    for copy in copies:
        copy.wait()


def outputs(keep, scale, around, other, decay, streams, table, fore, back, targets=()):
    length, width = streams[0].shape
    operands = [around, other, decay, *streams, *table, *fore, *back]
    shapes = [jax.ShapeDtypeStruct((length, 2 * width), BF16)] * 4
    spaces = [pltpu.HBM] * 4
    if not keep:
        shapes.append(jax.ShapeDtypeStruct(decay.shape, F32))
        spaces.append(pltpu.VMEM)
    ins = [pltpu.VMEM] * len(operands) + [pltpu.HBM] * len(targets)
    return pl.pallas_call(
        functools.partial(outputs_kernel, keep, scale),
        in_specs=[pl.BlockSpec(memory_space=space) for space in ins],
        out_specs=[pl.BlockSpec(memory_space=space) for space in spaces],
        out_shape=shapes,
        scratch_shapes=[pltpu.VMEM((length, width), BF16)] * 4
        + [pltpu.SemaphoreType.DMA((4, CHUNKS))],
        input_output_aliases={len(operands) + n: n for n in range(len(targets))},
        compiler_params=pltpu.CompilerParams(vmem_limit_bytes=16 << 20),
        name="outputs_keep" if keep else "outputs_sent",
    )(*operands, *targets)


def tie(*values):
    return lax.optimization_barrier(values)


def per_device(query, key, value, cotangent, decay, residue):
    length, total = query.shape
    blocks = total // LANES // 2
    count = lax.axis_size("seq")
    masks = [1 << i for i in range(2, count.bit_length() - 1)]
    decay, residue = decay.T, residue.T

    def swap(array, mask):
        flip = mask | 1
        return lax.ppermute(array, "seq", [(i, i ^ flip) for i in range(count)])

    first, decay, sent, kept = send_states(key, value, query, cotangent, decay)
    core_send, rate_sent, gated_sent, upstream_sent = first
    core_send, decay, gated_sent, upstream_sent, *kept = tie(
        core_send, decay, gated_sent, upstream_sent, *kept
    )
    core_other = swap(core_send, 1)
    core, rate, gated, upstream = keep_states(decay, kept)
    lags = [lag_part(False, gated_sent, upstream_sent, rate_sent, 0, GROUP)]
    core_other, lags[0] = tie(core_other, lags[0])
    chip_send, chip, core_sums = core_join(length, core, core_other, rate)
    chip_send, gated, upstream, gated_sent = tie(chip_send, gated, upstream, gated_sent)
    chip_other = swap(chip_send, 2)
    lags.append(lag_part(False, gated_sent, upstream_sent, rate_sent, GROUP, blocks - GROUP))
    lags.append(lag_part(True, gated, upstream, rate, 0, blocks))
    message = plane_join(length, chip, chip_other, [core_sums, *lags], rate)

    message, rate, rate_sent = tie(message, rate, rate_sent)
    weight, *table = tables(True, decay, residue, rate, length)
    weight_sent, *table_sent = tables(False, decay, residue, rate_sent, length)
    tasks = [
        (values, rates, weights, reverse, start)
        for rates, weights, pair in [
            (rate, weight, (gated, upstream)),
            (rate_sent, weight_sent, (gated_sent, upstream_sent)),
        ]
        for reverse, values in zip((False, True), pair)
        for start in range(0, blocks, GROUP)
    ]
    scans = []

    def some(number, *held):
        todo = tasks[len(scans) : len(scans) + number]
        values, *held = tie([task[0] for task in todo], *held)
        scans.extend(scan_part([(x, *task[1:]) for x, task in zip(values, todo)]))
        return held

    levels = []
    for mask in masks[:-1]:
        other = swap(message, mask)
        if mask == masks[0]:
            (message,) = some(2, message)
            other, *scans[-2:] = tie(other, *scans[-2:])
        levels.append(other)
        message = line_join(length, mask, mask == masks[-2], message, other, rate)
    top = swap(message, masks[-1])
    (message,) = some(3, message)
    top, *scans[-3:] = tie(top, *scans[-3:])
    keep, send = turn(length, masks, message, top, levels, chip, chip_other, rate)
    arrived = swap(send, 2)
    (send,) = some(3, send)
    arrived, *scans[-3:] = tie(arrived, *scans[-3:])
    own, send = chip_split(length, keep, arrived, core, core_other, rate)
    other = swap(send, 1)
    scale = 1.0 / math.sqrt(length * count)
    pieces = blocks // GROUP
    fore, back, fore_sent, back_sent = (scans[i * pieces : (i + 1) * pieces] for i in range(4))
    wide = outputs(True, scale, own, own, decay, kept, table, fore, back)
    *wide, grad = outputs(
        False, scale, other, own, decay, sent, table_sent, fore_sent, back_sent, wide
    )
    return (*wide, grad.T)


def solution(mesh):
    rows = P(("grp", "seq"), None)
    return jax.shard_map(
        per_device,
        mesh=mesh,
        in_specs=(rows, rows, rows, rows, P(), P()),
        out_specs=(rows, rows, rows, rows, P("grp", None)),
        check_vma=False,
    )
```

time: 31 us -> 29 us (0.935)
  starting transfers between devices: 10.1 us -> 8.3 us
  waiting for transfers between devices: 1.63 us -> 1.24 us
    pallas_call x0 -> x2, Pallas kernels: none -> 3.59 us  [outputs(): pl.pallas_call(functools.partial(outputs_kernel, keep, scale), in_specs=[...]
    pallas_call x14 -> x15, Pallas kernels: 18.3 us -> 14.9 us  [call(): pl.pallas_call(kernel, in_specs=[pl.BlockSpec(memory_space=space) for spa...]
    ppermute x6, starting transfers between devices: 10.1 us -> 8.3 us  [swap(): return lax.ppermute(array, 'seq', [(i, i ^ flip) for i in range(count)])]
    ppermute x6, waiting for transfers between devices: 1.63 us -> 1.24 us  [swap(): return lax.ppermute(array, 'seq', [(i, i ^ flip) for i in range(count)])]
  transfers between devices with their start and end apart: 6 -> 6, of which waited for: 4 -> 3; matrix products, arithmetic and copies ran while one was open for 0% -> 0% of each run, Pallas kernels for 35% -> 47%
where the time goes in v3:
time: 29 us; the launch traced here: 28.8 us
  Pallas kernels  18.5 us (64%)
  starting transfers between devices  8.3 us (29%)
  waiting for transfers between devices  1.24 us (4%)
  between operations  0.73 us (3%)
    pallas_call x15, Pallas kernels, call(): pl.pallas_call(kernel, in_specs=[pl.BlockSpec(memory_space=space) for spa...  14.9 us
    ppermute x6, starting transfers between devices, swap(): return lax.ppermute(array, 'seq', [(i, i ^ flip) for i in range(count)])  8.3 us
    pallas_call x2, Pallas kernels, outputs(): pl.pallas_call(functools.partial(outputs_kernel, keep, scale), in_specs=[...  3.59 us
    ppermute x6, waiting for transfers between devices, swap(): return lax.ppermute(array, 'seq', [(i, i ^ flip) for i in range(count)])  1.24 us
  transfers between devices with their start and end apart: 6, of which 3 were waited for; matrix products, arithmetic and copies ran while one was open for 0% of the time, Pallas kernels for 47%

profile of v3, /device:TPU:0, one launch (start us, length us, event | category | flops | bytes accessed | tf_op | source)
XLA Modules:
  0.0 28.8 jit_solution(790240142356301768)
XLA Ops:
  0.6 2.3 %send_states.1 = (f32[256,128]{1,0:T(8,128)S(1)}, f32[128,128]{1,0:T(8,128)S(1)}, f32[128,1024]{1,0:T(8,128)S(1)}, f32[128,1024]{1,0:T(8,128)S(1)}, f32[16,128]{...) custom-call(bf16[128,2048]{1,0:T(8,128)(2,1)} %refs_0_.1, ...), custom_call_target="tpu_custom_call" | custom-call | tf_op jit(solution)/shard_map/send_states/pallas_call | solution.py:97
  2.9 0.5 %collective-permute-start = (f32[256,128]{1,0:T(8,128)S(1)}, f32[256,128]{1,0:T(8,128)S(1)}, u32[]{:S(2)}, u32[]{:S(2)}) collective-permute-start(f32[256,128]{1,0:T(8,128)S(1)} %get-tuple-element.108), channel_id=1, source_target_pairs={{0,1},{1,0},{2,3},{3,2},{4,5},{5,4},{6,7},{7,6},{8,9},{9,8},{10,11... | collective-permute-start | bytes 393224 | tf_op jit(solution)/shard_map/ppermute | solution.py:653
  3.4 0.8 %lag_part.3.refs_1_ = f32[16,128]{1,0:T(8,128)S(1)} custom-call(f32[128,1024]{1,0:T(8,128)S(1)} %get-tuple-element.145.gated_ref.refs_6_.refs_0_, f32[128,1024]{1,0:T(8,128)S(1)} %get-tuple-element.147.upstream_ref.refs_3_.refs_6_, f32[128,128]{1,0:T(8,128)S(1)} %get-tuple-element.137.rate_ref.refs_7_.refs_1_.refs_4_), custom_call_target="tpu_custom_call" | custom-call | tf_op jit(solution)/shard_map/lag_part/pallas_call | solution.py:97
  4.2 0.8 %keep_states.1 = (f32[256,128]{1,0:T(8,128)S(1)}, f32[128,128]{1,0:T(8,128)S(1)}, f32[128,1024]{1,0:T(8,128)S(1)}, f32[128,1024]{1,0:T(8,128)S(1)}) custom-call(f32[16,128]{1,0:T(8,128)S(1)} %get-tuple-element.102.decay_ref.refs_2_, bf16[128,1024]{1,0:T(8,128)(2,1)S(1)} %get-tuple-element.103.refs_0_.refs_3_, ...), custom_call_target="tpu_custom_call" | custom-call | tf_op jit(solution)/shard_map/keep_states/pallas_call | solution.py:97
  5.0 0.0 collective-permute-done.other_ref.core_other_ref
  5.0 0.2 core_join.1
  5.2 2.7 %collective-permute-start.1 = (f32[128,128]{1,0:T(8,128)S(1)}, f32[128,128]{1,0:T(8,128)S(1)}, u32[]{:S(2)}, u32[]{:S(2)}) collective-permute-start(f32[128,128]{1,0:T(8,128)S(1)} %get-tuple-element.121), channel_id=1, source_target_pairs={{0,3},{1,2},{2,1},{3,0},{4,7},{5,6},{6,5},{7,4},{8,11},{9,10},{10,... | collective-permute-start | bytes 196616 | tf_op jit(solution)/shard_map/ppermute | solution.py:653
  7.9 0.8 %lag_part.4.refs_2_ = f32[16,128]{1,0:T(8,128)S(1)} custom-call(f32[128,1024]{1,0:T(8,128)S(1)} %get-tuple-element.145.gated_ref.refs_6_.refs_0_, f32[128,1024]{1,0:T(8,128)S(1)} %get-tuple-element.147.upstream_ref.refs_3_.refs_6_, f32[128,128]{1,0:T(8,128)S(1)} %get-tuple-element.137.rate_ref.refs_7_.refs_1_.refs_4_), custom_call_target="tpu_custom_call" | custom-call | tf_op jit(solution)/shard_map/lag_part/pallas_call | solution.py:97
  8.7 1.5 %lag_part.5.refs_3_ = f32[16,128]{1,0:T(8,128)S(1)} custom-call(f32[128,1024]{1,0:T(8,128)S(1)} %get-tuple-element.129.gated_ref.refs_0_.refs_3_, f32[128,1024]{1,0:T(8,128)S(1)} %get-tuple-element.135.upstream_ref.refs_0_.refs_3_, f32[128,128]{1,0:T(8,128)S(1)} %get-tuple-element.127.rate_ref.refs_4_.refs_1_.refs_3_), custom_call_target="tpu_custom_call" | custom-call | tf_op jit(solution)/shard_map/lag_part/pallas_call | solution.py:97
  10.2 0.2 collective-permute-done.1.other_ref.refs_2_
  10.4 0.0 copy-start
  10.4 0.2 plane_join.1.own_ref
  10.5 1.4 %collective-permute-start.2 = (f32[144,128]{1,0:T(8,128)S(1)}, f32[144,128]{1,0:T(8,128)S(1)}, u32[]{:S(2)}, u32[]{:S(2)}) collective-permute-start(f32[144,128]{1,0:T(8,128)S(1)} %plane_join.1.own_ref), channel_id=1, source_target_pairs={{0,5},{1,4},{2,7},{3,6},{4,1},{5,0},{6,3},{7,2},{8,13},{9,12},{10,... | collective-permute-start | bytes 221192 | tf_op jit(solution)/shard_map/ppermute | solution.py:653
  11.9 0.0 copy-done
  11.9 0.5 %tables.2 = (f32[128,128]{1,0:T(8,128)S(1)}, bf16[128,1024]{1,0:T(8,128)(2,1)S(1)}, bf16[128,1024]{1,0:T(8,128)(2,1)S(1)}, bf16[128,1024]{1,0:T(8,128)(2,1)S(1)}, bf16[128,1024]{1,0:T(8,128)(2,1)S(1)}) custom-call(f32[16,128]{1,0:T(8,128)S(1)} %get-tuple-element.102.decay_ref.refs_2_, f32[16,128]{1,0:T(8,128)S(1)} %bitcast.3, ...), custom_call_target="tpu_custom_call" | custom-call | tf_op jit(solution)/shard_map/tables/pallas_call | solution.py:97
  12.5 1.8 %scan.3 = (f32[128,512]{1,0:T(8,128)S(1)}, f32[128,512]{1,0:T(8,128)S(1)}) custom-call(f32[128,1024]{1,0:T(8,128)S(1)} %get-tuple-element.129.gated_ref.refs_0_.refs_3_, f32[128,128]{1,0:T(8,128)S(1)} %get-tuple-element.127.rate_ref.refs_4_.refs_1_.refs_3_, f32[128,128]{1,0:T(8,128)S(1)} %get-tuple-element.128.refs_2_.refs_5_, ...), custom_call_target="tpu_custom_call" | custom-call | tf_op jit(solution)/shard_map/scan/pallas_call | solution.py:97
  14.2 0.7 %collective-permute-done.2.other_ref.refs_0_ = f32[144,128]{1,0:T(8,128)S(1)} collective-permute-done((f32[144,128]{1,0:T(8,128)S(1)}, f32[144,128]{1,0:T(8,128)S(1)}, u32[]{:S(2)}, u32[]{:S(2)}) %collective-permute-start.2) | collective-permute-done | bytes 73760 | tf_op jit(solution)/shard_map/ppermute | solution.py:653
  14.9 0.2 line_join.1.own_ref
  15.0 2.2 %collective-permute-start.3 = (f32[80,128]{1,0:T(8,128)S(1)}, f32[80,128]{1,0:T(8,128)S(1)}, u32[]{:S(2)}, u32[]{:S(2)}) collective-permute-start(f32[80,128]{1,0:T(8,128)S(1)} %line_join.1.own_ref), channel_id=1, source_target_pairs={{0,9},{1,8},{2,11},{3,10},{4,13},{5,12},{6,15},{7,14},{8,1},{9,0},... | collective-permute-start | bytes 122888 | tf_op jit(solution)/shard_map/ppermute | solution.py:653
  17.2 0.5 %tables.3 = (f32[128,128]{1,0:T(8,128)S(1)}, bf16[128,1024]{1,0:T(8,128)(2,1)S(1)}, bf16[128,1024]{1,0:T(8,128)(2,1)S(1)}, bf16[128,1024]{1,0:T(8,128)(2,1)S(1)}, bf16[128,1024]{1,0:T(8,128)(2,1)S(1)}) custom-call(f32[16,128]{1,0:T(8,128)S(1)} %get-tuple-element.102.decay_ref.refs_2_, f32[16,128]{1,0:T(8,128)S(1)} %bitcast.4, ...), custom_call_target="tpu_custom_call" | custom-call | tf_op jit(solution)/shard_map/tables/pallas_call | solution.py:97
  17.8 2.7 %scan.4 = (f32[128,512]{1,0:T(8,128)S(1)}, f32[128,512]{1,0:T(8,128)S(1)}, f32[128,512]{1,0:T(8,128)S(1)}) custom-call(f32[128,1024]{1,0:T(8,128)S(1)} %get-tuple-element.135.upstream_ref.refs_0_.refs_3_, f32[128,128]{1,0:T(8,128)S(1)} %get-tuple-element.127.rate_ref.refs_4_.refs_1_.refs_3_, f32[128,128]{1,0:T(8,128)S(1)} %get-tuple-element.128.refs_2_.refs_5_, ...), custom_call_target="tpu_custom_call" | custom-call | tf_op jit(solution)/shard_map/scan/pallas_call | solution.py:97
  20.4 0.0 collective-permute-done.3.other_ref
  20.4 0.2 turn.1
  20.6 1.2 %collective-permute-start.4 = (f32[144,128]{1,0:T(8,128)S(1)}, f32[144,128]{1,0:T(8,128)S(1)}, u32[]{:S(2)}, u32[]{:S(2)}) collective-permute-start(f32[144,128]{1,0:T(8,128)S(1)} %get-tuple-element.144), channel_id=1, source_target_pairs={{0,3},{1,2},{2,1},{3,0},{4,7},{5,6},{6,5},{7,4},{8,11},{9,10},{10,... | collective-permute-start | bytes 221192 | tf_op jit(solution)/shard_map/ppermute | solution.py:653
  21.8 2.6 %scan.5 = (f32[128,512]{1,0:T(8,128)S(1)}, f32[128,512]{1,0:T(8,128)S(1)}, f32[128,512]{1,0:T(8,128)S(1)}) custom-call(f32[128,1024]{1,0:T(8,128)S(1)} %get-tuple-element.145.gated_ref.refs_6_.refs_0_, f32[128,128]{1,0:T(8,128)S(1)} %get-tuple-element.137.rate_ref.refs_7_.refs_1_.refs_4_, f32[128,128]{1,0:T(8,128)S(1)} %get-tuple-element.138.refs_8_.refs_2_.refs_5_, ...), custom_call_target="tpu_custom_call" | custom-call | tf_op jit(solution)/shard_map/scan/pallas_call | solution.py:97
  24.4 0.4 %collective-permute-done.4.other_ref = f32[144,128]{1,0:T(8,128)S(1)} collective-permute-done((f32[144,128]{1,0:T(8,128)S(1)}, f32[144,128]{1,0:T(8,128)S(1)}, u32[]{:S(2)}, u32[]{:S(2)}) %collective-permute-start.4) | collective-permute-done | bytes 73760 | tf_op jit(solution)/shard_map/ppermute | solution.py:653
  24.8 0.1 chip_split.1
  24.9 0.3 collective-permute-start.5
  25.2 1.5 %outputs_keep.1 = (bf16[128,2048]{1,0:T(8,128)(2,1)}, bf16[128,2048]{1,0:T(8,128)(2,1)}, bf16[128,2048]{1,0:T(8,128)(2,1)}, bf16[128,2048]{1,0:T(8,128)(2,1)}) custom-call(f32[272,128]{1,0:T(8,128)S(1)} %get-tuple-element.153.refs_0_.refs_1_, f32[272,128]{1,0:T(8,128)S(1)} %get-tuple-element.153.refs_0_.refs_1_, ...), custom_call_target="tpu_custom_call" | custom-call | tf_op jit(solution)/shard_map/outputs_keep/pallas_call | solution.py:627
  26.7 0.0 collective-permute-done.5.refs_0_
  26.7 2.1 %outputs_sent.1 = (bf16[128,2048]{1,0:T(8,128)(2,1)}, bf16[128,2048]{1,0:T(8,128)(2,1)}, bf16[128,2048]{1,0:T(8,128)(2,1)}, bf16[128,2048]{1,0:T(8,128)(2,1)}, f32[16,128]{1,0:T(8,128)}) custom-call(f32[272,128]{1,0:T(8,128)S(1)} %collective-permute-done.5.refs_0_, ...), custom_call_target="tpu_custom_call", output_to_operand_aliasing={{0}: (15, {}), {1}: (16, {}), {2}: (17, {}), {3}: (18, {})} | custom-call | tf_op jit(solution)/shard_map/outputs_sent/pallas_call | solution.py:627
Async XLA Ops:
  2.9 2.1 %collective-permute-start = (f32[256,128]{1,0:T(8,128)S(1)}, f32[256,128]{1,0:T(8,128)S(1)}, u32[]{:S(2)}, u32[]{:S(2)}) collective-permute-start(f32[256,128]{1,0:T(8,128)S(1)} %get-tuple-element.108), channel_id=1, source_target_pairs={{0,1},{1,0},{2,3},{3,2},{4,5},{5,4},{6,7},{7,6},{8,9},{9,8},{10,11... | collective-permute-start | bytes 393224 | tf_op jit(solution)/shard_map/ppermute | solution.py:653
  5.2 5.1 %collective-permute-start.1 = (f32[128,128]{1,0:T(8,128)S(1)}, f32[128,128]{1,0:T(8,128)S(1)}, u32[]{:S(2)}, u32[]{:S(2)}) collective-permute-start(f32[128,128]{1,0:T(8,128)S(1)} %get-tuple-element.121), channel_id=1, source_target_pairs={{0,3},{1,2},{2,1},{3,0},{4,7},{5,6},{6,5},{7,4},{8,11},{9,10},{10,... | collective-permute-start | bytes 196616 | tf_op jit(solution)/shard_map/ppermute | solution.py:653
  10.4 1.6 %copy-start = (f32[128,16]{0,1:T(8,128)S(1)}, f32[128,16]{0,1:T(8,128)}, u32[]{:S(2)}) copy-start(f32[128,16]{0,1:T(8,128)} %param.11) | copy-start | bytes 24580
  10.5 4.3 %collective-permute-start.2 = (f32[144,128]{1,0:T(8,128)S(1)}, f32[144,128]{1,0:T(8,128)S(1)}, u32[]{:S(2)}, u32[]{:S(2)}) collective-permute-start(f32[144,128]{1,0:T(8,128)S(1)} %plane_join.1.own_ref), channel_id=1, source_target_pairs={{0,5},{1,4},{2,7},{3,6},{4,1},{5,0},{6,3},{7,2},{8,13},{9,12},{10,... | collective-permute-start | bytes 221192 | tf_op jit(solution)/shard_map/ppermute | solution.py:653
  15.0 5.4 %collective-permute-start.3 = (f32[80,128]{1,0:T(8,128)S(1)}, f32[80,128]{1,0:T(8,128)S(1)}, u32[]{:S(2)}, u32[]{:S(2)}) collective-permute-start(f32[80,128]{1,0:T(8,128)S(1)} %line_join.1.own_ref), channel_id=1, source_target_pairs={{0,9},{1,8},{2,11},{3,10},{4,13},{5,12},{6,15},{7,14},{8,1},{9,0},... | collective-permute-start | bytes 122888 | tf_op jit(solution)/shard_map/ppermute | solution.py:653
  20.6 4.2 %collective-permute-start.4 = (f32[144,128]{1,0:T(8,128)S(1)}, f32[144,128]{1,0:T(8,128)S(1)}, u32[]{:S(2)}, u32[]{:S(2)}) collective-permute-start(f32[144,128]{1,0:T(8,128)S(1)} %get-tuple-element.144), channel_id=1, source_target_pairs={{0,3},{1,2},{2,1},{3,0},{4,7},{5,6},{6,5},{7,4},{8,11},{9,10},{10,... | collective-permute-start | bytes 221192 | tf_op jit(solution)/shard_map/ppermute | solution.py:653
  24.9 1.8 %collective-permute-start.5 = (f32[272,128]{1,0:T(8,128)S(1)}, f32[272,128]{1,0:T(8,128)S(1)}, u32[]{:S(2)}, u32[]{:S(2)}) collective-permute-start(f32[272,128]{1,0:T(8,128)S(1)} %get-tuple-element.152), channel_id=1, source_target_pairs={{0,1},{1,0},{2,3},{3,2},{4,5},{5,4},{6,7},{7,6},{8,9},{9,8},{10,11... | collective-permute-start | bytes 417800 | tf_op jit(solution)/shard_map/ppermute | solution.py:653

commit v4 on v3

--- a/solution.py
+++ b/solution.py
@@ -30,19 +30,44 @@
 
 
 def lanes_of(block):
-    return slice(block * LANES, (block + 1) * LANES)
+    if isinstance(block, int):
+        return slice(block * LANES, (block + 1) * LANES)
+    return pl.ds(pl.multiple_of(block * LANES, LANES), LANES)
 
 
 def rows_of(block):
-    return slice(block * MODES, (block + 1) * MODES)
-
-
-def dot3(left, right):
-    left_high, left_low = split(left)
-    right_high, right_low = split(right)
+    if isinstance(block, int):
+        return slice(block * MODES, (block + 1) * MODES)
+    return pl.ds(pl.multiple_of(block * MODES, MODES), MODES)
+
+
+def over_blocks(count, step, body):
+    if step == count:
+        for block in range(count):
+            body(block, block, 0)
+        return
+
+    def some(i, carry):
+        for n in range(step):
+            body(i * step + n, n, i * step)
+        return carry
+
+    lax.fori_loop(0, count // step, some, 0)
+
+
+def turned(by_filter, block):
+    if isinstance(block, int):
+        return by_filter
+    return pltpu.roll(by_filter, (LANES - block * PACK) % LANES, 1)
+
+
+STEP = 8
+
+
+def dot_split(left, right):
     return jnp.dot(
-        jnp.concatenate([left_high, left_high, left_low], axis=1),
-        jnp.concatenate([right_high, right_low, right_high], axis=0),
+        jnp.concatenate([left[0], left[0], left[1]], axis=1),
+        jnp.concatenate([right[0], right[1], right[0]], axis=0),
         preferred_element_type=F32,
     )
 
@@ -109,31 +134,32 @@
     return jnp.where(half == 0, by_filter, pltpu.roll(by_filter, LANES // 2, 1))
 
 
-def half_states(decay, k_ref, v_ref, q_ref, c_ref, state_ref, rate_ref, gated_ref, upstream_ref):
-    length, width = gated_ref.shape
+def power_tables(decay, block, length):
     time = lane_iota((LANES, length)).astype(F32)
-    blocks = width // LANES
-    for block in range(blocks):
-        lanes = lanes_of(block)
-        gated = k_ref[:, lanes].astype(F32) * v_ref[:, lanes].astype(F32)
-        upstream = q_ref[:, lanes].astype(F32) * c_ref[:, lanes].astype(F32)
-        gated_ref[:, lanes] = gated
-        upstream_ref[:, lanes] = upstream
-        rate = columns(decay, block * PACK)
-        rate_ref[rows_of(block)] = own_group(rate)
-        end = own_group(dot3(jnp.exp(-rate * (length - 1.0 - time)), gated))
-        start = own_group(dot3(jnp.exp(-rate * time), upstream))
-        state_ref[rows_of(block)] = end
-        state_ref[rows_of(blocks + block)] = start
+    rate = columns(decay, block * PACK)
+    return rate, jnp.exp(-rate * (length - 1.0 - time)), jnp.exp(-rate * time)
+
+
+def block_states(block, ends, starts, streams, state_ref, gated_ref, upstream_ref):
+    k_ref, v_ref, q_ref, c_ref = streams
+    blocks = gated_ref.shape[1] // LANES
+    lanes = lanes_of(block)
+    gated = k_ref[:, lanes].astype(F32) * v_ref[:, lanes].astype(F32)
+    upstream = q_ref[:, lanes].astype(F32) * c_ref[:, lanes].astype(F32)
+    gated_ref[:, lanes] = gated
+    upstream_ref[:, lanes] = upstream
+    state_ref[rows_of(block)] = own_group(dot_split(ends, split(gated)))
+    state_ref[rows_of(block + blocks)] = own_group(dot_split(starts, split(upstream)))
 
 
 def send_states_kernel(*refs):
     sources, decay_hbm = refs[:4], refs[4]
     state_ref, rate_ref, gated_ref, upstream_ref, decay_ref = refs[5:10]
     sent, kept = refs[10:14], refs[14:18]
-    sems, decay_sem = refs[18:]
+    table_ref, sems, decay_sem = refs[18:]
     half = kept_half(lax.axis_index("seq"))
-    width = gated_ref.shape[1]
+    length, width = gated_ref.shape
+    blocks = width // LANES
     decay_copy = pltpu.make_async_copy(decay_hbm, decay_ref, decay_sem)
     decay_copy.start()
     copies = []
@@ -143,20 +169,56 @@
             copy = pltpu.make_async_copy(
                 sources[n].at[:, pl.ds(at, width)], targets[n], sems.at[role, n]
             )
-            copy.start()
             copies.append(copy)
+    for copy in copies[:4]:
+        copy.start()
     decay_copy.wait()
+    for copy in copies[4:]:
+        copy.start()
     decay = of_half(decay_ref[...], 1 - half)
+    def make(block, place, first):
+        rate, *powers = power_tables(turned(decay, first), place, length)
+        rate_ref[rows_of(block)] = own_group(rate)
+        for n, power in enumerate(powers):
+            table_ref[2 * n, :, lanes_of(block)], table_ref[2 * n + 1, :, lanes_of(block)] = split(
+                power
+            )
+
+    over_blocks(blocks, STEP, make)
     for copy in copies[:4]:
         copy.wait()
-    half_states(decay, *sent, state_ref, rate_ref, gated_ref, upstream_ref)
+
+    def use(block, place, first):
+        high, low, start_high, start_low = (table_ref[n, :, lanes_of(block)] for n in range(4))
+        block_states(
+            block,
+            (high, low),
+            (start_high, start_low),
+            sent,
+            state_ref,
+            gated_ref,
+            upstream_ref,
+        )
+
+    over_blocks(blocks, STEP, use)
     for copy in copies[4:]:
         copy.wait()
 
 
 def keep_states_kernel(decay_ref, *refs):
+    streams = refs[:4]
+    state_ref, rate_ref, gated_ref, upstream_ref = refs[4:]
     decay = of_half(decay_ref[...], kept_half(lax.axis_index("seq")))
-    half_states(decay, *refs)
+    length, width = gated_ref.shape
+
+    def both(block, place, first):
+        rate, ends, starts = power_tables(turned(decay, first), place, length)
+        rate_ref[rows_of(block)] = own_group(rate)
+        block_states(
+            block, split(ends), split(starts), streams, state_ref, gated_ref, upstream_ref
+        )
+
+    over_blocks(width // LANES, STEP, both)
 
 
 def state_shapes(length, width):
@@ -179,7 +241,11 @@
         + [(decay.shape, F32)]
         + [((length, total // 2), k.dtype)] * 8,
         *arrays,
-        scratch=[pltpu.SemaphoreType.DMA((2, 4)), pltpu.SemaphoreType.DMA],
+        scratch=[
+            pltpu.VMEM((4, LANES, length * total // 2 // LANES), BF16),
+            pltpu.SemaphoreType.DMA((2, 4)),
+            pltpu.SemaphoreType.DMA,
+        ],
         ins_in=[pltpu.HBM] * 5,
     )
     return outs[:4], outs[4], outs[5:9], outs[9:]
@@ -233,14 +299,17 @@
     )
 
 
-GROUP = 4
-
-
-def lag_kernel(keep, first, count, gated_ref, upstream_ref, rate_ref, out_ref):
+GROUP = 2
+
+
+def lag_kernel(keep, first, count, gated_ref, upstream_ref, rate_ref, *refs):
+    out_ref = refs[-1]
     length, width = gated_ref.shape
     half = kept_half(lax.axis_index("seq"))
     offset = (half if keep else 1 - half) * (width // LANES)
     out = jnp.zeros((MODES, LANES), F32)
+    for cross_ref in refs[:-1]:
+        out = filter_sums(cross_ref[...], offset)
     for start in range(first, first + count, GROUP):
         blocks = range(start, start + GROUP)
         decays = [jnp.exp(-rate_ref[rows_of(block)]) for block in blocks]
@@ -259,12 +328,12 @@
             return tuple(states), tuple(totals)
 
         zeros = (jnp.zeros((MODES, LANES), F32),) * GROUP
-        _, totals = lax.fori_loop(0, length // 8, eight, (zeros, zeros))
+        _, totals = lax.fori_loop(0, length // 8, eight, (zeros, zeros), unroll=True)
         out = out + filter_sums(jnp.concatenate(totals, axis=0), offset + start)
     out_ref[...] = out
 
 
-def lag_part(keep, gated, upstream, rate, first, count):
+def lag_part(keep, gated, upstream, rate, first, count, *cross):
     return call(
         functools.partial(lag_kernel, keep, first, count),
         "lag_part",
@@ -272,6 +341,7 @@
         gated,
         upstream,
         rate,
+        *cross,
     )[0]
 
 
@@ -322,7 +392,7 @@
             return tuple(states)
 
         zeros = (jnp.zeros((MODES, LANES), F32),) * GROUP
-        lax.fori_loop(0, length // 8, eight, zeros)
+        lax.fori_loop(0, length // 8, eight, zeros, unroll=True)
 
 
 def scan_part(tasks):
@@ -363,7 +433,7 @@
     return (kept_half(index) * 2 + ((index >> 1) & 1)) * (rows // MODES)
 
 
-def core_kernel(length, own_ref, other_ref, rate_ref, send_ref, keep_ref, sums_ref):
+def core_kernel(length, own_ref, other_ref, rate_ref, send_ref, keep_ref, cross_ref):
     index = lax.axis_index("seq")
     half = own_ref.shape[0] // 2
     quarter = half // 2
@@ -380,7 +450,7 @@
     keep_ref[quarter:] = jnp.where(second, start[quarter:], start[:quarter])
     send_ref[:quarter] = jnp.where(second, end[:quarter], end[quarter:])
     send_ref[quarter:] = jnp.where(second, start[:quarter], start[quarter:])
-    sums_ref[...] = filter_sums(cross, kept_half(index) * (half // MODES))
+    cross_ref[...] = cross
 
 
 def core_join(length, own, other, rate):
@@ -388,7 +458,7 @@
     return call(
         functools.partial(core_kernel, length),
         "core_join",
-        [half, half, ((MODES, LANES), F32)],
+        [half, half, half],
         own,
         other,
         rate,
@@ -555,86 +625,90 @@
 def carried(high_ref, low_ref, lanes, state):
     high, low = split(state)
     high, low = spread(high), spread(low)
-    table = high_ref[:, lanes]
-    return jnp.dot(
-        jnp.concatenate([table, table, low_ref[:, lanes]], axis=1),
-        jnp.concatenate([high, low, high], axis=0),
-        preferred_element_type=F32,
-    )
-
-
-CHUNKS = 2
-
-
-def outputs_kernel(keep, scale, *refs):
-    around_ref, sums_refs, decay_ref = refs[0], refs[0:2], refs[2]
-    k_ref, v_ref, q_ref, c_ref = refs[3:7]
-    fh_ref, fl_ref, bh_ref, bl_ref = refs[7:11]
-    length, width = k_ref.shape
+    return dot_split((high_ref[:, lanes], low_ref[:, lanes]), (high, low))
+
+
+CHUNKS = 4
+
+
+def write_block(block, blocks, refs, results):
+    around_ref, k_ref, v_ref, q_ref, c_ref, fh_ref, fl_ref, bh_ref, bl_ref = refs[:9]
+    pieces = blocks // GROUP
+    fore_refs, back_refs = refs[9 : 9 + pieces], refs[9 + pieces : 9 + 2 * pieces]
+    out_ref, query_ref, key_ref, value_ref = results
+    lanes = lanes_of(block)
+    local = lanes_of(block % GROUP)
+    before = around_ref[rows_of(block)]
+    after = around_ref[rows_of(blocks + block)]
+    mixed = fore_refs[block // GROUP][:, local] + carried(fh_ref, fl_ref, lanes, before)
+    out_ref[:, lanes] = (q_ref[:, lanes].astype(F32) * mixed).astype(BF16)
+    query_ref[:, lanes] = (c_ref[:, lanes].astype(F32) * mixed).astype(BF16)
+    grad = back_refs[block // GROUP][:, local] + carried(bh_ref, bl_ref, lanes, after)
+    key_ref[:, lanes] = (grad * v_ref[:, lanes].astype(F32)).astype(BF16)
+    value_ref[:, lanes] = (grad * k_ref[:, lanes].astype(F32)).astype(BF16)
+
+
+def keep_outputs_kernel(*refs):
+    blocks = refs[1].shape[1] // LANES
+    for block in range(blocks):
+        write_block(block, blocks, refs[:-4], refs[-4:])
+
+
+def keep_outputs(operands):
+    shape = (operands[1].shape, BF16)
+    return call(keep_outputs_kernel, "keep_outputs", [shape] * 4, *operands)
+
+
+def sent_outputs_kernel(scale, *refs):
+    kept, own_ref, decay_ref = refs[:4], refs[4], refs[5]
+    targets, grad_ref = refs[-11:-7], refs[-7]
+    scratch, kept_sems, sems = refs[-6:-2], refs[-2], refs[-1]
+    refs = refs[6:-11]
+    around_ref = refs[0]
+    width = refs[1].shape[1]
     blocks = width // LANES
-    pieces = blocks // GROUP
-    fore_refs, back_refs = refs[11 : 11 + pieces], refs[11 + pieces : 11 + 2 * pieces]
-    rest = refs[11 + 2 * pieces :]
-    if not keep:
-        rest = rest[4:]
-    targets = rest[:4]
-    if not keep:
-        grad_ref, rest = rest[4], rest[1:]
-    scratch, sems = rest[4:8], rest[8]
-    out_ref, query_ref, key_ref, value_ref = scratch
     half = kept_half(lax.axis_index("seq"))
-    half = half if keep else 1 - half
     copies = []
+
+    def send(sources, which, start, size, sems):
+        at = pl.multiple_of(which * width + start, size)
+        for n in range(4):
+            copy = pltpu.make_async_copy(
+                sources[n].at[:, pl.ds(start, size)], targets[n].at[:, pl.ds(at, size)], sems.at[n]
+            )
+            copy.start()
+            copies.append(copy)
+
+    send(kept, half, 0, width, kept_sems)
     each = blocks // CHUNKS
     for chunk in range(CHUNKS):
         for block in range(chunk * each, (chunk + 1) * each):
-            lanes = lanes_of(block)
-            local = lanes_of(block % GROUP)
-            before = around_ref[rows_of(block)]
-            after = around_ref[rows_of(blocks + block)]
-            mixed = fore_refs[block // GROUP][:, local] + carried(fh_ref, fl_ref, lanes, before)
-            out_ref[:, lanes] = (q_ref[:, lanes].astype(F32) * mixed).astype(BF16)
-            query_ref[:, lanes] = (c_ref[:, lanes].astype(F32) * mixed).astype(BF16)
-            grad = back_refs[block // GROUP][:, local] + carried(bh_ref, bl_ref, lanes, after)
-            key_ref[:, lanes] = (grad * v_ref[:, lanes].astype(F32)).astype(BF16)
-            value_ref[:, lanes] = (grad * k_ref[:, lanes].astype(F32)).astype(BF16)
-        size = each * LANES
-        here = pl.ds(chunk * size, size)
-        there = pl.ds(pl.multiple_of(half * width + chunk * size, size), size)
-        for n in range(4):
-            copy = pltpu.make_async_copy(
-                scratch[n].at[:, here], targets[n].at[:, there], sems.at[n, chunk]
-            )
-            copy.start()
-            copies.append(copy)
-    if not keep:
-        base = 2 * blocks * MODES
-        sums = sums_refs[0][base:] + sums_refs[1][base:]
-        grad_ref[...] = sums * jnp.sqrt(2.0 * decay_ref[...] / MODES) * scale
+            write_block(block, blocks, refs, scratch)
+        send(scratch, 1 - half, chunk * each * LANES, each * LANES, sems.at[chunk])
+    base = 2 * blocks * MODES
+    sums = own_ref[base:] + around_ref[base:]
+    grad_ref[...] = sums * jnp.sqrt(2.0 * decay_ref[...] / MODES) * scale
     for copy in copies:
         copy.wait()
 
 
-def outputs(keep, scale, around, other, decay, streams, table, fore, back, targets=()):
-    length, width = streams[0].shape
-    operands = [around, other, decay, *streams, *table, *fore, *back]
-    shapes = [jax.ShapeDtypeStruct((length, 2 * width), BF16)] * 4
-    spaces = [pltpu.HBM] * 4
-    if not keep:
-        shapes.append(jax.ShapeDtypeStruct(decay.shape, F32))
-        spaces.append(pltpu.VMEM)
-    ins = [pltpu.VMEM] * len(operands) + [pltpu.HBM] * len(targets)
-    return pl.pallas_call(
-        functools.partial(outputs_kernel, keep, scale),
-        in_specs=[pl.BlockSpec(memory_space=space) for space in ins],
-        out_specs=[pl.BlockSpec(memory_space=space) for space in spaces],
-        out_shape=shapes,
-        scratch_shapes=[pltpu.VMEM((length, width), BF16)] * 4
-        + [pltpu.SemaphoreType.DMA((4, CHUNKS))],
-        input_output_aliases={len(operands) + n: n for n in range(len(targets))},
-        compiler_params=pltpu.CompilerParams(vmem_limit_bytes=16 << 20),
-        name="outputs_keep" if keep else "outputs_sent",
-    )(*operands, *targets)
+def sent_outputs(scale, kept, own, decay, operands):
+    length, width = kept[0].shape
+    return call(
+        functools.partial(sent_outputs_kernel, scale),
+        "sent_outputs",
+        [((length, 2 * width), BF16)] * 4 + [(decay.shape, F32)],
+        *kept,
+        own,
+        decay,
+        *operands,
+        scratch=[pltpu.VMEM((length, width), BF16)] * 4
+        + [pltpu.SemaphoreType.DMA((4,)), pltpu.SemaphoreType.DMA((CHUNKS, 4))],
+        outs_in=[pltpu.HBM] * 4 + [pltpu.VMEM],
+    )
+
+
+FILL = (4, 6, 6)
 
 
 def tie(*values):
@@ -659,14 +733,15 @@
     )
     core_other = swap(core_send, 1)
     core, rate, gated, upstream = keep_states(decay, kept)
-    lags = [lag_part(False, gated_sent, upstream_sent, rate_sent, 0, GROUP)]
-    core_other, lags[0] = tie(core_other, lags[0])
-    chip_send, chip, core_sums = core_join(length, core, core_other, rate)
+    core_other, core = tie(core_other, core)
+    chip_send, chip, core_cross = core_join(length, core, core_other, rate)
     chip_send, gated, upstream, gated_sent = tie(chip_send, gated, upstream, gated_sent)
     chip_other = swap(chip_send, 2)
-    lags.append(lag_part(False, gated_sent, upstream_sent, rate_sent, GROUP, blocks - GROUP))
-    lags.append(lag_part(True, gated, upstream, rate, 0, blocks))
-    message = plane_join(length, chip, chip_other, [core_sums, *lags], rate)
+    lags = [
+        lag_part(False, gated_sent, upstream_sent, rate_sent, 0, blocks),
+        lag_part(True, gated, upstream, rate, 0, blocks, core_cross),
+    ]
+    message = plane_join(length, chip, chip_other, lags, rate)
 
     message, rate, rate_sent = tie(message, rate, rate_sent)
     weight, *table = tables(True, decay, residue, rate, length)
@@ -682,36 +757,43 @@
     ]
     scans = []
 
-    def some(number, *held):
+    def fill(number, held, *more):
         todo = tasks[len(scans) : len(scans) + number]
-        values, *held = tie([task[0] for task in todo], *held)
+        held, *values = tie(held, *[task[0] for task in todo])
         scans.extend(scan_part([(x, *task[1:]) for x, task in zip(values, todo)]))
-        return held
+
+        def after(arrived):
+            arrived, *scans[-number:] = tie(arrived, *scans[-number:])
+            if more:
+                arrived, *_ = tie(arrived, *more)
+            return arrived
+
+        return held, after
 
     levels = []
     for mask in masks[:-1]:
-        other = swap(message, mask)
         if mask == masks[0]:
-            (message,) = some(2, message)
-            other, *scans[-2:] = tie(other, *scans[-2:])
-        levels.append(other)
-        message = line_join(length, mask, mask == masks[-2], message, other, rate)
-    top = swap(message, masks[-1])
-    (message,) = some(3, message)
-    top, *scans[-3:] = tie(top, *scans[-3:])
+            message, after = fill(FILL[0], message, table[0], table_sent[0])
+            levels.append(after(swap(message, mask)))
+        else:
+            levels.append(swap(message, mask))
+        message = line_join(length, mask, mask == masks[-2], message, levels[-1], rate)
+    message, after = fill(FILL[1], message)
+    top = after(swap(message, masks[-1]))
     keep, send = turn(length, masks, message, top, levels, chip, chip_other, rate)
-    arrived = swap(send, 2)
-    (send,) = some(3, send)
-    arrived, *scans[-3:] = tie(arrived, *scans[-3:])
+    send, after = fill(FILL[2], send)
+    arrived = after(swap(send, 2))
     own, send = chip_split(length, keep, arrived, core, core_other, rate)
-    other = swap(send, 1)
+    rest = len(tasks) - len(scans)
+    if rest:
+        send, after = fill(rest, send)
+        other = after(swap(send, 1))
+    else:
+        other = swap(send, 1)
     scale = 1.0 / math.sqrt(length * count)
-    pieces = blocks // GROUP
-    fore, back, fore_sent, back_sent = (scans[i * pieces : (i + 1) * pieces] for i in range(4))
-    wide = outputs(True, scale, own, own, decay, kept, table, fore, back)
-    *wide, grad = outputs(
-        False, scale, other, own, decay, sent, table_sent, fore_sent, back_sent, wide
-    )
+    cut = len(scans) // 2
+    done = keep_outputs([own, *kept, *table, *scans[:cut]])
+    *wide, grad = sent_outputs(scale, done, own, decay, [other, *sent, *table_sent, *scans[cut:]])
     return (*wide, grad.T)
 
 

time: 29 us -> 27.2 us (0.938)
  Pallas kernels: 18.5 us -> 15.6 us
  starting transfers between devices: 8.3 us -> 9.53 us
    pallas_call x2 -> x0, Pallas kernels: 3.59 us -> none  [outputs(): pl.pallas_call(functools.partial(outputs_kernel, keep, scale), in_specs=[...]
    ppermute x6, starting transfers between devices: 8.3 us -> 9.53 us  [swap(): return lax.ppermute(array, 'seq', [(i, i ^ flip) for i in range(count)])]
    pallas_call x15 -> x16, Pallas kernels: 14.9 us -> 15.6 us  [call(): pl.pallas_call(kernel, in_specs=[pl.BlockSpec(memory_space=space) for spa...]
  transfers between devices with their start and end apart: 6 -> 6, of which waited for: 3 -> 4; matrix products, arithmetic and copies ran while one was open for 0% -> 0% of each run, Pallas kernels for 47% -> 41%
where the time goes in v4:
time: 27.2 us; the launch traced here: 26.8 us
  Pallas kernels  15.6 us (57%)
  starting transfers between devices  9.53 us (35%)
  waiting for transfers between devices  0.97 us (4%)
  between operations  0.72 us (3%)
    pallas_call x16, Pallas kernels, call(): pl.pallas_call(kernel, in_specs=[pl.BlockSpec(memory_space=space) for spa...  15.6 us
    ppermute x6, starting transfers between devices, swap(): return lax.ppermute(array, 'seq', [(i, i ^ flip) for i in range(count)])  9.53 us
    ppermute x6, waiting for transfers between devices, swap(): return lax.ppermute(array, 'seq', [(i, i ^ flip) for i in range(count)])  0.97 us
  transfers between devices with their start and end apart: 6, of which 4 were waited for; matrix products, arithmetic and copies ran while one was open for 0% of the time, Pallas kernels for 41%

profile of v4, /device:TPU:0, one launch (start us, length us, event | category | flops | bytes accessed | tf_op | source)
XLA Modules:
  0.0 26.8 jit_solution(11543840602398113444)
XLA Ops:
  0.6 2.1 %send_states.1 = (f32[256,128]{1,0:T(8,128)S(1)}, f32[128,128]{1,0:T(8,128)S(1)}, f32[128,1024]{1,0:T(8,128)S(1)}, f32[128,1024]{1,0:T(8,128)S(1)}, f32[16,128]{...) custom-call(bf16[128,2048]{1,0:T(8,128)(2,1)} %refs_0_.1, ...), custom_call_target="tpu_custom_call" | custom-call | tf_op jit(solution)/shard_map/send_states/pallas_call | solution.py:122
  2.7 0.5 %collective-permute-start = (f32[256,128]{1,0:T(8,128)S(1)}, f32[256,128]{1,0:T(8,128)S(1)}, u32[]{:S(2)}, u32[]{:S(2)}) collective-permute-start(f32[256,128]{1,0:T(8,128)S(1)} %get-tuple-element.128), channel_id=1, source_target_pairs={{0,1},{1,0},{2,3},{3,2},{4,5},{5,4},{6,7},{7,6},{8,9},{9,8},{10,11... | collective-permute-start | bytes 393224 | tf_op jit(solution)/shard_map/ppermute | solution.py:727
  3.2 0.8 %keep_states.1 = (f32[256,128]{1,0:T(8,128)S(1)}, f32[128,128]{1,0:T(8,128)S(1)}, f32[128,1024]{1,0:T(8,128)S(1)}, f32[128,1024]{1,0:T(8,128)S(1)}) custom-call(f32[16,128]{1,0:T(8,128)S(1)} %get-tuple-element.129.decay_ref.refs_5_, bf16[128,1024]{1,0:T(8,128)(2,1)S(1)} %get-tuple-element.130.refs_0_.refs_1_, ...), custom_call_target="tpu_custom_call" | custom-call | tf_op jit(solution)/shard_map/keep_states/pallas_call | solution.py:122
  4.0 0.2 collective-permute-done.other_ref.core_other_ref
  4.2 0.1 core_join.1
  4.3 2.7 %collective-permute-start.1 = (f32[128,128]{1,0:T(8,128)S(1)}, f32[128,128]{1,0:T(8,128)S(1)}, u32[]{:S(2)}, u32[]{:S(2)}) collective-permute-start(f32[128,128]{1,0:T(8,128)S(1)} %get-tuple-element.143), channel_id=1, source_target_pairs={{0,3},{1,2},{2,1},{3,0},{4,7},{5,6},{6,5},{7,4},{8,11},{9,10},{10,... | collective-permute-start | bytes 196616 | tf_op jit(solution)/shard_map/ppermute | solution.py:727
  6.9 1.3 %lag_part.3.refs_1_ = f32[16,128]{1,0:T(8,128)S(1)} custom-call(f32[128,1024]{1,0:T(8,128)S(1)} %get-tuple-element.157.gated_ref.refs_0_.refs_3_.refs_6_.refs_9_, f32[128,1024]{1,0:T(8,128)S(1)} %get-tuple-element.171.upstream_ref.refs_0_.refs_3_.refs_6_.refs_9_, f32[128,128]{1,0:T(8,128)S(1)} %get-tuple-element.153.rate_ref.refs_2_.refs_1_.refs_4_.refs_7_.refs_10_.refs_3_, ...), custom_call_target="tpu_custom_call" | custom-call | tf_op jit(solution)/shard_map/lag_part/pallas_call | solution.py:122
  8.3 1.2 %lag_part.2.refs_0_ = f32[16,128]{1,0:T(8,128)S(1)} custom-call(f32[128,1024]{1,0:T(8,128)S(1)} %get-tuple-element.186.gated_ref.refs_12_.refs_15_.refs_0_.refs_3_, f32[128,1024]{1,0:T(8,128)S(1)} %get-tuple-element.190.upstream_ref.refs_6_.refs_9_.refs_12_.refs_15_, f32[128,128]{1,0:T(8,128)S(1)} %get-tuple-element.164.rate_ref.refs_13_.refs_16_.refs_1_.refs_4_.refs_7_.refs_10_), custom_call_target="tpu_custom_call" | custom-call | tf_op jit(solution)/shard_map/lag_part/pallas_call | solution.py:122
  9.5 0.0 collective-permute-done.1.other_ref.refs_2_
  9.5 0.0 copy-start
  9.6 0.2 plane_join.1.own_ref
  9.7 1.6 %collective-permute-start.2 = (f32[144,128]{1,0:T(8,128)S(1)}, f32[144,128]{1,0:T(8,128)S(1)}, u32[]{:S(2)}, u32[]{:S(2)}) collective-permute-start(f32[144,128]{1,0:T(8,128)S(1)} %plane_join.1.own_ref), channel_id=1, source_target_pairs={{0,5},{1,4},{2,7},{3,6},{4,1},{5,0},{6,3},{7,2},{8,13},{9,12},{10,... | collective-permute-start | bytes 221192 | tf_op jit(solution)/shard_map/ppermute | solution.py:727
  11.3 0.0 copy-done
  11.3 0.5 %tables.3 = (f32[128,128]{1,0:T(8,128)S(1)}, bf16[128,1024]{1,0:T(8,128)(2,1)S(1)}, bf16[128,1024]{1,0:T(8,128)(2,1)S(1)}, bf16[128,1024]{1,0:T(8,128)(2,1)S(1)}, bf16[128,1024]{1,0:T(8,128)(2,1)S(1)}) custom-call(f32[16,128]{1,0:T(8,128)S(1)} %get-tuple-element.129.decay_ref.refs_5_, f32[16,128]{1,0:T(8,128)S(1)} %bitcast.3, ...), custom_call_target="tpu_custom_call" | custom-call | tf_op jit(solution)/shard_map/tables/pallas_call | solution.py:122
  11.8 0.5 %tables.2 = (f32[128,128]{1,0:T(8,128)S(1)}, bf16[128,1024]{1,0:T(8,128)(2,1)S(1)}, bf16[128,1024]{1,0:T(8,128)(2,1)S(1)}, bf16[128,1024]{1,0:T(8,128)(2,1)S(1)}, bf16[128,1024]{1,0:T(8,128)(2,1)S(1)}) custom-call(f32[16,128]{1,0:T(8,128)S(1)} %get-tuple-element.129.decay_ref.refs_5_, f32[16,128]{1,0:T(8,128)S(1)} %bitcast.4, ...), custom_call_target="tpu_custom_call" | custom-call | tf_op jit(solution)/shard_map/tables/pallas_call | solution.py:122
  12.4 1.4 %scan.3 = (f32[128,256]{1,0:T(8,128)S(1)}, f32[128,256]{1,0:T(8,128)S(1)}, f32[128,256]{1,0:T(8,128)S(1)}, f32[128,256]{1,0:T(8,128)S(1)}) custom-call(f32[128,1024]{1,0:T(8,128)S(1)} %get-tuple-element.157.gated_ref.refs_0_.refs_3_.refs_6_.refs_9_, f32[128,128]{1,0:T(8,128)S(1)} %get-tuple-element.153.rate_ref.refs_2_.refs_1_.refs_4_.refs_7_.refs_10_.refs_3_, ...), custom_call_target="tpu_custom_call" | custom-call | tf_op jit(solution)/shard_map/scan/pallas_call | solution.py:122
  13.8 0.1 collective-permute-done.2.other_ref.refs_0_
  13.9 0.2 line_join.1.own_ref
  14.1 2.8 %collective-permute-start.3 = (f32[80,128]{1,0:T(8,128)S(1)}, f32[80,128]{1,0:T(8,128)S(1)}, u32[]{:S(2)}, u32[]{:S(2)}) collective-permute-start(f32[80,128]{1,0:T(8,128)S(1)} %line_join.1.own_ref), channel_id=1, source_target_pairs={{0,9},{1,8},{2,11},{3,10},{4,13},{5,12},{6,15},{7,14},{8,1},{9,0},... | collective-permute-start | bytes 122888 | tf_op jit(solution)/shard_map/ppermute | solution.py:727
  16.8 2.2 %scan.4 = (f32[128,256]{1,0:T(8,128)S(1)}, f32[128,256]{1,0:T(8,128)S(1)}, f32[128,256]{1,0:T(8,128)S(1)}, f32[128,256]{1,0:T(8,128)S(1)}, f32[128,256]{1,0:T(8,128)S(1)}, /*index=5*/f32[128,256]{1,0:T(8,128)S(1)}) custom-call(f32[128,1024]{1,0:T(8,128)S(1)} %get-tuple-element.171.upstream_ref.refs_0_.refs_3_.refs_6_.refs_9_, ...), custom_call_target="tpu_custom_call" | custom-call | tf_op jit(solution)/shard_map/scan/pallas_call | solution.py:122
  19.0 0.0 collective-permute-done.3.other_ref
  19.0 0.2 turn.1
  19.1 1.5 %collective-permute-start.4 = (f32[144,128]{1,0:T(8,128)S(1)}, f32[144,128]{1,0:T(8,128)S(1)}, u32[]{:S(2)}, u32[]{:S(2)}) collective-permute-start(f32[144,128]{1,0:T(8,128)S(1)} %get-tuple-element.184), channel_id=1, source_target_pairs={{0,3},{1,2},{2,1},{3,0},{4,7},{5,6},{6,5},{7,4},{8,11},{9,10},{10,... | collective-permute-start | bytes 221192 | tf_op jit(solution)/shard_map/ppermute | solution.py:727
  20.7 2.2 %scan.5 = (f32[128,256]{1,0:T(8,128)S(1)}, f32[128,256]{1,0:T(8,128)S(1)}, f32[128,256]{1,0:T(8,128)S(1)}, f32[128,256]{1,0:T(8,128)S(1)}, f32[128,256]{1,0:T(8,128)S(1)}, /*index=5*/f32[128,256]{1,0:T(8,128)S(1)}) custom-call(f32[128,1024]{1,0:T(8,128)S(1)} %get-tuple-element.186.gated_ref.refs_12_.refs_15_.refs_0_.refs_3_, ...), custom_call_target="tpu_custom_call" | custom-call | tf_op jit(solution)/shard_map/scan/pallas_call | solution.py:122
  22.8 0.4 %collective-permute-done.4.other_ref = f32[144,128]{1,0:T(8,128)S(1)} collective-permute-done((f32[144,128]{1,0:T(8,128)S(1)}, f32[144,128]{1,0:T(8,128)S(1)}, u32[]{:S(2)}, u32[]{:S(2)}) %collective-permute-start.4) | collective-permute-done | bytes 73760 | tf_op jit(solution)/shard_map/ppermute | solution.py:727
  23.3 0.4 %collective-permute-start.5 = (f32[272,128]{1,0:T(8,128)S(1)}, f32[272,128]{1,0:T(8,128)S(1)}, u32[]{:S(2)}, u32[]{:S(2)}) collective-permute-start(f32[272,128]{1,0:T(8,128)S(1)} %get-tuple-element.214), channel_id=1, source_target_pairs={{0,1},{1,0},{2,3},{3,2},{4,5},{5,4},{6,7},{7,6},{8,9},{9,8},{10,11... | collective-permute-start | bytes 417800 | tf_op jit(solution)/shard_map/ppermute | solution.py:727
  23.7 0.7 %keep_outputs.1 = (bf16[128,1024]{1,0:T(8,128)(2,1)S(1)}, bf16[128,1024]{1,0:T(8,128)(2,1)S(1)}, bf16[128,1024]{1,0:T(8,128)(2,1)S(1)}, bf16[128,1024]{1,0:T(8,128)(2,1)S(1)}) custom-call(f32[272,128]{1,0:T(8,128)S(1)} %get-tuple-element.198.refs_0_.refs_4_, bf16[128,1024]{1,0:T(8,128)(2,1)S(1)} %get-tuple-element.130.refs_0_.refs_1_, ...), custom_call_target="tpu_custom_call" | custom-call | tf_op jit(solution)/shard_map/keep_outputs/pallas_call | solution.py:122
  24.4 0.3 %collective-permute-done.5.refs_6_ = f32[272,128]{1,0:T(8,128)S(1)} collective-permute-done((f32[272,128]{1,0:T(8,128)S(1)}, f32[272,128]{1,0:T(8,128)S(1)}, u32[]{:S(2)}, u32[]{:S(2)}) %collective-permute-start.5) | collective-permute-done | bytes 139296 | tf_op jit(solution)/shard_map/ppermute | solution.py:727
  24.7 2.1 %sent_outputs.1 = (bf16[128,2048]{1,0:T(8,128)(2,1)}, bf16[128,2048]{1,0:T(8,128)(2,1)}, bf16[128,2048]{1,0:T(8,128)(2,1)}, bf16[128,2048]{1,0:T(8,128)(2,1)}, f32[16,128]{1,0:T(8,128)}) custom-call(bf16[128,1024]{1,0:T(8,128)(2,1)S(1)} %get-tuple-element.210.refs_0_, bf16[128,1024]{1,0:T(8,128)(2,1)S(1)} %get-tuple-element.211.refs_1_, ...), custom_call_target="tpu_custom_call" | custom-call | tf_op jit(solution)/shard_map/sent_outputs/pallas_call | solution.py:122
  (1 shorter events, 0.0 us)
Async XLA Ops:
  2.7 1.5 %collective-permute-start = (f32[256,128]{1,0:T(8,128)S(1)}, f32[256,128]{1,0:T(8,128)S(1)}, u32[]{:S(2)}, u32[]{:S(2)}) collective-permute-start(f32[256,128]{1,0:T(8,128)S(1)} %get-tuple-element.128), channel_id=1, source_target_pairs={{0,1},{1,0},{2,3},{3,2},{4,5},{5,4},{6,7},{7,6},{8,9},{9,8},{10,11... | collective-permute-start | bytes 393224 | tf_op jit(solution)/shard_map/ppermute | solution.py:727
  4.3 5.3 %collective-permute-start.1 = (f32[128,128]{1,0:T(8,128)S(1)}, f32[128,128]{1,0:T(8,128)S(1)}, u32[]{:S(2)}, u32[]{:S(2)}) collective-permute-start(f32[128,128]{1,0:T(8,128)S(1)} %get-tuple-element.143), channel_id=1, source_target_pairs={{0,3},{1,2},{2,1},{3,0},{4,7},{5,6},{6,5},{7,4},{8,11},{9,10},{10,... | collective-permute-start | bytes 196616 | tf_op jit(solution)/shard_map/ppermute | solution.py:727
  9.5 1.8 %copy-start = (f32[128,16]{0,1:T(8,128)S(1)}, f32[128,16]{0,1:T(8,128)}, u32[]{:S(2)}) copy-start(f32[128,16]{0,1:T(8,128)} %param.11) | copy-start | bytes 24580
  9.7 4.2 %collective-permute-start.2 = (f32[144,128]{1,0:T(8,128)S(1)}, f32[144,128]{1,0:T(8,128)S(1)}, u32[]{:S(2)}, u32[]{:S(2)}) collective-permute-start(f32[144,128]{1,0:T(8,128)S(1)} %plane_join.1.own_ref), channel_id=1, source_target_pairs={{0,5},{1,4},{2,7},{3,6},{4,1},{5,0},{6,3},{7,2},{8,13},{9,12},{10,... | collective-permute-start | bytes 221192 | tf_op jit(solution)/shard_map/ppermute | solution.py:727
  14.1 4.9 %collective-permute-start.3 = (f32[80,128]{1,0:T(8,128)S(1)}, f32[80,128]{1,0:T(8,128)S(1)}, u32[]{:S(2)}, u32[]{:S(2)}) collective-permute-start(f32[80,128]{1,0:T(8,128)S(1)} %line_join.1.own_ref), channel_id=1, source_target_pairs={{0,9},{1,8},{2,11},{3,10},{4,13},{5,12},{6,15},{7,14},{8,1},{9,0},... | collective-permute-start | bytes 122888 | tf_op jit(solution)/shard_map/ppermute | solution.py:727
  19.1 4.1 %collective-permute-start.4 = (f32[144,128]{1,0:T(8,128)S(1)}, f32[144,128]{1,0:T(8,128)S(1)}, u32[]{:S(2)}, u32[]{:S(2)}) collective-permute-start(f32[144,128]{1,0:T(8,128)S(1)} %get-tuple-element.184), channel_id=1, source_target_pairs={{0,3},{1,2},{2,1},{3,0},{4,7},{5,6},{6,5},{7,4},{8,11},{9,10},{10,... | collective-permute-start | bytes 221192 | tf_op jit(solution)/shard_map/ppermute | solution.py:727
  23.3 1.4 %collective-permute-start.5 = (f32[272,128]{1,0:T(8,128)S(1)}, f32[272,128]{1,0:T(8,128)S(1)}, u32[]{:S(2)}, u32[]{:S(2)}) collective-permute-start(f32[272,128]{1,0:T(8,128)S(1)} %get-tuple-element.214), channel_id=1, source_target_pairs={{0,1},{1,0},{2,3},{3,2},{4,5},{5,4},{6,7},{7,6},{8,9},{9,8},{10,11... | collective-permute-start | bytes 417800 | tf_op jit(solution)/shard_map/ppermute | solution.py:727

commit v5 on v4

--- a/solution.py
+++ b/solution.py
@@ -142,12 +142,13 @@
 
 def block_states(block, ends, starts, streams, state_ref, gated_ref, upstream_ref):
     k_ref, v_ref, q_ref, c_ref = streams
-    blocks = gated_ref.shape[1] // LANES
+    length, width = k_ref.shape
+    blocks = width // LANES
     lanes = lanes_of(block)
     gated = k_ref[:, lanes].astype(F32) * v_ref[:, lanes].astype(F32)
     upstream = q_ref[:, lanes].astype(F32) * c_ref[:, lanes].astype(F32)
-    gated_ref[:, lanes] = gated
-    upstream_ref[:, lanes] = upstream
+    gated_ref[pl.ds(block, length, stride=blocks), :] = gated
+    upstream_ref[pl.ds(block, length, stride=blocks), :] = upstream
     state_ref[rows_of(block)] = own_group(dot_split(ends, split(gated)))
     state_ref[rows_of(block + blocks)] = own_group(dot_split(starts, split(upstream)))
 
@@ -158,7 +159,7 @@
     sent, kept = refs[10:14], refs[14:18]
     table_ref, sems, decay_sem = refs[18:]
     half = kept_half(lax.axis_index("seq"))
-    length, width = gated_ref.shape
+    length, width = sent[0].shape
     blocks = width // LANES
     decay_copy = pltpu.make_async_copy(decay_hbm, decay_ref, decay_sem)
     decay_copy.start()
@@ -209,7 +210,7 @@
     streams = refs[:4]
     state_ref, rate_ref, gated_ref, upstream_ref = refs[4:]
     decay = of_half(decay_ref[...], kept_half(lax.axis_index("seq")))
-    length, width = gated_ref.shape
+    length, width = streams[0].shape
 
     def both(block, place, first):
         rate, ends, starts = power_tables(turned(decay, first), place, length)
@@ -226,8 +227,8 @@
     return [
         ((2 * blocks * MODES, LANES), F32),
         ((blocks * MODES, LANES), F32),
-        ((length, width), F32),
-        ((length, width), F32),
+        ((length * blocks, LANES), F32),
+        ((length * blocks, LANES), F32),
     ]
 
 
@@ -299,110 +300,95 @@
     )
 
 
-GROUP = 2
-
-
-def lag_kernel(keep, first, count, gated_ref, upstream_ref, rate_ref, *refs):
-    out_ref = refs[-1]
-    length, width = gated_ref.shape
+def by_mode(stack_ref, blocks):
+    return [stack_ref[pl.ds(n, blocks, stride=MODES), :] for n in range(MODES)]
+
+
+def lag_kernel(keep, gated_ref, upstream_ref, rate_ref, *refs):
+    *cross_refs, out_ref, stack_ref = refs
+    blocks = rate_ref.shape[0] // MODES
     half = kept_half(lax.axis_index("seq"))
-    offset = (half if keep else 1 - half) * (width // LANES)
+    offset = (half if keep else 1 - half) * blocks
+    decays = [jnp.exp(-rate) for rate in by_mode(rate_ref, blocks)]
     out = jnp.zeros((MODES, LANES), F32)
-    for cross_ref in refs[:-1]:
+    for cross_ref in cross_refs:
         out = filter_sums(cross_ref[...], offset)
-    for start in range(first, first + count, GROUP):
-        blocks = range(start, start + GROUP)
-        decays = [jnp.exp(-rate_ref[rows_of(block)]) for block in blocks]
-
-        def eight(i, carry, blocks=blocks, decays=decays):
-            states, totals = list(carry[0]), list(carry[1])
-            base = pl.multiple_of(i * 8, 8)
-            xs = [gated_ref[pl.ds(base, 8), lanes_of(block)] for block in blocks]
-            us = [upstream_ref[pl.ds(base, 8), lanes_of(block)] for block in blocks]
-            for j in range(8):
-                for n in range(GROUP):
-                    x = jnp.broadcast_to(xs[n][j : j + 1], (MODES, LANES))
-                    u = jnp.broadcast_to(us[n][j : j + 1], (MODES, LANES))
-                    states[n] = states[n] * decays[n] + x
-                    totals[n] = totals[n] + states[n] * u
-            return tuple(states), tuple(totals)
-
-        zeros = (jnp.zeros((MODES, LANES), F32),) * GROUP
-        _, totals = lax.fori_loop(0, length // 8, eight, (zeros, zeros), unroll=True)
-        out = out + filter_sums(jnp.concatenate(totals, axis=0), offset + start)
-    out_ref[...] = out
-
-
-def lag_part(keep, gated, upstream, rate, first, count, *cross):
-    return call(
-        functools.partial(lag_kernel, keep, first, count),
+
+    def step(i, carry):
+        states, totals = list(carry[0]), list(carry[1])
+        place = pl.ds(pl.multiple_of(i * blocks, blocks), blocks)
+        gated, upstream = gated_ref[place], upstream_ref[place]
+        for n in range(MODES):
+            states[n] = states[n] * decays[n] + gated
+            totals[n] = totals[n] + states[n] * upstream
+        return tuple(states), tuple(totals)
+
+    zeros = (jnp.zeros((blocks, LANES), F32),) * MODES
+    steps = gated_ref.shape[0] // blocks
+    _, totals = lax.fori_loop(0, steps, step, (zeros, zeros), unroll=UNROLL)
+    for n in range(MODES):
+        stack_ref[pl.ds(n, blocks, stride=MODES), :] = totals[n]
+    out_ref[...] = out + filter_sums(stack_ref[...], offset)
+
+
+def lag_part(keep, gated, upstream, rate, *cross):
+    return call(
+        functools.partial(lag_kernel, keep),
         "lag_part",
         [((MODES, LANES), F32)],
         gated,
         upstream,
         rate,
         *cross,
+        scratch=[pltpu.VMEM(rate.shape, F32)],
     )[0]
 
 
-def fold(first, second, shift, row):
-    low = (row & shift) == 0
-    kept = jnp.where(low, first, second)
-    moved = jnp.where(low, second, first)
-    return kept + pltpu.roll(moved, shift, 0)
-
-
-def scan_kernel(tasks, *refs):
-    row = row_iota((8, LANES))
-    for n, (reverse, start) in enumerate(tasks):
+def scan_kernel(reverses, *refs):
+    for n, reverse in enumerate(reverses):
         in_ref, rate_ref, weight_ref = refs[3 * n : 3 * n + 3]
-        out_ref = refs[3 * len(tasks) + n]
-        length = in_ref.shape[0]
-        blocks = range(start, start + GROUP)
-        decays = [jnp.exp(-rate_ref[rows_of(block)]) for block in blocks]
-        weights = [weight_ref[rows_of(block)] for block in blocks]
-
-        def eight(
+        out_ref = refs[3 * len(reverses) + n]
+        blocks = rate_ref.shape[0] // MODES
+        steps = in_ref.shape[0] // blocks
+        decays = [jnp.exp(-rate) for rate in by_mode(rate_ref, blocks)]
+        weights = by_mode(weight_ref, blocks)
+
+        def step(
             i,
-            carry,
+            states,
             reverse=reverse,
+            steps=steps,
             blocks=blocks,
             decays=decays,
             weights=weights,
             in_ref=in_ref,
             out_ref=out_ref,
         ):
-            states = list(carry)
-            at = length // 8 - 1 - i if reverse else i
-            base = pl.multiple_of(at * 8, 8)
-            rows = [in_ref[pl.ds(base, 8), lanes_of(block)] for block in blocks]
-            parts = [[None] * 8 for _ in blocks]
-            for j in reversed(range(8)) if reverse else range(8):
-                for n in range(GROUP):
-                    x = jnp.broadcast_to(rows[n][j : j + 1], (MODES, LANES))
-                    states[n] = states[n] * decays[n] + x
-                    product = states[n] * weights[n]
-                    parts[n][j] = product[:8] + product[8:]
-            for n, block in enumerate(blocks):
-                part = parts[n]
-                four = [fold(part[2 * j], part[2 * j + 1], 1, row) for j in range(4)]
-                two = [fold(four[2 * j], four[2 * j + 1], 2, row) for j in range(2)]
-                place = lanes_of(n)
-                out_ref[pl.ds(base, 8), place] = fold(two[0], two[1], 4, row)
+            at = steps - 1 - i if reverse else i
+            place = pl.ds(pl.multiple_of(at * blocks, blocks), blocks)
+            value = in_ref[place]
+            states = [state * decay + value for state, decay in zip(states, decays)]
+            terms = [state * weight for state, weight in zip(states, weights)]
+            while len(terms) > 1:
+                terms = [a + b for a, b in zip(terms[::2], terms[1::2])]
+            first = at // 8 * (8 * blocks) + at % 8
+            out_ref[pl.ds(first, blocks, stride=8), :] = terms[0]
             return tuple(states)
 
-        zeros = (jnp.zeros((MODES, LANES), F32),) * GROUP
-        lax.fori_loop(0, length // 8, eight, zeros, unroll=True)
+        zeros = (jnp.zeros((blocks, LANES), F32),) * MODES
+        lax.fori_loop(0, steps, step, zeros, unroll=UNROLL)
 
 
 def scan_part(tasks):
-    operands = [x for task in tasks for x in task[:3]]
-    return call(
-        functools.partial(scan_kernel, [task[3:] for task in tasks]),
+    return call(
+        functools.partial(scan_kernel, [task[3] for task in tasks]),
         "scan",
-        [((tasks[0][0].shape[0], GROUP * LANES), F32)] * len(tasks),
-        *operands,
-    )
+        [(task[0].shape, F32) for task in tasks],
+        *[x for task in tasks for x in task[:3]],
+    )
+
+
+UNROLL = 128
 
 
 def join(own, other, late, power, step_decay):
@@ -633,17 +619,20 @@
 
 def write_block(block, blocks, refs, results):
     around_ref, k_ref, v_ref, q_ref, c_ref, fh_ref, fl_ref, bh_ref, bl_ref = refs[:9]
-    pieces = blocks // GROUP
-    fore_refs, back_refs = refs[9 : 9 + pieces], refs[9 + pieces : 9 + 2 * pieces]
+    fore_ref, back_ref = refs[9:11]
     out_ref, query_ref, key_ref, value_ref = results
     lanes = lanes_of(block)
-    local = lanes_of(block % GROUP)
+    tiles = range(block * 8, fore_ref.shape[0], 8 * blocks)
+
+    def own(ref):
+        return jnp.concatenate([ref[i : i + 8] for i in tiles], axis=0)
+
     before = around_ref[rows_of(block)]
     after = around_ref[rows_of(blocks + block)]
-    mixed = fore_refs[block // GROUP][:, local] + carried(fh_ref, fl_ref, lanes, before)
+    mixed = own(fore_ref) + carried(fh_ref, fl_ref, lanes, before)
     out_ref[:, lanes] = (q_ref[:, lanes].astype(F32) * mixed).astype(BF16)
     query_ref[:, lanes] = (c_ref[:, lanes].astype(F32) * mixed).astype(BF16)
-    grad = back_refs[block // GROUP][:, local] + carried(bh_ref, bl_ref, lanes, after)
+    grad = own(back_ref) + carried(bh_ref, bl_ref, lanes, after)
     key_ref[:, lanes] = (grad * v_ref[:, lanes].astype(F32)).astype(BF16)
     value_ref[:, lanes] = (grad * k_ref[:, lanes].astype(F32)).astype(BF16)
 
@@ -708,7 +697,7 @@
     )
 
 
-FILL = (4, 6, 6)
+FILL = (1, 1, 2)
 
 
 def tie(*values):
@@ -738,8 +727,8 @@
     chip_send, gated, upstream, gated_sent = tie(chip_send, gated, upstream, gated_sent)
     chip_other = swap(chip_send, 2)
     lags = [
-        lag_part(False, gated_sent, upstream_sent, rate_sent, 0, blocks),
-        lag_part(True, gated, upstream, rate, 0, blocks, core_cross),
+        lag_part(False, gated_sent, upstream_sent, rate_sent),
+        lag_part(True, gated, upstream, rate, core_cross),
     ]
     message = plane_join(length, chip, chip_other, lags, rate)
 
@@ -747,13 +736,12 @@
     weight, *table = tables(True, decay, residue, rate, length)
     weight_sent, *table_sent = tables(False, decay, residue, rate_sent, length)
     tasks = [
-        (values, rates, weights, reverse, start)
+        (values, rates, weights, reverse)
         for rates, weights, pair in [
             (rate, weight, (gated, upstream)),
             (rate_sent, weight_sent, (gated_sent, upstream_sent)),
         ]
         for reverse, values in zip((False, True), pair)
-        for start in range(0, blocks, GROUP)
     ]
     scans = []
 

time: 27.2 us -> 27.1 us (level)
  the two profiles are of different devices: /device:TPU:0 before, /device:TPU:31 now
where the time goes in v5:
time: 27.1 us; the launch traced here: 26.9 us
  Pallas kernels  14.3 us (53%)
  waiting for transfers between devices  8.68 us (32%)
  starting transfers between devices  3.14 us (12%)
  between operations  0.71 us (3%)
    pallas_call x16, Pallas kernels, call(): pl.pallas_call(kernel, in_specs=[pl.BlockSpec(memory_space=space) for spa...  14.3 us
    ppermute x6, waiting for transfers between devices, swap(): return lax.ppermute(array, 'seq', [(i, i ^ flip) for i in range(count)])  8.68 us
    ppermute x6, starting transfers between devices, swap(): return lax.ppermute(array, 'seq', [(i, i ^ flip) for i in range(count)])  3.14 us
  transfers between devices with their start and end apart: 6, of which 6 were waited for; matrix products, arithmetic and copies ran while one was open for 0% of the time, Pallas kernels for 35%

profile of v5, /device:TPU:31, one launch (start us, length us, event | category | flops | bytes accessed | tf_op | source)
XLA Modules:
  0.0 26.9 jit_solution(14518315691105018973)
XLA Ops:
  0.6 2.1 %send_states.1 = (f32[256,128]{1,0:T(8,128)S(1)}, f32[128,128]{1,0:T(8,128)S(1)}, f32[1024,128]{1,0:T(8,128)S(1)}, f32[1024,128]{1,0:T(8,128)S(1)}, f32[16,128]{...) custom-call(bf16[128,2048]{1,0:T(8,128)(2,1)} %refs_0_.1, ...), custom_call_target="tpu_custom_call" | custom-call | tf_op jit(solution)/shard_map/send_states/pallas_call | solution.py:122
  2.7 0.7 %collective-permute-start = (f32[256,128]{1,0:T(8,128)S(1)}, f32[256,128]{1,0:T(8,128)S(1)}, u32[]{:S(2)}, u32[]{:S(2)}) collective-permute-start(f32[256,128]{1,0:T(8,128)S(1)} %get-tuple-element.90), channel_id=1, source_target_pairs={{0,1},{1,0},{2,3},{3,2},{4,5},{5,4},{6,7},{7,6},{8,9},{9,8},{10,11... | collective-permute-start | bytes 393224 | tf_op jit(solution)/shard_map/ppermute | solution.py:716
  3.4 0.9 %keep_states.1 = (f32[256,128]{1,0:T(8,128)S(1)}, f32[128,128]{1,0:T(8,128)S(1)}, f32[1024,128]{1,0:T(8,128)S(1)}, f32[1024,128]{1,0:T(8,128)S(1)}) custom-call(f32[16,128]{1,0:T(8,128)S(1)} %get-tuple-element.91.decay_ref.refs_5_, bf16[128,1024]{1,0:T(8,128)(2,1)S(1)} %get-tuple-element.92.refs_0_.refs_1_, ...), custom_call_target="tpu_custom_call" | custom-call | tf_op jit(solution)/shard_map/keep_states/pallas_call | solution.py:122
  4.3 0.1 collective-permute-done.other_ref.core_other_ref
  4.4 0.1 core_join.1
  4.5 0.5 %collective-permute-start.1 = (f32[128,128]{1,0:T(8,128)S(1)}, f32[128,128]{1,0:T(8,128)S(1)}, u32[]{:S(2)}, u32[]{:S(2)}) collective-permute-start(f32[128,128]{1,0:T(8,128)S(1)} %get-tuple-element.105), channel_id=1, source_target_pairs={{0,3},{1,2},{2,1},{3,0},{4,7},{5,6},{6,5},{7,4},{8,11},{9,10},{10,... | collective-permute-start | bytes 196616 | tf_op jit(solution)/shard_map/ppermute | solution.py:716
  5.0 1.3 %lag_part.3.refs_1_ = f32[16,128]{1,0:T(8,128)S(1)} custom-call(f32[1024,128]{1,0:T(8,128)S(1)} %get-tuple-element.114.gated_ref.refs_0_, f32[1024,128]{1,0:T(8,128)S(1)} %get-tuple-element.123.upstream_ref.refs_0_, f32[128,128]{1,0:T(8,128)S(1)} %get-tuple-element.115.rate_ref.refs_2_.refs_1_.refs_3_, f32[128,128]{1,0:T(8,128)S(1)} %get-tuple-element.111.refs_0_), custom_call_target="tpu_custom_call" | custom-call | tf_op jit(solution)/shard_map/lag_part/pallas_call | solution.py:122
  6.3 1.3 %lag_part.2.refs_0_ = f32[16,128]{1,0:T(8,128)S(1)} custom-call(f32[1024,128]{1,0:T(8,128)S(1)} %get-tuple-element.128.gated_ref.refs_0_, f32[1024,128]{1,0:T(8,128)S(1)} %get-tuple-element.130.upstream_ref.refs_3_, f32[128,128]{1,0:T(8,128)S(1)} %get-tuple-element.119.rate_ref.refs_1_.refs_4_), custom_call_target="tpu_custom_call" | custom-call | tf_op jit(solution)/shard_map/lag_part/pallas_call | solution.py:122
  7.6 1.0 %collective-permute-done.1.other_ref.refs_2_ = f32[128,128]{1,0:T(8,128)S(1)} collective-permute-done((f32[128,128]{1,0:T(8,128)S(1)}, f32[128,128]{1,0:T(8,128)S(1)}, u32[]{:S(2)}, u32[]{:S(2)}) %collective-permute-start.1) | collective-permute-done | bytes 65568 | tf_op jit(solution)/shard_map/ppermute | solution.py:716
  8.6 0.0 copy-start
  8.6 0.2 plane_join.1.own_ref
  8.8 0.5 %collective-permute-start.2 = (f32[144,128]{1,0:T(8,128)S(1)}, f32[144,128]{1,0:T(8,128)S(1)}, u32[]{:S(2)}, u32[]{:S(2)}) collective-permute-start(f32[144,128]{1,0:T(8,128)S(1)} %plane_join.1.own_ref), channel_id=1, source_target_pairs={{0,5},{1,4},{2,7},{3,6},{4,1},{5,0},{6,3},{7,2},{8,13},{9,12},{10,... | collective-permute-start | bytes 221192 | tf_op jit(solution)/shard_map/ppermute | solution.py:716
  9.2 0.1 copy-done
  9.3 0.5 %tables.3 = (f32[128,128]{1,0:T(8,128)S(1)}, bf16[128,1024]{1,0:T(8,128)(2,1)S(1)}, bf16[128,1024]{1,0:T(8,128)(2,1)S(1)}, bf16[128,1024]{1,0:T(8,128)(2,1)S(1)}, bf16[128,1024]{1,0:T(8,128)(2,1)S(1)}) custom-call(f32[16,128]{1,0:T(8,128)S(1)} %get-tuple-element.91.decay_ref.refs_5_, f32[16,128]{1,0:T(8,128)S(1)} %bitcast.3, ...), custom_call_target="tpu_custom_call" | custom-call | tf_op jit(solution)/shard_map/tables/pallas_call | solution.py:122
  9.8 0.5 %tables.2 = (f32[128,128]{1,0:T(8,128)S(1)}, bf16[128,1024]{1,0:T(8,128)(2,1)S(1)}, bf16[128,1024]{1,0:T(8,128)(2,1)S(1)}, bf16[128,1024]{1,0:T(8,128)(2,1)S(1)}, bf16[128,1024]{1,0:T(8,128)(2,1)S(1)}) custom-call(f32[16,128]{1,0:T(8,128)S(1)} %get-tuple-element.91.decay_ref.refs_5_, f32[16,128]{1,0:T(8,128)S(1)} %bitcast.4, ...), custom_call_target="tpu_custom_call" | custom-call | tf_op jit(solution)/shard_map/tables/pallas_call | solution.py:122
  10.3 1.1 %scan.3.refs_9_ = f32[1024,128]{1,0:T(8,128)S(1)} custom-call(f32[1024,128]{1,0:T(8,128)S(1)} %get-tuple-element.114.gated_ref.refs_0_, f32[128,128]{1,0:T(8,128)S(1)} %get-tuple-element.115.rate_ref.refs_2_.refs_1_.refs_3_, f32[128,128]{1,0:T(8,128)S(1)} %get-tuple-element.116.refs_2_), custom_call_target="tpu_custom_call" | custom-call | tf_op jit(solution)/shard_map/scan/pallas_call | solution.py:122
  11.4 1.6 %collective-permute-done.2.other_ref.refs_0_ = f32[144,128]{1,0:T(8,128)S(1)} collective-permute-done((f32[144,128]{1,0:T(8,128)S(1)}, f32[144,128]{1,0:T(8,128)S(1)}, u32[]{:S(2)}, u32[]{:S(2)}) %collective-permute-start.2) | collective-permute-done | bytes 73760 | tf_op jit(solution)/shard_map/ppermute | solution.py:716
  13.1 0.2 line_join.1.own_ref
  13.2 0.4 %collective-permute-start.3 = (f32[80,128]{1,0:T(8,128)S(1)}, f32[80,128]{1,0:T(8,128)S(1)}, u32[]{:S(2)}, u32[]{:S(2)}) collective-permute-start(f32[80,128]{1,0:T(8,128)S(1)} %line_join.1.own_ref), channel_id=1, source_target_pairs={{0,9},{1,8},{2,11},{3,10},{4,13},{5,12},{6,15},{7,14},{8,1},{9,0},... | collective-permute-start | bytes 122888 | tf_op jit(solution)/shard_map/ppermute | solution.py:716
  13.6 1.1 %scan.4.refs_10_ = f32[1024,128]{1,0:T(8,128)S(1)} custom-call(f32[1024,128]{1,0:T(8,128)S(1)} %get-tuple-element.123.upstream_ref.refs_0_, f32[128,128]{1,0:T(8,128)S(1)} %get-tuple-element.115.rate_ref.refs_2_.refs_1_.refs_3_, f32[128,128]{1,0:T(8,128)S(1)} %get-tuple-element.116.refs_2_), custom_call_target="tpu_custom_call" | custom-call | tf_op jit(solution)/shard_map/scan/pallas_call | solution.py:122
  14.7 4.0 %collective-permute-done.3.other_ref = f32[80,128]{1,0:T(8,128)S(1)} collective-permute-done((f32[80,128]{1,0:T(8,128)S(1)}, f32[80,128]{1,0:T(8,128)S(1)}, u32[]{:S(2)}, u32[]{:S(2)}) %collective-permute-start.3) | collective-permute-done | bytes 40992 | tf_op jit(solution)/shard_map/ppermute | solution.py:716
  18.8 0.2 turn.1
  18.9 0.6 %collective-permute-start.4 = (f32[144,128]{1,0:T(8,128)S(1)}, f32[144,128]{1,0:T(8,128)S(1)}, u32[]{:S(2)}, u32[]{:S(2)}) collective-permute-start(f32[144,128]{1,0:T(8,128)S(1)} %get-tuple-element.127), channel_id=1, source_target_pairs={{0,3},{1,2},{2,1},{3,0},{4,7},{5,6},{6,5},{7,4},{8,11},{9,10},{10,... | collective-permute-start | bytes 221192 | tf_op jit(solution)/shard_map/ppermute | solution.py:716
  19.5 2.2 %scan.5 = (f32[1024,128]{1,0:T(8,128)S(1)}, f32[1024,128]{1,0:T(8,128)S(1)}) custom-call(f32[1024,128]{1,0:T(8,128)S(1)} %get-tuple-element.128.gated_ref.refs_0_, f32[128,128]{1,0:T(8,128)S(1)} %get-tuple-element.119.rate_ref.refs_1_.refs_4_, f32[128,128]{1,0:T(8,128)S(1)} %get-tuple-element.129.refs_2_.refs_5_, ...), custom_call_target="tpu_custom_call" | custom-call | tf_op jit(solution)/shard_map/scan/pallas_call | solution.py:122
  21.7 1.5 %collective-permute-done.4.other_ref = f32[144,128]{1,0:T(8,128)S(1)} collective-permute-done((f32[144,128]{1,0:T(8,128)S(1)}, f32[144,128]{1,0:T(8,128)S(1)}, u32[]{:S(2)}, u32[]{:S(2)}) %collective-permute-start.4) | collective-permute-done | bytes 73760 | tf_op jit(solution)/shard_map/ppermute | solution.py:716
  23.3 0.5 %collective-permute-start.5 = (f32[272,128]{1,0:T(8,128)S(1)}, f32[272,128]{1,0:T(8,128)S(1)}, u32[]{:S(2)}, u32[]{:S(2)}) collective-permute-start(f32[272,128]{1,0:T(8,128)S(1)} %get-tuple-element.144), channel_id=1, source_target_pairs={{0,1},{1,0},{2,3},{3,2},{4,5},{5,4},{6,7},{7,6},{8,9},{9,8},{10,11... | collective-permute-start | bytes 417800 | tf_op jit(solution)/shard_map/ppermute | solution.py:716
  23.8 0.7 %keep_outputs.1 = (bf16[128,1024]{1,0:T(8,128)(2,1)S(1)}, bf16[128,1024]{1,0:T(8,128)(2,1)S(1)}, bf16[128,1024]{1,0:T(8,128)(2,1)S(1)}, bf16[128,1024]{1,0:T(8,128)(2,1)S(1)}) custom-call(f32[272,128]{1,0:T(8,128)S(1)} %get-tuple-element.134.refs_0_.refs_4_, bf16[128,1024]{1,0:T(8,128)(2,1)S(1)} %get-tuple-element.92.refs_0_.refs_1_, ...), custom_call_target="tpu_custom_call" | custom-call | tf_op jit(solution)/shard_map/keep_outputs/pallas_call | solution.py:122
  24.4 0.3 %collective-permute-done.5.refs_6_ = f32[272,128]{1,0:T(8,128)S(1)} collective-permute-done((f32[272,128]{1,0:T(8,128)S(1)}, f32[272,128]{1,0:T(8,128)S(1)}, u32[]{:S(2)}, u32[]{:S(2)}) %collective-permute-start.5) | collective-permute-done | bytes 139296 | tf_op jit(solution)/shard_map/ppermute | solution.py:716
  24.8 2.1 %sent_outputs.1 = (bf16[128,2048]{1,0:T(8,128)(2,1)}, bf16[128,2048]{1,0:T(8,128)(2,1)}, bf16[128,2048]{1,0:T(8,128)(2,1)}, bf16[128,2048]{1,0:T(8,128)(2,1)}, f32[16,128]{1,0:T(8,128)}) custom-call(bf16[128,1024]{1,0:T(8,128)(2,1)S(1)} %get-tuple-element.140.refs_0_, bf16[128,1024]{1,0:T(8,128)(2,1)S(1)} %get-tuple-element.141.refs_1_, ...), custom_call_target="tpu_custom_call" | custom-call | tf_op jit(solution)/shard_map/sent_outputs/pallas_call | solution.py:122
  (1 shorter events, 0.0 us)
Async XLA Ops:
  2.7 1.7 %collective-permute-start = (f32[256,128]{1,0:T(8,128)S(1)}, f32[256,128]{1,0:T(8,128)S(1)}, u32[]{:S(2)}, u32[]{:S(2)}) collective-permute-start(f32[256,128]{1,0:T(8,128)S(1)} %get-tuple-element.90), channel_id=1, source_target_pairs={{0,1},{1,0},{2,3},{3,2},{4,5},{5,4},{6,7},{7,6},{8,9},{9,8},{10,11... | collective-permute-start | bytes 393224 | tf_op jit(solution)/shard_map/ppermute | solution.py:716
  4.5 4.1 %collective-permute-start.1 = (f32[128,128]{1,0:T(8,128)S(1)}, f32[128,128]{1,0:T(8,128)S(1)}, u32[]{:S(2)}, u32[]{:S(2)}) collective-permute-start(f32[128,128]{1,0:T(8,128)S(1)} %get-tuple-element.105), channel_id=1, source_target_pairs={{0,3},{1,2},{2,1},{3,0},{4,7},{5,6},{6,5},{7,4},{8,11},{9,10},{10,... | collective-permute-start | bytes 196616 | tf_op jit(solution)/shard_map/ppermute | solution.py:716
  8.6 0.7 %copy-start = (f32[128,16]{0,1:T(8,128)S(1)}, f32[128,16]{0,1:T(8,128)}, u32[]{:S(2)}) copy-start(f32[128,16]{0,1:T(8,128)} %param.11) | copy-start | bytes 24580
  8.8 4.3 %collective-permute-start.2 = (f32[144,128]{1,0:T(8,128)S(1)}, f32[144,128]{1,0:T(8,128)S(1)}, u32[]{:S(2)}, u32[]{:S(2)}) collective-permute-start(f32[144,128]{1,0:T(8,128)S(1)} %plane_join.1.own_ref), channel_id=1, source_target_pairs={{0,5},{1,4},{2,7},{3,6},{4,1},{5,0},{6,3},{7,2},{8,13},{9,12},{10,... | collective-permute-start | bytes 221192 | tf_op jit(solution)/shard_map/ppermute | solution.py:716
  13.2 5.5 %collective-permute-start.3 = (f32[80,128]{1,0:T(8,128)S(1)}, f32[80,128]{1,0:T(8,128)S(1)}, u32[]{:S(2)}, u32[]{:S(2)}) collective-permute-start(f32[80,128]{1,0:T(8,128)S(1)} %line_join.1.own_ref), channel_id=1, source_target_pairs={{0,9},{1,8},{2,11},{3,10},{4,13},{5,12},{6,15},{7,14},{8,1},{9,0},... | collective-permute-start | bytes 122888 | tf_op jit(solution)/shard_map/ppermute | solution.py:716
  18.9 4.3 %collective-permute-start.4 = (f32[144,128]{1,0:T(8,128)S(1)}, f32[144,128]{1,0:T(8,128)S(1)}, u32[]{:S(2)}, u32[]{:S(2)}) collective-permute-start(f32[144,128]{1,0:T(8,128)S(1)} %get-tuple-element.127), channel_id=1, source_target_pairs={{0,3},{1,2},{2,1},{3,0},{4,7},{5,6},{6,5},{7,4},{8,11},{9,10},{10,... | collective-permute-start | bytes 221192 | tf_op jit(solution)/shard_map/ppermute | solution.py:716
  23.3 1.5 %collective-permute-start.5 = (f32[272,128]{1,0:T(8,128)S(1)}, f32[272,128]{1,0:T(8,128)S(1)}, u32[]{:S(2)}, u32[]{:S(2)}) collective-permute-start(f32[272,128]{1,0:T(8,128)S(1)} %get-tuple-element.144), channel_id=1, source_target_pairs={{0,1},{1,0},{2,3},{3,2},{4,5},{5,4},{6,7},{7,6},{8,9},{9,8},{10,11... | collective-permute-start | bytes 417800 | tf_op jit(solution)/shard_map/ppermute | solution.py:716

commit v6 on v5

--- a/solution.py
+++ b/solution.py
@@ -304,43 +304,44 @@
     return [stack_ref[pl.ds(n, blocks, stride=MODES), :] for n in range(MODES)]
 
 
-def lag_kernel(keep, gated_ref, upstream_ref, rate_ref, *refs):
-    *cross_refs, out_ref, stack_ref = refs
-    blocks = rate_ref.shape[0] // MODES
-    half = kept_half(lax.axis_index("seq"))
-    offset = (half if keep else 1 - half) * blocks
-    decays = [jnp.exp(-rate) for rate in by_mode(rate_ref, blocks)]
-    out = jnp.zeros((MODES, LANES), F32)
-    for cross_ref in cross_refs:
-        out = filter_sums(cross_ref[...], offset)
-
-    def step(i, carry):
-        states, totals = list(carry[0]), list(carry[1])
-        place = pl.ds(pl.multiple_of(i * blocks, blocks), blocks)
-        gated, upstream = gated_ref[place], upstream_ref[place]
+def lag_kernel(*refs):
+    *half_refs, cross_ref, out_ref, stack_ref = refs
+    kept = kept_half(lax.axis_index("seq"))
+    blocks = half_refs[2].shape[0] // MODES
+    rows = blocks * MODES
+    out = filter_sums(cross_ref[...], kept * blocks)
+    for role, half in enumerate((1 - kept, kept)):
+        gated_ref, upstream_ref, rate_ref = half_refs[3 * role : 3 * role + 3]
+        decays = [jnp.exp(-rate) for rate in by_mode(rate_ref, blocks)]
+
+        def step(i, carry, gated_ref=gated_ref, upstream_ref=upstream_ref, decays=decays):
+            states, totals = list(carry[0]), list(carry[1])
+            place = pl.ds(pl.multiple_of(i * blocks, blocks), blocks)
+            gated, upstream = gated_ref[place], upstream_ref[place]
+            for n in range(MODES):
+                states[n] = states[n] * decays[n] + gated
+                totals[n] = totals[n] + states[n] * upstream
+            return tuple(states), tuple(totals)
+
+        zeros = (jnp.zeros((blocks, LANES), F32),) * MODES
+        steps = gated_ref.shape[0] // blocks
+        _, totals = lax.fori_loop(0, steps, step, (zeros, zeros), unroll=UNROLL)
         for n in range(MODES):
-            states[n] = states[n] * decays[n] + gated
-            totals[n] = totals[n] + states[n] * upstream
-        return tuple(states), tuple(totals)
-
-    zeros = (jnp.zeros((blocks, LANES), F32),) * MODES
-    steps = gated_ref.shape[0] // blocks
-    _, totals = lax.fori_loop(0, steps, step, (zeros, zeros), unroll=UNROLL)
-    for n in range(MODES):
-        stack_ref[pl.ds(n, blocks, stride=MODES), :] = totals[n]
-    out_ref[...] = out + filter_sums(stack_ref[...], offset)
-
-
-def lag_part(keep, gated, upstream, rate, *cross):
-    return call(
-        functools.partial(lag_kernel, keep),
+            stack_ref[pl.ds(role * rows + n, blocks, stride=MODES), :] = totals[n]
+        out = out + filter_sums(stack_ref[role * rows : (role + 1) * rows], half * blocks)
+    out_ref[...] = out
+
+
+def lag_part(sent, kept, cross):
+    rows, lanes = cross.shape
+    return call(
+        lag_kernel,
         "lag_part",
         [((MODES, LANES), F32)],
-        gated,
-        upstream,
-        rate,
-        *cross,
-        scratch=[pltpu.VMEM(rate.shape, F32)],
+        *sent,
+        *kept,
+        cross,
+        scratch=[pltpu.VMEM((2 * rows, lanes), F32)],
     )[0]
 
 
@@ -727,8 +728,9 @@
     chip_send, gated, upstream, gated_sent = tie(chip_send, gated, upstream, gated_sent)
     chip_other = swap(chip_send, 2)
     lags = [
-        lag_part(False, gated_sent, upstream_sent, rate_sent),
-        lag_part(True, gated, upstream, rate, core_cross),
+        lag_part(
+            (gated_sent, upstream_sent, rate_sent), (gated, upstream, rate), core_cross
+        )
     ]
     message = plane_join(length, chip, chip_other, lags, rate)
 

time: 27.1 us -> 27.1 us (level)
  the two profiles are of different devices: /device:TPU:31 before, /device:TPU:25 now
where the time goes in v6:
time: 27.1 us; the launch traced here: 26.9 us
  Pallas kernels  14.2 us (52%)
  waiting for transfers between devices  6.79 us (25%)
  starting transfers between devices  5.18 us (19%)
  between operations  0.7 us (3%)
    pallas_call x15, Pallas kernels, call(): pl.pallas_call(kernel, in_specs=[pl.BlockSpec(memory_space=space) for spa...  14.2 us
    ppermute x6, waiting for transfers between devices, swap(): return lax.ppermute(array, 'seq', [(i, i ^ flip) for i in range(count)])  6.79 us
    ppermute x6, starting transfers between devices, swap(): return lax.ppermute(array, 'seq', [(i, i ^ flip) for i in range(count)])  5.18 us
  transfers between devices with their start and end apart: 6, of which 6 were waited for; matrix products, arithmetic and copies ran while one was open for 0% of the time, Pallas kernels for 35%

profile of v6, /device:TPU:25, one launch (start us, length us, event | category | flops | bytes accessed | tf_op | source)
XLA Modules:
  0.0 26.9 jit_solution(2652120103180089877)
XLA Ops:
  0.6 2.1 %send_states.1 = (f32[256,128]{1,0:T(8,128)S(1)}, f32[128,128]{1,0:T(8,128)S(1)}, f32[1024,128]{1,0:T(8,128)S(1)}, f32[1024,128]{1,0:T(8,128)S(1)}, f32[16,128]{...) custom-call(bf16[128,2048]{1,0:T(8,128)(2,1)} %refs_0_.1, ...), custom_call_target="tpu_custom_call" | custom-call | tf_op jit(solution)/shard_map/send_states/pallas_call | solution.py:122
  2.7 0.7 %collective-permute-start = (f32[256,128]{1,0:T(8,128)S(1)}, f32[256,128]{1,0:T(8,128)S(1)}, u32[]{:S(2)}, u32[]{:S(2)}) collective-permute-start(f32[256,128]{1,0:T(8,128)S(1)} %get-tuple-element.90), channel_id=1, source_target_pairs={{0,1},{1,0},{2,3},{3,2},{4,5},{5,4},{6,7},{7,6},{8,9},{9,8},{10,11... | collective-permute-start | bytes 393224 | tf_op jit(solution)/shard_map/ppermute | solution.py:717
  3.4 0.9 %keep_states.1 = (f32[256,128]{1,0:T(8,128)S(1)}, f32[128,128]{1,0:T(8,128)S(1)}, f32[1024,128]{1,0:T(8,128)S(1)}, f32[1024,128]{1,0:T(8,128)S(1)}) custom-call(f32[16,128]{1,0:T(8,128)S(1)} %get-tuple-element.91.decay_ref.refs_5_, bf16[128,1024]{1,0:T(8,128)(2,1)S(1)} %get-tuple-element.92.refs_0_.refs_1_, ...), custom_call_target="tpu_custom_call" | custom-call | tf_op jit(solution)/shard_map/keep_states/pallas_call | solution.py:122
  4.3 0.1 collective-permute-done.other_ref.core_other_ref
  4.4 0.1 core_join.1
  4.5 1.6 %collective-permute-start.1 = (f32[128,128]{1,0:T(8,128)S(1)}, f32[128,128]{1,0:T(8,128)S(1)}, u32[]{:S(2)}, u32[]{:S(2)}) collective-permute-start(f32[128,128]{1,0:T(8,128)S(1)} %get-tuple-element.105), channel_id=1, source_target_pairs={{0,3},{1,2},{2,1},{3,0},{4,7},{5,6},{6,5},{7,4},{8,11},{9,10},{10,... | collective-permute-start | bytes 196616 | tf_op jit(solution)/shard_map/ppermute | solution.py:717
  6.0 2.4 %lag_part.1.refs_0_ = f32[16,128]{1,0:T(8,128)S(1)} custom-call(f32[1024,128]{1,0:T(8,128)S(1)} %get-tuple-element.128.refs_0_, f32[1024,128]{1,0:T(8,128)S(1)} %get-tuple-element.130.refs_1_.refs_3_, f32[128,128]{1,0:T(8,128)S(1)} %get-tuple-element.119.refs_2_.rate_ref.refs_1_.refs_4_, f32[1024,128]{1,0:T(8,128)S(1)} %get-tuple-element.114.refs_3_.refs_0_, ...), custom_call_target="tpu_custom_call" | custom-call | tf_op jit(solution)/shard_map/lag_part/pallas_call | solution.py:122
  8.4 0.2 collective-permute-done.1.other_ref.refs_2_
  8.6 0.0 copy-start
  8.6 0.2 plane_join.1.own_ref
  8.8 0.5 %collective-permute-start.2 = (f32[144,128]{1,0:T(8,128)S(1)}, f32[144,128]{1,0:T(8,128)S(1)}, u32[]{:S(2)}, u32[]{:S(2)}) collective-permute-start(f32[144,128]{1,0:T(8,128)S(1)} %plane_join.1.own_ref), channel_id=1, source_target_pairs={{0,5},{1,4},{2,7},{3,6},{4,1},{5,0},{6,3},{7,2},{8,13},{9,12},{10,... | collective-permute-start | bytes 221192 | tf_op jit(solution)/shard_map/ppermute | solution.py:717
  9.2 0.1 copy-done
  9.3 0.5 %tables.3 = (f32[128,128]{1,0:T(8,128)S(1)}, bf16[128,1024]{1,0:T(8,128)(2,1)S(1)}, bf16[128,1024]{1,0:T(8,128)(2,1)S(1)}, bf16[128,1024]{1,0:T(8,128)(2,1)S(1)}, bf16[128,1024]{1,0:T(8,128)(2,1)S(1)}) custom-call(f32[16,128]{1,0:T(8,128)S(1)} %get-tuple-element.91.decay_ref.refs_5_, f32[16,128]{1,0:T(8,128)S(1)} %bitcast.3, ...), custom_call_target="tpu_custom_call" | custom-call | tf_op jit(solution)/shard_map/tables/pallas_call | solution.py:122
  9.8 0.5 %tables.2 = (f32[128,128]{1,0:T(8,128)S(1)}, bf16[128,1024]{1,0:T(8,128)(2,1)S(1)}, bf16[128,1024]{1,0:T(8,128)(2,1)S(1)}, bf16[128,1024]{1,0:T(8,128)(2,1)S(1)}, bf16[128,1024]{1,0:T(8,128)(2,1)S(1)}) custom-call(f32[16,128]{1,0:T(8,128)S(1)} %get-tuple-element.91.decay_ref.refs_5_, f32[16,128]{1,0:T(8,128)S(1)} %bitcast.4, ...), custom_call_target="tpu_custom_call" | custom-call | tf_op jit(solution)/shard_map/tables/pallas_call | solution.py:122
  10.3 1.1 %scan.3.refs_9_ = f32[1024,128]{1,0:T(8,128)S(1)} custom-call(f32[1024,128]{1,0:T(8,128)S(1)} %get-tuple-element.114.refs_3_.refs_0_, f32[128,128]{1,0:T(8,128)S(1)} %get-tuple-element.115.rate_ref.refs_5_.refs_1_.refs_3_, f32[128,128]{1,0:T(8,128)S(1)} %get-tuple-element.116.refs_2_), custom_call_target="tpu_custom_call" | custom-call | tf_op jit(solution)/shard_map/scan/pallas_call | solution.py:122
  11.4 1.6 %collective-permute-done.2.other_ref.refs_0_ = f32[144,128]{1,0:T(8,128)S(1)} collective-permute-done((f32[144,128]{1,0:T(8,128)S(1)}, f32[144,128]{1,0:T(8,128)S(1)}, u32[]{:S(2)}, u32[]{:S(2)}) %collective-permute-start.2) | collective-permute-done | bytes 73760 | tf_op jit(solution)/shard_map/ppermute | solution.py:717
  13.1 0.2 line_join.1.own_ref
  13.2 0.4 %collective-permute-start.3 = (f32[80,128]{1,0:T(8,128)S(1)}, f32[80,128]{1,0:T(8,128)S(1)}, u32[]{:S(2)}, u32[]{:S(2)}) collective-permute-start(f32[80,128]{1,0:T(8,128)S(1)} %line_join.1.own_ref), channel_id=1, source_target_pairs={{0,9},{1,8},{2,11},{3,10},{4,13},{5,12},{6,15},{7,14},{8,1},{9,0},... | collective-permute-start | bytes 122888 | tf_op jit(solution)/shard_map/ppermute | solution.py:717
  13.6 1.1 %scan.4.refs_10_ = f32[1024,128]{1,0:T(8,128)S(1)} custom-call(f32[1024,128]{1,0:T(8,128)S(1)} %get-tuple-element.123.refs_4_.refs_0_, f32[128,128]{1,0:T(8,128)S(1)} %get-tuple-element.115.rate_ref.refs_5_.refs_1_.refs_3_, f32[128,128]{1,0:T(8,128)S(1)} %get-tuple-element.116.refs_2_), custom_call_target="tpu_custom_call" | custom-call | tf_op jit(solution)/shard_map/scan/pallas_call | solution.py:122
  14.7 4.0 %collective-permute-done.3.other_ref = f32[80,128]{1,0:T(8,128)S(1)} collective-permute-done((f32[80,128]{1,0:T(8,128)S(1)}, f32[80,128]{1,0:T(8,128)S(1)}, u32[]{:S(2)}, u32[]{:S(2)}) %collective-permute-start.3) | collective-permute-done | bytes 40992 | tf_op jit(solution)/shard_map/ppermute | solution.py:717
  18.8 0.2 turn.1
  18.9 1.6 %collective-permute-start.4 = (f32[144,128]{1,0:T(8,128)S(1)}, f32[144,128]{1,0:T(8,128)S(1)}, u32[]{:S(2)}, u32[]{:S(2)}) collective-permute-start(f32[144,128]{1,0:T(8,128)S(1)} %get-tuple-element.127), channel_id=1, source_target_pairs={{0,3},{1,2},{2,1},{3,0},{4,7},{5,6},{6,5},{7,4},{8,11},{9,10},{10,... | collective-permute-start | bytes 221192 | tf_op jit(solution)/shard_map/ppermute | solution.py:717
  20.5 2.2 %scan.5 = (f32[1024,128]{1,0:T(8,128)S(1)}, f32[1024,128]{1,0:T(8,128)S(1)}) custom-call(f32[1024,128]{1,0:T(8,128)S(1)} %get-tuple-element.128.refs_0_, f32[128,128]{1,0:T(8,128)S(1)} %get-tuple-element.119.refs_2_.rate_ref.refs_1_.refs_4_, f32[128,128]{1,0:T(8,128)S(1)} %get-tuple-element.129.refs_2_.refs_5_, ...), custom_call_target="tpu_custom_call" | custom-call | tf_op jit(solution)/shard_map/scan/pallas_call | solution.py:122
  22.7 0.5 %collective-permute-done.4.other_ref = f32[144,128]{1,0:T(8,128)S(1)} collective-permute-done((f32[144,128]{1,0:T(8,128)S(1)}, f32[144,128]{1,0:T(8,128)S(1)}, u32[]{:S(2)}, u32[]{:S(2)}) %collective-permute-start.4) | collective-permute-done | bytes 73760 | tf_op jit(solution)/shard_map/ppermute | solution.py:717
  23.3 0.5 %collective-permute-start.5 = (f32[272,128]{1,0:T(8,128)S(1)}, f32[272,128]{1,0:T(8,128)S(1)}, u32[]{:S(2)}, u32[]{:S(2)}) collective-permute-start(f32[272,128]{1,0:T(8,128)S(1)} %get-tuple-element.144), channel_id=1, source_target_pairs={{0,1},{1,0},{2,3},{3,2},{4,5},{5,4},{6,7},{7,6},{8,9},{9,8},{10,11... | collective-permute-start | bytes 417800 | tf_op jit(solution)/shard_map/ppermute | solution.py:717
  23.8 0.7 %keep_outputs.1 = (bf16[128,1024]{1,0:T(8,128)(2,1)S(1)}, bf16[128,1024]{1,0:T(8,128)(2,1)S(1)}, bf16[128,1024]{1,0:T(8,128)(2,1)S(1)}, bf16[128,1024]{1,0:T(8,128)(2,1)S(1)}) custom-call(f32[272,128]{1,0:T(8,128)S(1)} %get-tuple-element.134.refs_0_.refs_4_, bf16[128,1024]{1,0:T(8,128)(2,1)S(1)} %get-tuple-element.92.refs_0_.refs_1_, ...), custom_call_target="tpu_custom_call" | custom-call | tf_op jit(solution)/shard_map/keep_outputs/pallas_call | solution.py:122
  24.4 0.3 %collective-permute-done.5.refs_6_ = f32[272,128]{1,0:T(8,128)S(1)} collective-permute-done((f32[272,128]{1,0:T(8,128)S(1)}, f32[272,128]{1,0:T(8,128)S(1)}, u32[]{:S(2)}, u32[]{:S(2)}) %collective-permute-start.5) | collective-permute-done | bytes 139296 | tf_op jit(solution)/shard_map/ppermute | solution.py:717
  24.8 2.1 %sent_outputs.1 = (bf16[128,2048]{1,0:T(8,128)(2,1)}, bf16[128,2048]{1,0:T(8,128)(2,1)}, bf16[128,2048]{1,0:T(8,128)(2,1)}, bf16[128,2048]{1,0:T(8,128)(2,1)}, f32[16,128]{1,0:T(8,128)}) custom-call(bf16[128,1024]{1,0:T(8,128)(2,1)S(1)} %get-tuple-element.140.refs_0_, bf16[128,1024]{1,0:T(8,128)(2,1)S(1)} %get-tuple-element.141.refs_1_, ...), custom_call_target="tpu_custom_call" | custom-call | tf_op jit(solution)/shard_map/sent_outputs/pallas_call | solution.py:122
  (1 shorter events, 0.0 us)
Async XLA Ops:
  2.7 1.7 %collective-permute-start = (f32[256,128]{1,0:T(8,128)S(1)}, f32[256,128]{1,0:T(8,128)S(1)}, u32[]{:S(2)}, u32[]{:S(2)}) collective-permute-start(f32[256,128]{1,0:T(8,128)S(1)} %get-tuple-element.90), channel_id=1, source_target_pairs={{0,1},{1,0},{2,3},{3,2},{4,5},{5,4},{6,7},{7,6},{8,9},{9,8},{10,11... | collective-permute-start | bytes 393224 | tf_op jit(solution)/shard_map/ppermute | solution.py:717
  4.5 4.1 %collective-permute-start.1 = (f32[128,128]{1,0:T(8,128)S(1)}, f32[128,128]{1,0:T(8,128)S(1)}, u32[]{:S(2)}, u32[]{:S(2)}) collective-permute-start(f32[128,128]{1,0:T(8,128)S(1)} %get-tuple-element.105), channel_id=1, source_target_pairs={{0,3},{1,2},{2,1},{3,0},{4,7},{5,6},{6,5},{7,4},{8,11},{9,10},{10,... | collective-permute-start | bytes 196616 | tf_op jit(solution)/shard_map/ppermute | solution.py:717
  8.6 0.7 %copy-start = (f32[128,16]{0,1:T(8,128)S(1)}, f32[128,16]{0,1:T(8,128)}, u32[]{:S(2)}) copy-start(f32[128,16]{0,1:T(8,128)} %param.11) | copy-start | bytes 24580
  8.8 4.3 %collective-permute-start.2 = (f32[144,128]{1,0:T(8,128)S(1)}, f32[144,128]{1,0:T(8,128)S(1)}, u32[]{:S(2)}, u32[]{:S(2)}) collective-permute-start(f32[144,128]{1,0:T(8,128)S(1)} %plane_join.1.own_ref), channel_id=1, source_target_pairs={{0,5},{1,4},{2,7},{3,6},{4,1},{5,0},{6,3},{7,2},{8,13},{9,12},{10,... | collective-permute-start | bytes 221192 | tf_op jit(solution)/shard_map/ppermute | solution.py:717
  13.2 5.5 %collective-permute-start.3 = (f32[80,128]{1,0:T(8,128)S(1)}, f32[80,128]{1,0:T(8,128)S(1)}, u32[]{:S(2)}, u32[]{:S(2)}) collective-permute-start(f32[80,128]{1,0:T(8,128)S(1)} %line_join.1.own_ref), channel_id=1, source_target_pairs={{0,9},{1,8},{2,11},{3,10},{4,13},{5,12},{6,15},{7,14},{8,1},{9,0},... | collective-permute-start | bytes 122888 | tf_op jit(solution)/shard_map/ppermute | solution.py:717
  18.9 4.3 %collective-permute-start.4 = (f32[144,128]{1,0:T(8,128)S(1)}, f32[144,128]{1,0:T(8,128)S(1)}, u32[]{:S(2)}, u32[]{:S(2)}) collective-permute-start(f32[144,128]{1,0:T(8,128)S(1)} %get-tuple-element.127), channel_id=1, source_target_pairs={{0,3},{1,2},{2,1},{3,0},{4,7},{5,6},{6,5},{7,4},{8,11},{9,10},{10,... | collective-permute-start | bytes 221192 | tf_op jit(solution)/shard_map/ppermute | solution.py:717
  23.3 1.5 %collective-permute-start.5 = (f32[272,128]{1,0:T(8,128)S(1)}, f32[272,128]{1,0:T(8,128)S(1)}, u32[]{:S(2)}, u32[]{:S(2)}) collective-permute-start(f32[272,128]{1,0:T(8,128)S(1)} %get-tuple-element.144), channel_id=1, source_target_pairs={{0,1},{1,0},{2,3},{3,2},{4,5},{5,4},{6,7},{7,6},{8,9},{9,8},{10,11... | collective-permute-start | bytes 417800 | tf_op jit(solution)/shard_map/ppermute | solution.py:717
